TPU v7x, 32 devices: a whole 2x2x4 slice. The times are simulated.
32 devices in a mesh: energy: 8 (over z, y), section: 4 (over x, core).
Axes of the slice: x: 2, y: 2, z: 4, core: 2. Of those that a mesh axis runs over, the one named last changes fastest.
Arguments:
- onsite: float32 [8, 256], P('section'), may hold values from -1 to 1
- hopping: float32 [8, 256, 256], P('section'), may hold values from -0.125 to 0.125
- coupling: float32 [8, 256, 256], P('section'), may hold values from -4 to 4
- broadening: float32 [8], P('energy'), may hold values from 1.5 to 3
- born_sigma: float32 [8, 8, 2, 256, 256], P('energy', 'section'), may hold values from -0.046875 to 0.046875
- phonon_shift: int32 [4], replicated, may hold values from -2 to 2
- phonon_local: float32 [4, 256, 256], replicated, may hold values from 0.5 to 4
- phonon_side: float32 [4, 256, 256], replicated, may hold values from 0.2 to 2
Outputs:
- next_sigma: float32 [8, 8, 2, 256, 256], P('energy', 'section')
All inputs are finite; a program needn't handle non-finite values.
Results may differ from a plain program's by a relative error of at most 0.0001.
Values sent between devices are 32-bit elements; how exact they have to be, the bound alone decides.
No kernel may reach another device: no remote copies, remote signals or barrier semaphores. Data moves between devices by JAX's collectives and lax.ppermute only.
A program may use at most 128 MiB of HBM per device.

v0:
```python
import functools

import jax
import jax.numpy as jnp
from jax import lax
from jax.experimental import pallas as pl
from jax.experimental.pallas import tpu as pltpu
from jax.sharding import PartitionSpec as P

F32 = jnp.float32
BF16 = jnp.bfloat16
VMEM = pl.BlockSpec(memory_space=pltpu.VMEM)


def split(value):
    high = value.astype(BF16)
    return high, (value - high.astype(F32)).astype(BF16)


def product(left, right):
    def dot(a, b):
        return jnp.dot(a, b, preferred_element_type=F32)

    return dot(left[0], right[0]) + (dot(left[0], right[1]) + dot(left[1], right[0]))


def parts(real, imag):
    return split(real), split(imag), split(real + imag)


def complex_product(left, right):
    first = product(left[0], right[0])
    second = product(left[1], right[1])
    third = product(left[2], right[2])
    return first - second, third - (first + second)


def start_series(real, imag):
    shape = real.shape
    eye = lax.broadcasted_iota(jnp.int32, shape, 0) == lax.broadcasted_iota(jnp.int32, shape, 1)
    diag_real = jnp.where(eye, real, 0.0)
    diag_imag = jnp.where(eye, imag, 0.0)

    def inverse(axis):
        a = jnp.sum(diag_real, axis, keepdims=True)
        b = jnp.sum(diag_imag, axis, keepdims=True)
        modulus = a * a + b * b
        return a / modulus, -b / modulus

    col_real, col_imag = inverse(0)
    row_real, row_imag = inverse(1)
    e_real = jnp.where(eye, 0.0, imag * col_imag - real * col_real)
    e_imag = jnp.where(eye, 0.0, -(real * col_imag + imag * col_real))
    t_real = e_real + jnp.where(eye, 1.0, 0.0)
    x_real = row_real * t_real - row_imag * e_imag
    x_imag = row_real * e_imag + row_imag * t_real
    return e_real, e_imag, x_real, x_imag


def is_active(step, sections):
    slot = lax.axis_index("section")
    return jnp.logical_or(slot == step, slot == sections - 1 - step)


def series_square(real, imag):
    e_real, e_imag, x_real, x_imag = start_series(real, imag)
    e_parts = parts(e_real, e_imag)
    return x_real, x_imag, parts(*complex_product(e_parts, e_parts))


def half_of(sections):
    return lax.axis_index("section") >= sections // 2


def is_at(step, sections):
    slot = lax.axis_index("section")
    return jnp.logical_or(slot == step, slot == sections - 1 - step)


def chain_core(real, imag, link, link_t, out):
    x_real, x_imag, f_parts = series_square(real, imag)
    right = split(link)
    left = split(link_t)
    a_real = product(left, split(x_real))
    a_imag = product(left, split(x_imag))
    b_real, b_imag = complex_product(parts(a_real, a_imag), f_parts)
    g_real, g_imag = complex_product(f_parts, f_parts)
    w_real = product(split(g_real), right) + link
    w_imag = product(split(g_imag), right)
    s_real, s_imag = complex_product(parts(b_real + a_real, b_imag + a_imag), parts(w_real, w_imag))
    out[0] = s_real
    out[1] = s_imag


def call(body, out_shape, operands, products, name):
    dimension = operands[0].shape[-1]
    size = dimension * dimension
    return pl.pallas_call(
        body,
        out_shape=out_shape,
        in_specs=[VMEM] * len(operands),
        out_specs=jax.tree.map(lambda _: VMEM, out_shape),
        compiler_params=pltpu.CompilerParams(vmem_limit_bytes=12 << 20),
        cost_estimate=pl.CostEstimate(
            flops=6 * products * size * dimension, bytes_accessed=4 * 8 * size, transcendentals=0
        ),
        name=name,
    )(*operands)


def link_ways(sections, refs, links):
    table, near, away = refs[0], links[0][1], links[0][2]
    if len(links) == 1:
        return table[near], table[away]
    right_half = half_of(sections)
    plain = refs[1][...]
    turned = plain.T
    link, link_t = (turned, plain) if links[1][1] else (plain, turned)
    return jnp.where(right_half, link, table[near]), jnp.where(right_half, link_t, table[away])


def chain_step(sections, active, pack, block, sigmas, links, name, after=()):
    arrays = [pack] + list(sigmas) + [link[0] for link in links]
    count = len(arrays)

    def body(*refs):
        out = refs[-1]
        source = refs[0]
        given = refs[1 : 1 + len(sigmas)]

        def work():
            real, imag = source[2 * block], source[2 * block + 1]
            if len(given) == 1:
                real, imag = real - given[0][0], imag - given[0][1]
            elif len(given) == 2:
                outer = is_at(0, sections)
                real = real - jnp.where(outer, given[0][0], given[1][0])
                imag = imag - jnp.where(outer, given[0][1], given[1][1])
            link, link_t = link_ways(sections, refs[1 + len(sigmas) : count], links)
            chain_core(real, imag, link, link_t, out)

        if active is None:
            work()
        else:
            mine = is_at(active, sections)
            pl.when(mine)(work)

            @pl.when(jnp.logical_not(mine))
            def _():
                out[...] = jnp.zeros_like(out)

    shape = jax.ShapeDtypeStruct((2,) + pack.shape[1:], F32)
    return call(body, shape, arrays + list(after), 16, name)


def green_step(sections, active, pack, block, first, second, name, passed=(), joined=()):
    arrays = [pack] + [a for a in first + second if a is not None]
    count = len(arrays)
    arrays = arrays + list(passed) + [a for pair in joined for a in pair]
    size = 1 + len(joined)

    def body(*refs):
        outs = refs[-2:]

        def put(place, value):
            if joined:
                outs[place][0] = value
            else:
                outs[place][...] = value

        def work():
            rest = list(refs[1:count])
            value = [refs[0][2 * block], refs[0][2 * block + 1]]
            outer = is_at(0, sections)
            for pair in (first, second):
                taken = [None if a is None else rest.pop(0) for a in pair]
                for place in (0, 1):
                    terms = [
                        jnp.zeros_like(value[0]) if t is None else t[place] for t in taken
                    ]
                    term = terms[0] if len(terms) == 1 else jnp.where(outer, *terms)
                    value[place] = value[place] - term
            x_real, x_imag, f_parts = series_square(*value)
            b_real, b_imag = complex_product(parts(x_real, x_imag), f_parts)
            g_real, g_imag = complex_product(f_parts, f_parts)
            b_real = b_real + x_real
            b_imag = b_imag + x_imag
            s_real, s_imag = complex_product(parts(b_real, b_imag), parts(g_real, g_imag))
            put(0, b_real + s_real)
            put(1, b_imag + s_imag)

        if active is None:
            work()
        else:
            mine = is_at(active, sections)
            pl.when(mine)(work)

            @pl.when(jnp.logical_not(mine))
            def _():
                for place in (0, 1):
                    if passed:
                        put(place, refs[count + place][...])
                    else:
                        put(place, jnp.zeros(refs[0].shape[1:], F32))

        for number in range(len(joined)):
            for place in (0, 1):
                outs[place][1 + number] = refs[count + len(passed) + 2 * number + place][...]

    flat = jax.ShapeDtypeStruct(((size,) if joined else ()) + pack.shape[1:], F32)
    return call(body, (flat, flat), arrays, 12, name)


def prepare_kernel(
    sections, spread, broadening, onsite, hopping, coupling, born, pack, edge, plain, hop, cup, sig, sems
):
    blocks, dimension = onsite.shape
    copies = []
    for index in range(blocks):
        for order, (source, target) in enumerate(
            (
                (hopping.at[index], hop.at[index]),
                (born.at[0, index], sig.at[index]),
                (coupling.at[index], cup.at[index]),
            )
        ):
            copy = pltpu.make_async_copy(source, target, sems.at[3 * index + order])
            copy.start()
            copies.append(copy)
    right_half = half_of(sections)
    flip = right_half.astype(jnp.int32)
    shape = (dimension, dimension)
    eye = lax.broadcasted_iota(jnp.int32, shape, 0) == lax.broadcasted_iota(jnp.int32, shape, 1)
    position = lax.axis_index("energy").astype(F32)
    energy = -2.0 + position * (4.0 / (spread - 1))
    broad = broadening[...]
    for index in range(blocks):
        place = jnp.where(right_half, blocks - 1 - index, index)
        copies[3 * index].wait()
        block = hop[index]
        level = energy - onsite[pl.ds(index, 1), :]
        real = jnp.where(eye, jnp.broadcast_to(level, shape), 0.0) - 0.5 * (block + block.T)
        copies[3 * index + 1].wait()
        pack[2 * place] = real - sig[index, 0]
        pack[2 * place + 1] = jnp.where(eye, jnp.broadcast_to(broad, shape), 0.0) - sig[index, 1]
        copies[3 * index + 2].wait()
        link = cup[index]
        if index < blocks - 1:
            place = 2 * blocks + 2 * jnp.where(right_half, blocks - 2 - index, index)
            pack[place + flip] = link
            pack[place + 1 - flip] = link.T
        else:
            plain[...] = link
            edge[0] = link
            edge[1] = link.T


def prepare(sections, spread, broadening, onsite, hopping, coupling, born):
    blocks, dimension = onsite.shape
    outside = pl.BlockSpec(memory_space=pltpu.HBM)
    return pl.pallas_call(
        functools.partial(prepare_kernel, sections, spread),
        out_shape=(
            jax.ShapeDtypeStruct((4 * blocks - 2, dimension, dimension), F32),
            jax.ShapeDtypeStruct((2, dimension, dimension), F32),
            jax.ShapeDtypeStruct((dimension, dimension), F32),
        ),
        in_specs=[VMEM, VMEM, outside, outside, outside],
        out_specs=(VMEM, VMEM, VMEM),
        scratch_shapes=[
            pltpu.VMEM((blocks, dimension, dimension), F32),
            pltpu.VMEM((blocks, dimension, dimension), F32),
            pltpu.VMEM((blocks, 2, dimension, dimension), F32),
            pltpu.SemaphoreType.DMA((3 * blocks,)),
        ],
        compiler_params=pltpu.CompilerParams(vmem_limit_bytes=16 << 20),
        name="prepare",
    )(broadening.reshape(1, 1), onsite, hopping, coupling, born)


OWN, NEXT, OTHER, PAIR, LONE = range(5)


def is_even():
    return lax.axis_index("energy") % 2 == 0


def first_is_far():
    slot = lax.axis_index("energy")
    return (slot // 2) % 2 == slot % 2


def weights(shifts, local_weight, side_weight, after):
    shape = jax.ShapeDtypeStruct((5,) + local_weight.shape[1:], F32)

    def body(shift_ref, local_ref, side_ref, _, local_out, side_out):
        even = is_even()
        low, high = jnp.where(even, NEXT, OTHER), jnp.where(even, OTHER, NEXT)
        far_low, far_high = jnp.where(even, PAIR, LONE), jnp.where(even, LONE, PAIR)
        for source, target in ((local_ref, local_out), (side_ref, side_out)):
            for shift, place in ((0, OWN), (-1, low), (1, high), (-2, far_low), (2, far_high)):
                total = jnp.zeros(source.shape[1:], F32)
                for mode in range(source.shape[0]):
                    total = total + jnp.where(shift_ref[mode] == shift, source[mode], 0.0)
                target[place] = total

    return pl.pallas_call(
        body,
        out_shape=(shape, shape),
        in_specs=[pl.BlockSpec(memory_space=pltpu.SMEM)] + [VMEM] * 3,
        out_specs=(VMEM, VMEM),
        compiler_params=pltpu.CompilerParams(vmem_limit_bytes=12 << 20),
        cost_estimate=pl.CostEstimate(flops=1 << 20, bytes_accessed=8 << 20, transcendentals=0),
        name="weights",
    )(shifts, local_weight, side_weight, after)


def side_terms(sections, side_weight, real, partner, imag, ahead, behind):
    blocks, dimension = real.shape[0], real.shape[-1]
    flat = (dimension, dimension)

    def body(weight, real, partner, imag, ahead, behind, for_partner, own, middle, shared):
        outer = is_at(0, sections)
        chosen = first_is_far()
        for index in range(blocks):
            far = jnp.where(chosen, ahead[index], behind[index])
            near = jnp.where(chosen, behind[index], ahead[index])
            value = imag[index]
            for_partner[index] = weight[NEXT] * value + weight[OTHER] * far
            own[index] = weight[OWN] * value + weight[LONE] * far + weight[PAIR] * near
        last = blocks - 1
        middle[0] = partner[last]
        middle[1] = for_partner[last]
        middle[2] = own[last]
        for place, table in enumerate((real, partner, for_partner, own)):
            shared[place] = jnp.where(outer, table[last], table[0])

    def shape(count):
        return jax.ShapeDtypeStruct((count,) + flat, F32)

    return call(
        body,
        (shape(blocks), shape(blocks), shape(3), shape(4)),
        [side_weight, real, partner, imag, ahead, behind],
        1,
        "side_terms",
    )


def combine(sections, tables):
    names = list(tables)
    blocks, dimension = tables["real"].shape[0], tables["real"].shape[-1]

    def body(*refs):
        t = dict(zip(names, refs))
        to_first, to_second, to_partner, own = refs[len(names) :]
        a, b = t["local_weight"], t["side_weight"]
        outer = is_at(0, sections)
        chosen = first_is_far()
        last = blocks - 1
        for index in range(blocks):
            sides = []
            for place, name in enumerate(("real", "partner", "side_partner", "side_own")):
                table = t[name]
                if index == 0:
                    side = jnp.where(outer, 0.0, t["shared"][place])
                else:
                    side = table[index - 1]
                if index < last:
                    side = side + table[index + 1]
                else:
                    middle = t["middle_real"][...] if place == 0 else t["middle"][place - 1]
                    side = side + jnp.where(outer, t["shared"][place], middle)
                sides.append(side)
            n_real, n_partner, n_for, n_own = sides
            real, partner, imag = t["real"][index], t["partner"][index], t["imag"][index]
            ahead, behind = t["ahead"][index], t["behind"][index]
            far = jnp.where(chosen, ahead, behind)
            near = jnp.where(chosen, behind, ahead)
            pair = a[PAIR] * real + a[NEXT] * partner + b[PAIR] * n_real + b[NEXT] * n_partner
            lone = a[LONE] * real + b[LONE] * n_real
            to_first[index] = jnp.where(chosen, pair, lone)
            to_second[index] = jnp.where(chosen, lone, pair)
            to_partner[index] = a[NEXT] * imag + a[OTHER] * far + n_for
            own[2 * index] = (
                a[OWN] * real + a[OTHER] * partner + b[OWN] * n_real + b[OTHER] * n_partner
            )
            own[2 * index + 1] = a[OWN] * imag + a[LONE] * far + a[PAIR] * near + n_own

    def shape(count):
        return jax.ShapeDtypeStruct((count, dimension, dimension), F32)

    return call(
        body,
        (shape(blocks), shape(blocks), shape(blocks), shape(2 * blocks)),
        [tables[name] for name in names],
        1,
        "combine",
    )


def finish(sections, own, from_first, from_second, from_partner):
    blocks, dimension = from_first.shape[0], from_first.shape[-1]

    def body(own, from_first, from_second, from_partner, out):
        right_half = half_of(sections)
        for index in range(blocks):
            place = jnp.where(right_half, blocks - 1 - index, index)
            out[0, place, 0] = own[2 * index] + (from_first[index] + from_second[index])
            out[0, place, 1] = own[2 * index + 1] + from_partner[index]

    shape = jax.ShapeDtypeStruct((1, blocks, 2, dimension, dimension), F32)
    return call(body, shape, [own, from_first, from_second, from_partner], 1, "finish")


def local(
    onsite, hopping, coupling, broadening, born_sigma, phonon_shift, phonon_local, phonon_side
):
    blocks = onsite.shape[0]
    sections = lax.axis_size("section")
    spread = lax.axis_size("energy")
    assert born_sigma.shape[0] == 1 and spread % 2 == 0
    assert sections % 4 == 0 and sections // 4 == 1 and blocks >= 2
    half = sections // 2
    last = blocks - 1
    inwards = [(0, 1), (sections - 1, sections - 2)]
    outwards = [(b, a) for a, b in inwards]
    across = [(half - 1, half), (half, half - 1)]

    def over_section(value, route):
        return lax.ppermute(value, "section", route)

    def over_energy(value, route):
        return lax.ppermute(value, "energy", route)

    swap = [(e, e ^ 1) for e in range(spread)]
    pairs = [(e, e ^ 2) for e in range(spread)]
    first_swap = [(a, b) for a, b in pairs if b < spread]
    pairs = [(e, ((e + 2) ^ 2) - 2) for e in range(spread)]
    second_swap = [(a, b) for a, b in pairs if 0 <= b < spread]

    pack, edge, plain = prepare(
        sections, spread, broadening, onsite, hopping, coupling, born_sigma
    )
    before = over_section(plain, [(s, s + 1) for s in range(half - 1, sections - 1)])

    def inner_link(table, index, reverse=False):
        place = 2 * blocks + 2 * index
        return [(table, place + 1, place) if reverse else (table, place, place + 1)]

    end_link = [(edge, 0, 1), (before, True)]
    end_back = [(edge, 1, 0), (before, False)]

    first = []
    sigma = None
    for step in range(half):
        entering = []
        for index in range(blocks):
            entering.append(sigma)
            given = [] if sigma is None else [sigma]
            link = inner_link(pack, index) if index < last else end_link
            sigma = chain_step(sections, step, pack, index, given, link, f"inward{step}{index}")
        first.append(entering)
        leaving = sigma
        sigma = over_section(sigma, inwards if step < half - 1 else across)

    local_weight, side_weight = weights(phonon_shift, phonon_local, phonon_side, leaving)
    pack_in = over_section(pack, outwards)
    arriving = sigma
    earlier = tuple(first[step][last] for step in range(half))
    sigma = over_section(arriving, outwards)
    ready = green_step(
        sections, half - 1, pack, last, earlier[1:], (arriving,), f"green{last}inner"
    )
    for index in range(last, -1, -1):
        link = inner_link(pack_in, index - 1, True) if index > 0 else end_back
        after = ready if index == last else ()
        sigma = chain_step(
            sections, 0, pack_in, index, [sigma], link, f"relay{index}", after=after
        )
    green = green_step(
        sections, 0, pack, last, earlier[:1], (sigma,), f"green{last}outer", passed=ready
    )
    second = (sigma, arriving)
    joined = []
    for index in range(last, 0, -1):
        joined.insert(0, green)
        link = inner_link(pack, index - 1, True)
        second = (
            chain_step(
                sections, None, pack, index, second, link, f"outward{index}", after=green
            ),
        )
        earlier = tuple(first[step][index - 1] for step in range(half))
        green = green_step(
            sections,
            None,
            pack,
            index - 1,
            earlier,
            second,
            f"green{index - 1}",
            joined=joined if index == 1 else (),
        )
    real, imag = green
    partner = over_energy(real, swap)
    ahead = over_energy(imag, first_swap)
    behind = over_energy(imag, second_swap)
    middle_real = over_section(joined[-1][0], across)

    side_partner, side_own, middle, shared = side_terms(
        sections, side_weight, real, partner, imag, ahead, behind
    )
    middle = over_section(middle, across)
    shared = over_section(shared, inwards + outwards)
    to_first, to_second, to_partner, own = combine(
        sections,
        {
            "local_weight": local_weight,
            "side_weight": side_weight,
            "real": real,
            "partner": partner,
            "imag": imag,
            "ahead": ahead,
            "behind": behind,
            "side_partner": side_partner,
            "side_own": side_own,
            "middle_real": middle_real,
            "middle": middle,
            "shared": shared,
        },
    )
    return finish(
        sections,
        own,
        over_energy(to_first, first_swap),
        over_energy(to_second, second_swap),
        over_energy(to_partner, swap),
    )


def solution(mesh):
    in_specs = (
        P("section", None),
        P("section", None, None),
        P("section", None, None),
        P("energy"),
        P("energy", "section", None, None, None),
        P(),
        P(),
        P(),
    )
    out_specs = P("energy", "section", None, None, None)
    return jax.shard_map(local, mesh=mesh, in_specs=in_specs, out_specs=out_specs, check_vma=False)
```

profile of v0, /device:TPU:1, one launch (start us, length us, event | category | flops | bytes accessed | tf_op | source)
XLA Modules:
  0.0 90.8 jit_solution(2366816085686263766)
XLA Ops:
  0.7 1.2 %copy-done = f32[1,2,2,256,256]{4,3,2,1,0:T(8,128)S(1)} copy-done((f32[1,2,2,256,256]{4,3,2,1,0:T(8,128)S(1)}, f32[1,2,2,256,256]{4,3,2,1,0:T(8,128)}, u32[]{:S(2)}) %copy-start) | copy-done | bytes 1048600
  1.9 1.0 %copy-done.3 = f32[2,256,256]{2,1,0:T(8,128)S(1)} copy-done((f32[2,256,256]{2,1,0:T(8,128)S(1)}, f32[2,256,256]{2,1,0:T(8,128)}, u32[]{:S(2)}) %copy-start.3) | copy-done | bytes 524312
  2.9 1.0 %copy-done.4 = f32[2,256,256]{2,1,0:T(8,128)S(1)} copy-done((f32[2,256,256]{2,1,0:T(8,128)S(1)}, f32[2,256,256]{2,1,0:T(8,128)}, u32[]{:S(2)}) %copy-start.4) | copy-done | bytes 524312
  4.6 0.9 prepare.1
  5.5 4.5 %collective-permute-start = (f32[256,256]{1,0:T(8,128)S(1)}, f32[256,256]{1,0:T(8,128)S(1)}, u32[]{:S(2)}, u32[]{:S(2)}) collective-permute-start(f32[256,256]{1,0:T(8,128)S(1)} %get-tuple-element.26), channel_id=1, source_target_pairs={{1,2},{2,3},{5,6},{6,7},{9,10},{10,11},{13,14},{14,15},{17,18},{18... | collective-permute-start | bytes 786440 | tf_op jit(solution)/shard_map/ppermute | solution.py:431
  10.1 3.2 %collective-permute-done.refs_3_ = f32[256,256]{1,0:T(8,128)S(1)} collective-permute-done((f32[256,256]{1,0:T(8,128)S(1)}, f32[256,256]{1,0:T(8,128)S(1)}, u32[]{:S(2)}, u32[]{:S(2)}) %collective-permute-start) | collective-permute-done | bytes 262176 | tf_op jit(solution)/shard_map/ppermute | solution.py:431
  13.4 1.3 %collective-permute-start.1 = (f32[2,256,256]{2,1,0:T(8,128)S(1)}, f32[2,256,256]{2,1,0:T(8,128)S(1)}, u32[]{:S(2)}, u32[]{:S(2)}) collective-permute-start(f32[2,256,256]{2,1,0:T(8,128)S(1)} %inward01.1), channel_id=1, source_target_pairs={{0,1},{3,2},{4,5},{7,6},{8,9},{11,10},{12,13},{15,14},{16,17},{19,... | collective-permute-start | bytes 1572872 | tf_op jit(solution)/shard_map/ppermute | solution.py:431
  14.7 3.2 %collective-permute-start.2 = (f32[6,256,256]{2,1,0:T(8,128)S(1)}, f32[6,256,256]{2,1,0:T(8,128)S(1)}, u32[]{:S(2)}, u32[]{:S(2)}) collective-permute-start(f32[6,256,256]{2,1,0:T(8,128)S(1)} %get-tuple-element.24.refs_0_.refs_1_.refs_2_.refs_3_), channel_id=1, source_target_pairs={{1,0},{2,3},{5,4},{6,7},{9,8},{10,11},{13,12},{14,15},{17,16},{18,... | collective-permute-start | bytes 4718600 | tf_op jit(solution)/shard_map/ppermute | solution.py:431
  17.9 2.3 %inward10.1.refs_1_ = f32[2,256,256]{2,1,0:T(8,128)S(1)} custom-call(f32[6,256,256]{2,1,0:T(8,128)S(1)} %get-tuple-element.24.refs_0_.refs_1_.refs_2_.refs_3_, f32[2,256,256]{2,1,0:T(8,128)S(1)} %collective-permute-done.1.refs_1_, f32[6,256,256]{2,1,0:T(8,128)S(1)} %get-tuple-element.24.refs_0_.refs_1_.refs_2_.refs_3_), custom_call_target="tpu_custom_call" | custom-call | flops 1610612736 | bytes 2097152 | tf_op jit(solution)/shard_map/inward10/pallas_call | solution.py:98
  20.1 2.3 %inward11.1._ = f32[2,256,256]{2,1,0:T(8,128)S(1)} custom-call(f32[6,256,256]{2,1,0:T(8,128)S(1)} %get-tuple-element.24.refs_0_.refs_1_.refs_2_.refs_3_, f32[2,256,256]{2,1,0:T(8,128)S(1)} %inward10.1.refs_1_, f32[2,256,256]{2,1,0:T(8,128)S(1)} %get-tuple-element.25.refs_2_, f32[256,256]{1,0:T(8,128)S(1)} %collective-permute-done.refs_3_), custom_call_target="tpu_custom_call" | custom-call | flops 1610612736 | bytes 2097152 | tf_op jit(solution)/shard_map/inward11/pallas_call | solution.py:98
  22.4 4.4 %collective-permute-start.3 = (f32[2,256,256]{2,1,0:T(8,128)S(1)}, f32[2,256,256]{2,1,0:T(8,128)S(1)}, u32[]{:S(2)}, u32[]{:S(2)}) collective-permute-start(f32[2,256,256]{2,1,0:T(8,128)S(1)} %inward11.1._), channel_id=1, source_target_pairs={{1,2},{2,1},{5,6},{6,5},{9,10},{10,9},{13,14},{14,13},{17,18},{18,... | collective-permute-start | bytes 1572872 | tf_op jit(solution)/shard_map/ppermute | solution.py:431
  26.8 6.8 %collective-permute-done.3.refs_2_ = f32[2,256,256]{2,1,0:T(8,128)S(1)} collective-permute-done((f32[2,256,256]{2,1,0:T(8,128)S(1)}, f32[2,256,256]{2,1,0:T(8,128)S(1)}, u32[]{:S(2)}, u32[]{:S(2)}) %collective-permute-start.3) | collective-permute-done | bytes 524320 | tf_op jit(solution)/shard_map/ppermute | solution.py:431
  33.7 1.3 %collective-permute-start.4 = (f32[2,256,256]{2,1,0:T(8,128)S(1)}, f32[2,256,256]{2,1,0:T(8,128)S(1)}, u32[]{:S(2)}, u32[]{:S(2)}) collective-permute-start(f32[2,256,256]{2,1,0:T(8,128)S(1)} %collective-permute-done.3.refs_2_), channel_id=1, source_target_pairs={{1,0},{2,3},{5,4},{6,7},{9,8},{10,11},{13,12},{14,15},{17,16},{18,... | collective-permute-start | bytes 1572872 | tf_op jit(solution)/shard_map/ppermute | solution.py:431
  35.0 1.9 %green1inner.1 = (f32[256,256]{1,0:T(8,128)S(1)}, f32[256,256]{1,0:T(8,128)S(1)}) custom-call(f32[6,256,256]{2,1,0:T(8,128)S(1)} %get-tuple-element.24.refs_0_.refs_1_.refs_2_.refs_3_, f32[2,256,256]{2,1,0:T(8,128)S(1)} %inward10.1.refs_1_, f32[2,256,256]{2,1,0:T(8,128)S(1)} %collective-permute-done.3.refs_2_), custom_call_target="tpu_custom_call" | custom-call | flops 1207959552 | bytes 2097152 | tf_op jit(solution)/shard_map/green1inner/pallas_call | solution.py:98
  37.3 2.3 %outward1.1.refs_2_ = f32[2,256,256]{2,1,0:T(8,128)S(1)} custom-call(f32[6,256,256]{2,1,0:T(8,128)S(1)} %get-tuple-element.24.refs_0_.refs_1_.refs_2_.refs_3_, f32[2,256,256]{2,1,0:T(8,128)S(1)} %relay0.1.refs_2_.refs_1_, f32[2,256,256]{2,1,0:T(8,128)S(1)} %collective-permute-done.3.refs_2_, ...), custom_call_target="tpu_custom_call" | custom-call | flops 1610612736 | bytes 2097152 | tf_op jit(solution)/shard_map/outward1/pallas_call | solution.py:98
  39.6 1.8 %green0.1 = (f32[2,256,256]{2,1,0:T(8,128)S(1)}, f32[2,256,256]{2,1,0:T(8,128)S(1)}) custom-call(f32[6,256,256]{2,1,0:T(8,128)S(1)} %get-tuple-element.24.refs_0_.refs_1_.refs_2_.refs_3_, f32[2,256,256]{2,1,0:T(8,128)S(1)} %collective-permute-done.1.refs_1_, f32[2,256,256]{2,1,0:T(8,128)S(1)} %outward1.1.refs_2_, ...), custom_call_target="tpu_custom_call" | custom-call | flops 1207959552 | bytes 2097152 | tf_op jit(solution)/shard_map/green0/pallas_call | solution.py:98
  41.4 1.3 %collective-permute-start.5 = (f32[2,256,256]{2,1,0:T(8,128)S(1)}, f32[2,256,256]{2,1,0:T(8,128)S(1)}, u32[]{:S(2)}, u32[]{:S(2)}) collective-permute-start(f32[2,256,256]{2,1,0:T(8,128)S(1)} %get-tuple-element.33.real.refs_2_), channel_id=1, source_target_pairs={{0,4},{4,0},{8,12},{12,8},{16,20},{20,16},{24,28},{28,24},{1,5},{5... | collective-permute-start | bytes 1572872 | tf_op jit(solution)/shard_map/ppermute | solution.py:434
  42.8 0.7 collective-permute-start.7
  43.4 3.9 %collective-permute-start.6 = (f32[2,256,256]{2,1,0:T(8,128)S(1)}, f32[2,256,256]{2,1,0:T(8,128)S(1)}, u32[]{:S(2)}, u32[]{:S(2)}) collective-permute-start(f32[2,256,256]{2,1,0:T(8,128)S(1)} %get-tuple-element.34.imag.refs_4_), channel_id=1, source_target_pairs={{0,8},{4,12},{8,0},{12,4},{16,24},{20,28},{24,16},{28,20},{1,9},{5... | collective-permute-start | bytes 1572872 | tf_op jit(solution)/shard_map/ppermute | solution.py:434
  47.3 1.4 %weights.1 = (f32[5,256,256]{2,1,0:T(8,128)S(1)}, f32[5,256,256]{2,1,0:T(8,128)S(1)}) custom-call(s32[4]{0:T(128)S(1)} %copy-done.6, f32[4,256,256]{2,1,0:T(8,128)S(1)} %copy-done.1, f32[4,256,256]{2,1,0:T(8,128)S(1)} %copy-done.2, f32[2,256,256]{2,1,0:T(8,128)S(1)} %inward11.1._), custom_call_target="tpu_custom_call" | custom-call | flops 1048576 | bytes 8388608 | tf_op jit(solution)/shard_map/weights/pallas_call | solution.py:307
  48.7 0.8 collective-permute-done.5.partner.refs_3_
  49.5 4.6 %collective-permute-done.6.ahead.refs_5_ = f32[2,256,256]{2,1,0:T(8,128)S(1)} collective-permute-done((f32[2,256,256]{2,1,0:T(8,128)S(1)}, f32[2,256,256]{2,1,0:T(8,128)S(1)}, u32[]{:S(2)}, u32[]{:S(2)}) %collective-permute-start.6) | collective-permute-done | bytes 524320 | tf_op jit(solution)/shard_map/ppermute | solution.py:434
  54.8 7.2 %collective-permute-start.10 = (f32[4,256,256]{2,1,0:T(8,128)S(1)}, f32[4,256,256]{2,1,0:T(8,128)S(1)}, u32[]{:S(2)}, u32[]{:S(2)}) collective-permute-start(f32[4,256,256]{2,1,0:T(8,128)S(1)} %get-tuple-element.38), channel_id=1, source_target_pairs={{0,1},{3,2},{1,0},{2,3},{4,5},{7,6},{5,4},{6,7},{8,9},{11,10},{9,8... | collective-permute-start | bytes 3145736 | tf_op jit(solution)/shard_map/ppermute | solution.py:431
  62.0 3.0 %collective-permute-start.9 = (f32[3,256,256]{2,1,0:T(8,128)S(1)}, f32[3,256,256]{2,1,0:T(8,128)S(1)}, u32[]{:S(2)}, u32[]{:S(2)}) collective-permute-start(f32[3,256,256]{2,1,0:T(8,128)S(1)} %get-tuple-element.37), channel_id=1, source_target_pairs={{1,2},{2,1},{5,6},{6,5},{9,10},{10,9},{13,14},{14,13},{17,18},{18,... | collective-permute-start | bytes 2359304 | tf_op jit(solution)/shard_map/ppermute | solution.py:431
  65.1 2.5 %collective-permute-start.8 = (f32[256,256]{1,0:T(8,128)S(1)}, f32[256,256]{1,0:T(8,128)S(1)}, u32[]{:S(2)}, u32[]{:S(2)}) collective-permute-start(f32[256,256]{1,0:T(8,128)S(1)} %get-tuple-element.31.refs_4_.refs_3_), channel_id=1, source_target_pairs={{1,2},{2,1},{5,6},{6,5},{9,10},{10,9},{13,14},{14,13},{17,18},{18,... | collective-permute-start | bytes 786440 | tf_op jit(solution)/shard_map/ppermute | solution.py:431
  67.6 10.5 %collective-permute-done.8.refs_9_ = f32[256,256]{1,0:T(8,128)S(1)} collective-permute-done((f32[256,256]{1,0:T(8,128)S(1)}, f32[256,256]{1,0:T(8,128)S(1)}, u32[]{:S(2)}, u32[]{:S(2)}) %collective-permute-start.8) | collective-permute-done | bytes 262176 | tf_op jit(solution)/shard_map/ppermute | solution.py:431
  78.1 1.0 %combine.1 = (f32[2,256,256]{2,1,0:T(8,128)S(1)}, f32[2,256,256]{2,1,0:T(8,128)S(1)}, f32[2,256,256]{2,1,0:T(8,128)S(1)}, f32[4,256,256]{2,1,0:T(8,128)S(1)}) custom-call(f32[5,256,256]{2,1,0:T(8,128)S(1)} %get-tuple-element.27.refs_0_, f32[5,256,256]{2,1,0:T(8,128)S(1)} %get-tuple-element.28.weight.refs_1_, ...), custom_call_target="tpu_custom_call" | custom-call | flops 100663296 | bytes 2097152 | tf_op jit(solution)/shard_map/combine/pallas_call | solution.py:98
  79.1 1.8 %collective-permute-start.11 = (f32[2,256,256]{2,1,0:T(8,128)S(1)}, f32[2,256,256]{2,1,0:T(8,128)S(1)}, u32[]{:S(2)}, u32[]{:S(2)}) collective-permute-start(f32[2,256,256]{2,1,0:T(8,128)S(1)} %get-tuple-element.40), channel_id=1, source_target_pairs={{0,8},{4,12},{8,0},{12,4},{16,24},{20,28},{24,16},{28,20},{1,9},{5... | collective-permute-start | bytes 1572872 | tf_op jit(solution)/shard_map/ppermute | solution.py:434
  80.9 0.7 collective-permute-start.12
  81.9 5.6 %collective-permute-done.11.from_first = f32[2,256,256]{2,1,0:T(8,128)S(1)} collective-permute-done((f32[2,256,256]{2,1,0:T(8,128)S(1)}, f32[2,256,256]{2,1,0:T(8,128)S(1)}, u32[]{:S(2)}, u32[]{:S(2)}) %collective-permute-start.11) | collective-permute-done | bytes 524320 | tf_op jit(solution)/shard_map/ppermute | solution.py:434
  87.5 2.2 %collective-permute-done.13.from_partner = f32[2,256,256]{2,1,0:T(8,128)S(1)} collective-permute-done((f32[2,256,256]{2,1,0:T(8,128)S(1)}, f32[2,256,256]{2,1,0:T(8,128)S(1)}, u32[]{:S(2)}, u32[]{:S(2)}) %collective-permute-start.13) | collective-permute-done | bytes 524320 | tf_op jit(solution)/shard_map/ppermute | solution.py:434
  89.7 1.1 %finish.1 = f32[1,2,2,256,256]{4,3,2,1,0:T(8,128)} custom-call(f32[4,256,256]{2,1,0:T(8,128)S(1)} %get-tuple-element.39.own, f32[2,256,256]{2,1,0:T(8,128)S(1)} %collective-permute-done.11.from_first, f32[2,256,256]{2,1,0:T(8,128)S(1)} %collective-permute-done.12.from_second, f32[2,256,256]{2,1,0:T(8,128)S(1)} %collective-permute-done.13.from_partner), custom_call_target="tpu_custom_call" | custom-call | flops 100663296 | bytes 2097152 | tf_op jit(solution)/shard_map/finish/pallas_call | solution.py:98
  (25 shorter events, 2.0 us)
Async XLA Ops:
  0.7 1.2 %copy-start = (f32[1,2,2,256,256]{4,3,2,1,0:T(8,128)S(1)}, f32[1,2,2,256,256]{4,3,2,1,0:T(8,128)}, u32[]{:S(2)}) copy-start(f32[1,2,2,256,256]{4,3,2,1,0:T(8,128)} %born.1) | copy-start | bytes 3145732
  1.9 1.0 %copy-start.3 = (f32[2,256,256]{2,1,0:T(8,128)S(1)}, f32[2,256,256]{2,1,0:T(8,128)}, u32[]{:S(2)}) copy-start(f32[2,256,256]{2,1,0:T(8,128)} %hopping.1) | copy-start | bytes 1572868
  2.9 1.0 %copy-start.4 = (f32[2,256,256]{2,1,0:T(8,128)S(1)}, f32[2,256,256]{2,1,0:T(8,128)}, u32[]{:S(2)}) copy-start(f32[2,256,256]{2,1,0:T(8,128)} %coupling.1) | copy-start | bytes 1572868
  4.0 0.7 copy-start.5
  5.5 7.8 %collective-permute-start = (f32[256,256]{1,0:T(8,128)S(1)}, f32[256,256]{1,0:T(8,128)S(1)}, u32[]{:S(2)}, u32[]{:S(2)}) collective-permute-start(f32[256,256]{1,0:T(8,128)S(1)} %get-tuple-element.26), channel_id=1, source_target_pairs={{1,2},{2,3},{5,6},{6,7},{9,10},{10,11},{13,14},{14,15},{17,18},{18... | collective-permute-start | bytes 786440 | tf_op jit(solution)/shard_map/ppermute | solution.py:431
  13.4 4.5 %collective-permute-start.1 = (f32[2,256,256]{2,1,0:T(8,128)S(1)}, f32[2,256,256]{2,1,0:T(8,128)S(1)}, u32[]{:S(2)}, u32[]{:S(2)}) collective-permute-start(f32[2,256,256]{2,1,0:T(8,128)S(1)} %inward01.1), channel_id=1, source_target_pairs={{0,1},{3,2},{4,5},{7,6},{8,9},{11,10},{12,13},{15,14},{16,17},{19,... | collective-permute-start | bytes 1572872 | tf_op jit(solution)/shard_map/ppermute | solution.py:431
  14.7 22.2 %collective-permute-start.2 = (f32[6,256,256]{2,1,0:T(8,128)S(1)}, f32[6,256,256]{2,1,0:T(8,128)S(1)}, u32[]{:S(2)}, u32[]{:S(2)}) collective-permute-start(f32[6,256,256]{2,1,0:T(8,128)S(1)} %get-tuple-element.24.refs_0_.refs_1_.refs_2_.refs_3_), channel_id=1, source_target_pairs={{1,0},{2,3},{5,4},{6,7},{9,8},{10,11},{13,12},{14,15},{17,16},{18,... | collective-permute-start | bytes 4718600 | tf_op jit(solution)/shard_map/ppermute | solution.py:431
  22.4 11.2 %collective-permute-start.3 = (f32[2,256,256]{2,1,0:T(8,128)S(1)}, f32[2,256,256]{2,1,0:T(8,128)S(1)}, u32[]{:S(2)}, u32[]{:S(2)}) collective-permute-start(f32[2,256,256]{2,1,0:T(8,128)S(1)} %inward11.1._), channel_id=1, source_target_pairs={{1,2},{2,1},{5,6},{6,5},{9,10},{10,9},{13,14},{14,13},{17,18},{18,... | collective-permute-start | bytes 1572872 | tf_op jit(solution)/shard_map/ppermute | solution.py:431
  33.7 3.2 %collective-permute-start.4 = (f32[2,256,256]{2,1,0:T(8,128)S(1)}, f32[2,256,256]{2,1,0:T(8,128)S(1)}, u32[]{:S(2)}, u32[]{:S(2)}) collective-permute-start(f32[2,256,256]{2,1,0:T(8,128)S(1)} %collective-permute-done.3.refs_2_), channel_id=1, source_target_pairs={{1,0},{2,3},{5,4},{6,7},{9,8},{10,11},{13,12},{14,15},{17,16},{18,... | collective-permute-start | bytes 1572872 | tf_op jit(solution)/shard_map/ppermute | solution.py:431
  39.5 7.8 %copy-start.1 = (f32[4,256,256]{2,1,0:T(8,128)S(1)}, f32[4,256,256]{2,1,0:T(8,128)}, u32[]{:S(2)}) copy-start(f32[4,256,256]{2,1,0:T(8,128)} %local_ref.1) | copy-start | bytes 3145732
  39.6 7.8 %copy-start.2 = (f32[4,256,256]{2,1,0:T(8,128)S(1)}, f32[4,256,256]{2,1,0:T(8,128)}, u32[]{:S(2)}) copy-start(f32[4,256,256]{2,1,0:T(8,128)} %side_ref.1) | copy-start | bytes 3145732
  39.6 7.7 %copy-start.6 = (s32[4]{0:T(128)S(1)}, s32[4]{0:T(128)}, u32[]{:S(2)}) copy-start(s32[4]{0:T(128)} %shift_ref.1) | copy-start | bytes 52
  41.4 8.1 %collective-permute-start.5 = (f32[2,256,256]{2,1,0:T(8,128)S(1)}, f32[2,256,256]{2,1,0:T(8,128)S(1)}, u32[]{:S(2)}, u32[]{:S(2)}) collective-permute-start(f32[2,256,256]{2,1,0:T(8,128)S(1)} %get-tuple-element.33.real.refs_2_), channel_id=1, source_target_pairs={{0,4},{4,0},{8,12},{12,8},{16,20},{20,16},{24,28},{28,24},{1,5},{5... | collective-permute-start | bytes 1572872 | tf_op jit(solution)/shard_map/ppermute | solution.py:434
  42.8 6.8 %collective-permute-start.7 = (f32[2,256,256]{2,1,0:T(8,128)S(1)}, f32[2,256,256]{2,1,0:T(8,128)S(1)}, u32[]{:S(2)}, u32[]{:S(2)}) collective-permute-start(f32[2,256,256]{2,1,0:T(8,128)S(1)} %get-tuple-element.34.imag.refs_4_), channel_id=1, source_target_pairs={{8,16},{12,20},{16,8},{20,12},{9,17},{13,21},{17,9},{21,13},{10,18... | collective-permute-start | bytes 1572872 | tf_op jit(solution)/shard_map/ppermute | solution.py:434
  43.4 10.7 %collective-permute-start.6 = (f32[2,256,256]{2,1,0:T(8,128)S(1)}, f32[2,256,256]{2,1,0:T(8,128)S(1)}, u32[]{:S(2)}, u32[]{:S(2)}) collective-permute-start(f32[2,256,256]{2,1,0:T(8,128)S(1)} %get-tuple-element.34.imag.refs_4_), channel_id=1, source_target_pairs={{0,8},{4,12},{8,0},{12,4},{16,24},{20,28},{24,16},{28,20},{1,9},{5... | collective-permute-start | bytes 1572872 | tf_op jit(solution)/shard_map/ppermute | solution.py:434
  54.8 23.3 %collective-permute-start.10 = (f32[4,256,256]{2,1,0:T(8,128)S(1)}, f32[4,256,256]{2,1,0:T(8,128)S(1)}, u32[]{:S(2)}, u32[]{:S(2)}) collective-permute-start(f32[4,256,256]{2,1,0:T(8,128)S(1)} %get-tuple-element.38), channel_id=1, source_target_pairs={{0,1},{3,2},{1,0},{2,3},{4,5},{7,6},{5,4},{6,7},{8,9},{11,10},{9,8... | collective-permute-start | bytes 3145736 | tf_op jit(solution)/shard_map/ppermute | solution.py:431
  62.0 16.1 %collective-permute-start.9 = (f32[3,256,256]{2,1,0:T(8,128)S(1)}, f32[3,256,256]{2,1,0:T(8,128)S(1)}, u32[]{:S(2)}, u32[]{:S(2)}) collective-permute-start(f32[3,256,256]{2,1,0:T(8,128)S(1)} %get-tuple-element.37), channel_id=1, source_target_pairs={{1,2},{2,1},{5,6},{6,5},{9,10},{10,9},{13,14},{14,13},{17,18},{18,... | collective-permute-start | bytes 2359304 | tf_op jit(solution)/shard_map/ppermute | solution.py:431
  65.1 13.0 %collective-permute-start.8 = (f32[256,256]{1,0:T(8,128)S(1)}, f32[256,256]{1,0:T(8,128)S(1)}, u32[]{:S(2)}, u32[]{:S(2)}) collective-permute-start(f32[256,256]{1,0:T(8,128)S(1)} %get-tuple-element.31.refs_4_.refs_3_), channel_id=1, source_target_pairs={{1,2},{2,1},{5,6},{6,5},{9,10},{10,9},{13,14},{14,13},{17,18},{18,... | collective-permute-start | bytes 786440 | tf_op jit(solution)/shard_map/ppermute | solution.py:431
  79.1 8.4 %collective-permute-start.11 = (f32[2,256,256]{2,1,0:T(8,128)S(1)}, f32[2,256,256]{2,1,0:T(8,128)S(1)}, u32[]{:S(2)}, u32[]{:S(2)}) collective-permute-start(f32[2,256,256]{2,1,0:T(8,128)S(1)} %get-tuple-element.40), channel_id=1, source_target_pairs={{0,8},{4,12},{8,0},{12,4},{16,24},{20,28},{24,16},{28,20},{1,9},{5... | collective-permute-start | bytes 1572872 | tf_op jit(solution)/shard_map/ppermute | solution.py:434
  80.9 6.6 %collective-permute-start.12 = (f32[2,256,256]{2,1,0:T(8,128)S(1)}, f32[2,256,256]{2,1,0:T(8,128)S(1)}, u32[]{:S(2)}, u32[]{:S(2)}) collective-permute-start(f32[2,256,256]{2,1,0:T(8,128)S(1)} %get-tuple-element.41), channel_id=1, source_target_pairs={{8,16},{12,20},{16,8},{20,12},{9,17},{13,21},{17,9},{21,13},{10,18... | collective-permute-start | bytes 1572872 | tf_op jit(solution)/shard_map/ppermute | solution.py:434
  81.6 8.1 %collective-permute-start.13 = (f32[2,256,256]{2,1,0:T(8,128)S(1)}, f32[2,256,256]{2,1,0:T(8,128)S(1)}, u32[]{:S(2)}, u32[]{:S(2)}) collective-permute-start(f32[2,256,256]{2,1,0:T(8,128)S(1)} %get-tuple-element.42), channel_id=1, source_target_pairs={{0,4},{4,0},{8,12},{12,8},{16,20},{20,16},{24,28},{28,24},{1,5},{5... | collective-permute-start | bytes 1572872 | tf_op jit(solution)/shard_map/ppermute | solution.py:434
where the time goes:
time: 91.4 us; the launch traced here: 90.8 us
  starting transfers between devices  36.1 us (39%)
  waiting for transfers between devices  33.9 us (37%)
  Pallas kernels  15.9 us (17%)
  local copies, waits for them, and re-layouts  4 us (4%)
    ppermute x8, starting transfers between devices, over_section(): return lax.ppermute(value, 'section', route)  27.4 us
    ppermute x8, waiting for transfers between devices, over_section(): return lax.ppermute(value, 'section', route)  20.6 us
    pallas_call x13, Pallas kernels, call(): pl.pallas_call(body, out_shape=out_shape, in_specs=[VMEM] * len(operands)...  13.7 us
    ppermute x6, waiting for transfers between devices, over_energy(): return lax.ppermute(value, 'energy', route)  13.3 us
    ppermute x6, starting transfers between devices, over_energy(): return lax.ppermute(value, 'energy', route)  8.64 us
    unnamed x14, local copies, waits for them, and re-layouts  4 us
  transfers between devices with their start and end apart: 14, of which 7 were waited for; matrix products, arithmetic and copies ran while one was open for 0% of the time, Pallas kernels for 9%

commit v1 on v0

--- a/solution.py
+++ b/solution.py
@@ -6,6 +6,7 @@
 from jax.experimental import pallas as pl
 from jax.experimental.pallas import tpu as pltpu
 from jax.sharding import PartitionSpec as P
+
 
 F32 = jnp.float32
 BF16 = jnp.bfloat16
@@ -55,11 +56,6 @@
     x_real = row_real * t_real - row_imag * e_imag
     x_imag = row_real * e_imag + row_imag * t_real
     return e_real, e_imag, x_real, x_imag
-
-
-def is_active(step, sections):
-    slot = lax.axis_index("section")
-    return jnp.logical_or(slot == step, slot == sections - 1 - step)
 
 
 def series_square(real, imag):
@@ -92,7 +88,18 @@
     out[1] = s_imag
 
 
-def call(body, out_shape, operands, products, name):
+def inverse_core(real, imag, put):
+    x_real, x_imag, f_parts = series_square(real, imag)
+    b_real, b_imag = complex_product(parts(x_real, x_imag), f_parts)
+    g_real, g_imag = complex_product(f_parts, f_parts)
+    b_real = b_real + x_real
+    b_imag = b_imag + x_imag
+    s_real, s_imag = complex_product(parts(b_real, b_imag), parts(g_real, g_imag))
+    put(0, b_real + s_real)
+    put(1, b_imag + s_imag)
+
+
+def call(body, out_shape, operands, products):
     dimension = operands[0].shape[-1]
     size = dimension * dimension
     return pl.pallas_call(
@@ -104,22 +111,38 @@
         cost_estimate=pl.CostEstimate(
             flops=6 * products * size * dimension, bytes_accessed=4 * 8 * size, transcendentals=0
         ),
-        name=name,
     )(*operands)
 
 
+def enter_step(sections, active, coupled_half, pack, given):
+    place = pack.shape[0] - 2
+
+    def body(source, value, out):
+        mine = is_at(active, sections)
+        coupled = half_of(sections) if coupled_half else jnp.logical_not(half_of(sections))
+
+        @pl.when(jnp.logical_and(mine, coupled))
+        def _():
+            link, link_t = split(source[place]), split(source[place + 1])
+            for part in (0, 1):
+                out[part] = product(split(product(link, split(value[part]))), link_t)
+
+        @pl.when(jnp.logical_not(jnp.logical_and(mine, coupled)))
+        def _():
+            out[...] = value[...]
+
+    return call(body, jax.ShapeDtypeStruct(given.shape, F32), [pack, given], 4)
+
+
 def link_ways(sections, refs, links):
-    table, near, away = refs[0], links[0][1], links[0][2]
-    if len(links) == 1:
-        return table[near], table[away]
+    ways = [(ref[link[1]], ref[link[2]]) for ref, link in zip(refs, links)]
+    if len(ways) == 1:
+        return ways[0]
     right_half = half_of(sections)
-    plain = refs[1][...]
-    turned = plain.T
-    link, link_t = (turned, plain) if links[1][1] else (plain, turned)
-    return jnp.where(right_half, link, table[near]), jnp.where(right_half, link_t, table[away])
-
-
-def chain_step(sections, active, pack, block, sigmas, links, name, after=()):
+    return tuple(jnp.where(right_half, b, a) for a, b in zip(*ways))
+
+
+def chain_step(sections, active, pack, block, sigmas, links, after=(), leaves=False):
     arrays = [pack] + list(sigmas) + [link[0] for link in links]
     count = len(arrays)
 
@@ -137,7 +160,18 @@
                 real = real - jnp.where(outer, given[0][0], given[1][0])
                 imag = imag - jnp.where(outer, given[0][1], given[1][1])
             link, link_t = link_ways(sections, refs[1 + len(sigmas) : count], links)
-            chain_core(real, imag, link, link_t, out)
+            if not leaves:
+                chain_core(real, imag, link, link_t, out)
+                return
+
+            def put(place, value):
+                out[place] = value
+
+            right_half = half_of(sections)
+            pl.when(right_half)(lambda: inverse_core(real, imag, put))
+            pl.when(jnp.logical_not(right_half))(
+                lambda: chain_core(real, imag, link, link_t, out)
+            )
 
         if active is None:
             work()
@@ -150,13 +184,13 @@
                 out[...] = jnp.zeros_like(out)
 
     shape = jax.ShapeDtypeStruct((2,) + pack.shape[1:], F32)
-    return call(body, shape, arrays + list(after), 16, name)
-
-
-def green_step(sections, active, pack, block, first, second, name, passed=(), joined=()):
+    return call(body, shape, arrays + list(after), 16)
+
+
+def green_step(sections, active, pack, block, first, second, passed=(), joined=(), after=()):
     arrays = [pack] + [a for a in first + second if a is not None]
     count = len(arrays)
-    arrays = arrays + list(passed) + [a for pair in joined for a in pair]
+    arrays = arrays + list(passed) + [a for pair in joined for a in pair] + list(after)
     size = 1 + len(joined)
 
     def body(*refs):
@@ -180,14 +214,7 @@
                     ]
                     term = terms[0] if len(terms) == 1 else jnp.where(outer, *terms)
                     value[place] = value[place] - term
-            x_real, x_imag, f_parts = series_square(*value)
-            b_real, b_imag = complex_product(parts(x_real, x_imag), f_parts)
-            g_real, g_imag = complex_product(f_parts, f_parts)
-            b_real = b_real + x_real
-            b_imag = b_imag + x_imag
-            s_real, s_imag = complex_product(parts(b_real, b_imag), parts(g_real, g_imag))
-            put(0, b_real + s_real)
-            put(1, b_imag + s_imag)
+            inverse_core(*value, put)
 
         if active is None:
             work()
@@ -208,11 +235,11 @@
                 outs[place][1 + number] = refs[count + len(passed) + 2 * number + place][...]
 
     flat = jax.ShapeDtypeStruct(((size,) if joined else ()) + pack.shape[1:], F32)
-    return call(body, (flat, flat), arrays, 12, name)
+    return call(body, (flat, flat), arrays, 12)
 
 
 def prepare_kernel(
-    sections, spread, broadening, onsite, hopping, coupling, born, pack, edge, plain, hop, cup, sig, sems
+    sections, spread, broadening, onsite, hopping, coupling, born, pack, hop, cup, sig, sems
 ):
     blocks, dimension = onsite.shape
     copies = []
@@ -250,9 +277,8 @@
             pack[place + flip] = link
             pack[place + 1 - flip] = link.T
         else:
-            plain[...] = link
-            edge[0] = link
-            edge[1] = link.T
+            pack[4 * blocks - 2] = link
+            pack[4 * blocks - 1] = link.T
 
 
 def prepare(sections, spread, broadening, onsite, hopping, coupling, born):
@@ -260,13 +286,9 @@
     outside = pl.BlockSpec(memory_space=pltpu.HBM)
     return pl.pallas_call(
         functools.partial(prepare_kernel, sections, spread),
-        out_shape=(
-            jax.ShapeDtypeStruct((4 * blocks - 2, dimension, dimension), F32),
-            jax.ShapeDtypeStruct((2, dimension, dimension), F32),
-            jax.ShapeDtypeStruct((dimension, dimension), F32),
-        ),
+        out_shape=jax.ShapeDtypeStruct((4 * blocks, dimension, dimension), F32),
         in_specs=[VMEM, VMEM, outside, outside, outside],
-        out_specs=(VMEM, VMEM, VMEM),
+        out_specs=VMEM,
         scratch_shapes=[
             pltpu.VMEM((blocks, dimension, dimension), F32),
             pltpu.VMEM((blocks, dimension, dimension), F32),
@@ -315,11 +337,11 @@
     )(shifts, local_weight, side_weight, after)
 
 
-def side_terms(sections, side_weight, real, partner, imag, ahead, behind):
+def side_terms(sections, side_weight, real, partner, imag, ahead, behind, after):
     blocks, dimension = real.shape[0], real.shape[-1]
     flat = (dimension, dimension)
 
-    def body(weight, real, partner, imag, ahead, behind, for_partner, own, middle, shared):
+    def body(weight, real, partner, imag, ahead, behind, _, for_partner, own, middle, shared):
         outer = is_at(0, sections)
         chosen = first_is_far()
         for index in range(blocks):
@@ -341,9 +363,8 @@
     return call(
         body,
         (shape(blocks), shape(blocks), shape(3), shape(4)),
-        [side_weight, real, partner, imag, ahead, behind],
+        [side_weight, real, partner, imag, ahead, behind, after],
         1,
-        "side_terms",
     )
 
 
@@ -395,7 +416,6 @@
         (shape(blocks), shape(blocks), shape(blocks), shape(2 * blocks)),
         [tables[name] for name in names],
         1,
-        "combine",
     )
 
 
@@ -410,10 +430,10 @@
             out[0, place, 1] = own[2 * index + 1] + from_partner[index]
 
     shape = jax.ShapeDtypeStruct((1, blocks, 2, dimension, dimension), F32)
-    return call(body, shape, [own, from_first, from_second, from_partner], 1, "finish")
-
-
-def local(
+    return call(body, shape, [own, from_first, from_second, from_partner], 1)
+
+
+def step(
     onsite, hopping, coupling, broadening, born_sigma, phonon_shift, phonon_local, phonon_side
 ):
     blocks = onsite.shape[0]
@@ -439,68 +459,57 @@
     pairs = [(e, ((e + 2) ^ 2) - 2) for e in range(spread)]
     second_swap = [(a, b) for a, b in pairs if 0 <= b < spread]
 
-    pack, edge, plain = prepare(
-        sections, spread, broadening, onsite, hopping, coupling, born_sigma
-    )
-    before = over_section(plain, [(s, s + 1) for s in range(half - 1, sections - 1)])
+    pack = prepare(sections, spread, broadening, onsite, hopping, coupling, born_sigma)
 
     def inner_link(table, index, reverse=False):
         place = 2 * blocks + 2 * index
         return [(table, place + 1, place) if reverse else (table, place, place + 1)]
 
-    end_link = [(edge, 0, 1), (before, True)]
-    end_back = [(edge, 1, 0), (before, False)]
+    end = 4 * blocks - 2
 
     first = []
     sigma = None
     for step in range(half):
         entering = []
+        if step > 0:
+            sigma = enter_step(sections, step, 1, pack, sigma)
         for index in range(blocks):
             entering.append(sigma)
             given = [] if sigma is None else [sigma]
-            link = inner_link(pack, index) if index < last else end_link
-            sigma = chain_step(sections, step, pack, index, given, link, f"inward{step}{index}")
+            leaves = index == last
+            link = [(pack, end, end + 1)] if leaves else inner_link(pack, index)
+            sigma = chain_step(sections, step, pack, index, given, link, leaves=leaves)
         first.append(entering)
         leaving = sigma
         sigma = over_section(sigma, inwards if step < half - 1 else across)
 
-    local_weight, side_weight = weights(phonon_shift, phonon_local, phonon_side, leaving)
-    pack_in = over_section(pack, outwards)
-    arriving = sigma
+    all_weights = weights(phonon_shift, phonon_local, phonon_side, leaving)
+    local_weight, side_weight = all_weights
+    pack_in = over_section(lax.optimization_barrier((pack, leaving))[0], outwards)
+    arriving = enter_step(sections, half - 1, 0, pack, sigma)
     earlier = tuple(first[step][last] for step in range(half))
     sigma = over_section(arriving, outwards)
-    ready = green_step(
-        sections, half - 1, pack, last, earlier[1:], (arriving,), f"green{last}inner"
-    )
+    ready = green_step(sections, half - 1, pack, last, earlier[1:], (arriving,), after=all_weights)
     for index in range(last, -1, -1):
-        link = inner_link(pack_in, index - 1, True) if index > 0 else end_back
+        link = (
+            inner_link(pack_in, index - 1, True)
+            if index > 0
+            else [(pack, end + 1, end), (pack_in, end, end + 1)]
+        )
         after = ready if index == last else ()
-        sigma = chain_step(
-            sections, 0, pack_in, index, [sigma], link, f"relay{index}", after=after
-        )
-    green = green_step(
-        sections, 0, pack, last, earlier[:1], (sigma,), f"green{last}outer", passed=ready
-    )
+        sigma = chain_step(sections, 0, pack_in, index, [sigma], link, after=after)
+    green = green_step(sections, 0, pack, last, earlier[:1], (sigma,), passed=ready)
     second = (sigma, arriving)
     joined = []
     for index in range(last, 0, -1):
         joined.insert(0, green)
         link = inner_link(pack, index - 1, True)
         second = (
-            chain_step(
-                sections, None, pack, index, second, link, f"outward{index}", after=green
-            ),
+            chain_step(sections, None, pack, index, second, link, after=green),
         )
         earlier = tuple(first[step][index - 1] for step in range(half))
         green = green_step(
-            sections,
-            None,
-            pack,
-            index - 1,
-            earlier,
-            second,
-            f"green{index - 1}",
-            joined=joined if index == 1 else (),
+            sections, None, pack, index - 1, earlier, second, joined=joined if index == 1 else ()
         )
     real, imag = green
     partner = over_energy(real, swap)
@@ -509,7 +518,7 @@
     middle_real = over_section(joined[-1][0], across)
 
     side_partner, side_own, middle, shared = side_terms(
-        sections, side_weight, real, partner, imag, ahead, behind
+        sections, side_weight, real, partner, imag, ahead, behind, middle_real
     )
     middle = over_section(middle, across)
     shared = over_section(shared, inwards + outwards)
@@ -551,4 +560,4 @@
         P(),
     )
     out_specs = P("energy", "section", None, None, None)
-    return jax.shard_map(local, mesh=mesh, in_specs=in_specs, out_specs=out_specs, check_vma=False)
+    return jax.shard_map(step, mesh=mesh, in_specs=in_specs, out_specs=out_specs, check_vma=False)

time: 91.4 us -> 87.3 us (0.955)
  starting transfers between devices: 36.1 us -> 28.3 us
  waiting for transfers between devices: 33.9 us -> 36.6 us
  Pallas kernels: 15.9 us -> 17.1 us
    ppermute x8 -> x7, starting transfers between devices: 27.4 us -> 18.9 us  [over_section(): return lax.ppermute(value, 'section', route)]
    ppermute x8 -> x7, waiting for transfers between devices: 20.6 us -> 28.8 us  [over_section(): return lax.ppermute(value, 'section', route)]
    ppermute x6, waiting for transfers between devices: 13.3 us -> 7.81 us  [over_energy(): return lax.ppermute(value, 'energy', route)]
    pallas_call x13 -> x15, Pallas kernels: 13.7 us -> 14.8 us  [call(): pl.pallas_call(body, out_shape=out_shape, in_specs=[VMEM] * len(operands)...]
  transfers between devices with their start and end apart: 14 -> 13, of which waited for: 7 -> 6; matrix products, arithmetic and copies ran while one was open for 0% -> 0% of each run, Pallas kernels for 9% -> 5%
where the time goes in v1:
time: 87.3 us; the launch traced here: 86.9 us
  waiting for transfers between devices  36.6 us (42%)
  starting transfers between devices  28.3 us (32%)
  Pallas kernels  17.1 us (20%)
  local copies, waits for them, and re-layouts  4 us (5%)
  between operations  0.92 us (1%)
    ppermute x7, waiting for transfers between devices, over_section(): return lax.ppermute(value, 'section', route)  28.8 us
    ppermute x7, starting transfers between devices, over_section(): return lax.ppermute(value, 'section', route)  18.9 us
    pallas_call x15, Pallas kernels, call(): pl.pallas_call(body, out_shape=out_shape, in_specs=[VMEM] * len(operands)...  14.8 us
    ppermute x6, starting transfers between devices, over_energy(): return lax.ppermute(value, 'energy', route)  9.4 us
    ppermute x6, waiting for transfers between devices, over_energy(): return lax.ppermute(value, 'energy', route)  7.81 us
    unnamed x14, local copies, waits for them, and re-layouts  4 us
  transfers between devices with their start and end apart: 13, of which 6 were waited for; matrix products, arithmetic and copies ran while one was open for 0% of the time, Pallas kernels for 5%

profile of v1, /device:TPU:1, one launch (start us, length us, event | category | flops | bytes accessed | tf_op | source)
XLA Modules:
  0.0 86.9 jit_solution(13953407637153818525)
XLA Ops:
  0.7 1.2 %copy-done.2 = f32[1,2,2,256,256]{4,3,2,1,0:T(8,128)S(1)} copy-done((f32[1,2,2,256,256]{4,3,2,1,0:T(8,128)S(1)}, f32[1,2,2,256,256]{4,3,2,1,0:T(8,128)}, u32[]{:S(2)}) %copy-start.2) | copy-done | bytes 1048600
  1.9 1.0 %copy-done.3 = f32[2,256,256]{2,1,0:T(8,128)S(1)} copy-done((f32[2,256,256]{2,1,0:T(8,128)S(1)}, f32[2,256,256]{2,1,0:T(8,128)}, u32[]{:S(2)}) %copy-start.3) | copy-done | bytes 524312
  2.9 1.0 %copy-done.4 = f32[2,256,256]{2,1,0:T(8,128)S(1)} copy-done((f32[2,256,256]{2,1,0:T(8,128)S(1)}, f32[2,256,256]{2,1,0:T(8,128)}, u32[]{:S(2)}) %copy-start.4) | copy-done | bytes 524312
  4.0 0.7 copy-done.5
  4.6 0.9 %prepare.1.refs_0_.refs_1_.refs_2_.source.refs_3_ = f32[8,256,256]{2,1,0:T(8,128)S(1)} custom-call(f32[1,1]{1,0:T(1,128)} %bitcast.1.broadening, f32[2,256]{1,0:T(2,128)S(1)} %copy-done.5, f32[2,256,256]{2,1,0:T(8,128)S(1)} %copy-done.3, f32[2,256,256]{2,1,0:T(8,128)S(1)} %copy-done.4, f32[1,2,2,256,256]{4,3,2,1,0:T(8,128)S(1)} %copy-done.2), custom_call_target="tpu_custom_call" | custom-call | tf_op jit(solution)/shard_map/prepare/pallas_call | solution.py:287
  5.7 1.3 %collective-permute-start = (f32[2,256,256]{2,1,0:T(8,128)S(1)}, f32[2,256,256]{2,1,0:T(8,128)S(1)}, u32[]{:S(2)}, u32[]{:S(2)}) collective-permute-start(f32[2,256,256]{2,1,0:T(8,128)S(1)} %shard_map.83), channel_id=1, source_target_pairs={{0,1},{3,2},{4,5},{7,6},{8,9},{11,10},{12,13},{15,14},{16,17},{19,... | collective-permute-start | bytes 1572872 | tf_op jit(solution)/shard_map/ppermute | solution.py:451
  7.0 5.9 %collective-permute-done.value = f32[2,256,256]{2,1,0:T(8,128)S(1)} collective-permute-done((f32[2,256,256]{2,1,0:T(8,128)S(1)}, f32[2,256,256]{2,1,0:T(8,128)S(1)}, u32[]{:S(2)}, u32[]{:S(2)}) %collective-permute-start) | collective-permute-done | bytes 524320 | tf_op jit(solution)/shard_map/ppermute | solution.py:451
  12.8 2.3 %shard_map.85.refs_1_ = f32[2,256,256]{2,1,0:T(8,128)S(1)} custom-call(f32[8,256,256]{2,1,0:T(8,128)S(1)} %prepare.1.refs_0_.refs_1_.refs_2_.source.refs_3_, f32[2,256,256]{2,1,0:T(8,128)S(1)} %shard_map.84.refs_1_, f32[8,256,256]{2,1,0:T(8,128)S(1)} %prepare.1.refs_0_.refs_1_.refs_2_.source.refs_3_), custom_call_target="tpu_custom_call" | custom-call | flops 1610612736 | bytes 2097152 | tf_op jit(solution)/shard_map/pallas_call | solution.py:105
  15.1 2.5 %shard_map.86._ = f32[2,256,256]{2,1,0:T(8,128)S(1)} custom-call(f32[8,256,256]{2,1,0:T(8,128)S(1)} %prepare.1.refs_0_.refs_1_.refs_2_.source.refs_3_, f32[2,256,256]{2,1,0:T(8,128)S(1)} %shard_map.85.refs_1_, f32[8,256,256]{2,1,0:T(8,128)S(1)} %prepare.1.refs_0_.refs_1_.refs_2_.source.refs_3_), custom_call_target="tpu_custom_call" | custom-call | flops 1610612736 | bytes 2097152 | tf_op jit(solution)/shard_map/pallas_call | solution.py:105
  17.7 1.6 %collective-permute-start.1 = (f32[8,256,256]{2,1,0:T(8,128)S(1)}, f32[8,256,256]{2,1,0:T(8,128)S(1)}, u32[]{:S(2)}, u32[]{:S(2)}) collective-permute-start(f32[8,256,256]{2,1,0:T(8,128)S(1)} %prepare.1.refs_0_.refs_1_.refs_2_.source.refs_3_), channel_id=1, source_target_pairs={{1,0},{2,3},{5,4},{6,7},{9,8},{10,11},{13,12},{14,15},{17,16},{18,... | collective-permute-start | bytes 6291464 | tf_op jit(solution)/shard_map/ppermute | solution.py:451
  19.2 4.3 %collective-permute-start.2 = (f32[2,256,256]{2,1,0:T(8,128)S(1)}, f32[2,256,256]{2,1,0:T(8,128)S(1)}, u32[]{:S(2)}, u32[]{:S(2)}) collective-permute-start(f32[2,256,256]{2,1,0:T(8,128)S(1)} %shard_map.86._), channel_id=1, source_target_pairs={{1,2},{2,1},{5,6},{6,5},{9,10},{10,9},{13,14},{14,13},{17,18},{18,... | collective-permute-start | bytes 1572872 | tf_op jit(solution)/shard_map/ppermute | solution.py:451
  23.6 6.8 %collective-permute-done.2.value = f32[2,256,256]{2,1,0:T(8,128)S(1)} collective-permute-done((f32[2,256,256]{2,1,0:T(8,128)S(1)}, f32[2,256,256]{2,1,0:T(8,128)S(1)}, u32[]{:S(2)}, u32[]{:S(2)}) %collective-permute-start.2) | collective-permute-done | bytes 524320 | tf_op jit(solution)/shard_map/ppermute | solution.py:451
  30.4 0.8 shard_map.87.refs_2_
  31.2 1.3 %collective-permute-start.3 = (f32[2,256,256]{2,1,0:T(8,128)S(1)}, f32[2,256,256]{2,1,0:T(8,128)S(1)}, u32[]{:S(2)}, u32[]{:S(2)}) collective-permute-start(f32[2,256,256]{2,1,0:T(8,128)S(1)} %shard_map.87.refs_2_), channel_id=1, source_target_pairs={{1,0},{2,3},{5,4},{6,7},{9,8},{10,11},{13,12},{14,15},{17,16},{18,... | collective-permute-start | bytes 1572872 | tf_op jit(solution)/shard_map/ppermute | solution.py:451
  32.6 1.4 %weights.1 = (f32[5,256,256]{2,1,0:T(8,128)S(1)}, f32[5,256,256]{2,1,0:T(8,128)S(1)}) custom-call(s32[4]{0:T(128)S(1)} %copy-done.6, f32[4,256,256]{2,1,0:T(8,128)S(1)} %copy-done, f32[4,256,256]{2,1,0:T(8,128)S(1)} %copy-done.1, f32[2,256,256]{2,1,0:T(8,128)S(1)} %shard_map.86._), custom_call_target="tpu_custom_call" | custom-call | flops 1048576 | bytes 8388608 | tf_op jit(solution)/shard_map/weights/pallas_call | solution.py:329
  34.0 1.9 %shard_map.88 = (f32[256,256]{1,0:T(8,128)S(1)}, f32[256,256]{1,0:T(8,128)S(1)}) custom-call(f32[8,256,256]{2,1,0:T(8,128)S(1)} %prepare.1.refs_0_.refs_1_.refs_2_.source.refs_3_, f32[2,256,256]{2,1,0:T(8,128)S(1)} %shard_map.85.refs_1_, f32[2,256,256]{2,1,0:T(8,128)S(1)} %shard_map.87.refs_2_, f32[5,256,256]{2,1,0:T(8,128)S(1)} %get-tuple-element.22.refs_3_.refs_0_, ...), custom_call_target="tpu_custom_call" | custom-call | flops 1207959552 | bytes 2097152 | tf_op jit(solution)/shard_map/pallas_call | solution.py:105
  36.3 2.3 %shard_map.92.refs_2_ = f32[2,256,256]{2,1,0:T(8,128)S(1)} custom-call(f32[8,256,256]{2,1,0:T(8,128)S(1)} %prepare.1.refs_0_.refs_1_.refs_2_.source.refs_3_, f32[2,256,256]{2,1,0:T(8,128)S(1)} %shard_map.90.refs_2_.refs_1_, f32[2,256,256]{2,1,0:T(8,128)S(1)} %shard_map.87.refs_2_, f32[8,256,256]{2,1,0:T(8,128)S(1)} %prepare.1.refs_0_.refs_1_.refs_2_.source.refs_3_, ...), custom_call_target="tpu_custom_call" | custom-call | flops 1610612736 | bytes 2097152 | tf_op jit(solution)/shard_map/pallas_call | solution.py:105
  38.6 1.9 %shard_map.93 = (f32[2,256,256]{2,1,0:T(8,128)S(1)}, f32[2,256,256]{2,1,0:T(8,128)S(1)}) custom-call(f32[8,256,256]{2,1,0:T(8,128)S(1)} %prepare.1.refs_0_.refs_1_.refs_2_.source.refs_3_, f32[2,256,256]{2,1,0:T(8,128)S(1)} %shard_map.84.refs_1_, f32[2,256,256]{2,1,0:T(8,128)S(1)} %shard_map.92.refs_2_, f32[256,256]{1,0:T(8,128)S(1)} %get-tuple-element.27.refs_4_.refs_3_, ...), custom_call_target="tpu_custom_call" | custom-call | flops 1207959552 | bytes 2097152 | tf_op jit(solution)/shard_map/pallas_call | solution.py:105
  40.4 2.1 %collective-permute-start.4 = (f32[2,256,256]{2,1,0:T(8,128)S(1)}, f32[2,256,256]{2,1,0:T(8,128)S(1)}, u32[]{:S(2)}, u32[]{:S(2)}) collective-permute-start(f32[2,256,256]{2,1,0:T(8,128)S(1)} %get-tuple-element.29.real.refs_2_), channel_id=1, source_target_pairs={{0,4},{4,0},{8,12},{12,8},{16,20},{20,16},{24,28},{28,24},{1,5},{5... | collective-permute-start | bytes 1572872 | tf_op jit(solution)/shard_map/ppermute | solution.py:454
  42.5 0.7 collective-permute-start.6
  43.2 3.9 %collective-permute-start.5 = (f32[2,256,256]{2,1,0:T(8,128)S(1)}, f32[2,256,256]{2,1,0:T(8,128)S(1)}, u32[]{:S(2)}, u32[]{:S(2)}) collective-permute-start(f32[2,256,256]{2,1,0:T(8,128)S(1)} %get-tuple-element.30.imag.refs_4_), channel_id=1, source_target_pairs={{0,8},{4,12},{8,0},{12,4},{16,24},{20,28},{24,16},{28,20},{1,9},{5... | collective-permute-start | bytes 1572872 | tf_op jit(solution)/shard_map/ppermute | solution.py:454
  47.1 2.9 %collective-permute-start.7 = (f32[256,256]{1,0:T(8,128)S(1)}, f32[256,256]{1,0:T(8,128)S(1)}, u32[]{:S(2)}, u32[]{:S(2)}) collective-permute-start(f32[256,256]{1,0:T(8,128)S(1)} %get-tuple-element.27.refs_4_.refs_3_), channel_id=1, source_target_pairs={{1,2},{2,1},{5,6},{6,5},{9,10},{10,9},{13,14},{14,13},{17,18},{18,... | collective-permute-start | bytes 786440 | tf_op jit(solution)/shard_map/ppermute | solution.py:451
  50.0 5.1 %collective-permute-done.7._.refs_9_ = f32[256,256]{1,0:T(8,128)S(1)} collective-permute-done((f32[256,256]{1,0:T(8,128)S(1)}, f32[256,256]{1,0:T(8,128)S(1)}, u32[]{:S(2)}, u32[]{:S(2)}) %collective-permute-start.7) | collective-permute-done | bytes 262176 | tf_op jit(solution)/shard_map/ppermute | solution.py:451
  55.7 4.9 %collective-permute-start.9 = (f32[4,256,256]{2,1,0:T(8,128)S(1)}, f32[4,256,256]{2,1,0:T(8,128)S(1)}, u32[]{:S(2)}, u32[]{:S(2)}) collective-permute-start(f32[4,256,256]{2,1,0:T(8,128)S(1)} %get-tuple-element.34), channel_id=1, source_target_pairs={{0,1},{3,2},{1,0},{2,3},{4,5},{7,6},{5,4},{6,7},{8,9},{11,10},{9,8... | collective-permute-start | bytes 3145736 | tf_op jit(solution)/shard_map/ppermute | solution.py:451
  60.7 2.6 %collective-permute-start.8 = (f32[3,256,256]{2,1,0:T(8,128)S(1)}, f32[3,256,256]{2,1,0:T(8,128)S(1)}, u32[]{:S(2)}, u32[]{:S(2)}) collective-permute-start(f32[3,256,256]{2,1,0:T(8,128)S(1)} %get-tuple-element.33), channel_id=1, source_target_pairs={{1,2},{2,1},{5,6},{6,5},{9,10},{10,9},{13,14},{14,13},{17,18},{18,... | collective-permute-start | bytes 2359304 | tf_op jit(solution)/shard_map/ppermute | solution.py:451
  63.3 11.0 %collective-permute-done.8.refs_10_ = f32[3,256,256]{2,1,0:T(8,128)S(1)} collective-permute-done((f32[3,256,256]{2,1,0:T(8,128)S(1)}, f32[3,256,256]{2,1,0:T(8,128)S(1)}, u32[]{:S(2)}, u32[]{:S(2)}) %collective-permute-start.8) | collective-permute-done | bytes 786464 | tf_op jit(solution)/shard_map/ppermute | solution.py:451
  74.3 1.0 %shard_map.95 = (f32[2,256,256]{2,1,0:T(8,128)S(1)}, f32[2,256,256]{2,1,0:T(8,128)S(1)}, f32[2,256,256]{2,1,0:T(8,128)S(1)}, f32[4,256,256]{2,1,0:T(8,128)S(1)}) custom-call(f32[5,256,256]{2,1,0:T(8,128)S(1)} %get-tuple-element.22.refs_3_.refs_0_, f32[5,256,256]{2,1,0:T(8,128)S(1)} %get-tuple-element.23.refs_4_.weight.refs_1_, ...), custom_call_target="tpu_custom_call" | custom-call | flops 100663296 | bytes 2097152 | tf_op jit(solution)/shard_map/pallas_call | solution.py:105
  75.3 1.8 %collective-permute-start.10 = (f32[2,256,256]{2,1,0:T(8,128)S(1)}, f32[2,256,256]{2,1,0:T(8,128)S(1)}, u32[]{:S(2)}, u32[]{:S(2)}) collective-permute-start(f32[2,256,256]{2,1,0:T(8,128)S(1)} %get-tuple-element.36), channel_id=1, source_target_pairs={{0,8},{4,12},{8,0},{12,4},{16,24},{20,28},{24,16},{28,20},{1,9},{5... | collective-permute-start | bytes 1572872 | tf_op jit(solution)/shard_map/ppermute | solution.py:454
  77.0 0.7 collective-permute-start.11
  78.0 5.6 %collective-permute-done.10.from_first = f32[2,256,256]{2,1,0:T(8,128)S(1)} collective-permute-done((f32[2,256,256]{2,1,0:T(8,128)S(1)}, f32[2,256,256]{2,1,0:T(8,128)S(1)}, u32[]{:S(2)}, u32[]{:S(2)}) %collective-permute-start.10) | collective-permute-done | bytes 524320 | tf_op jit(solution)/shard_map/ppermute | solution.py:454
  83.6 2.2 %collective-permute-done.12.from_partner = f32[2,256,256]{2,1,0:T(8,128)S(1)} collective-permute-done((f32[2,256,256]{2,1,0:T(8,128)S(1)}, f32[2,256,256]{2,1,0:T(8,128)S(1)}, u32[]{:S(2)}, u32[]{:S(2)}) %collective-permute-start.12) | collective-permute-done | bytes 524320 | tf_op jit(solution)/shard_map/ppermute | solution.py:454
  85.8 1.1 %shard_map.96 = f32[1,2,2,256,256]{4,3,2,1,0:T(8,128)} custom-call(f32[4,256,256]{2,1,0:T(8,128)S(1)} %get-tuple-element.35.own, f32[2,256,256]{2,1,0:T(8,128)S(1)} %collective-permute-done.10.from_first, f32[2,256,256]{2,1,0:T(8,128)S(1)} %collective-permute-done.11.from_second, f32[2,256,256]{2,1,0:T(8,128)S(1)} %collective-permute-done.12.from_partner), custom_call_target="tpu_custom_call" | custom-call | flops 100663296 | bytes 2097152 | tf_op jit(solution)/shard_map/pallas_call | solution.py:105
  (25 shorter events, 1.5 us)
Async XLA Ops:
  0.7 1.2 %copy-start.2 = (f32[1,2,2,256,256]{4,3,2,1,0:T(8,128)S(1)}, f32[1,2,2,256,256]{4,3,2,1,0:T(8,128)}, u32[]{:S(2)}) copy-start(f32[1,2,2,256,256]{4,3,2,1,0:T(8,128)} %born.1) | copy-start | bytes 3145732
  1.9 1.0 %copy-start.3 = (f32[2,256,256]{2,1,0:T(8,128)S(1)}, f32[2,256,256]{2,1,0:T(8,128)}, u32[]{:S(2)}) copy-start(f32[2,256,256]{2,1,0:T(8,128)} %hopping.1) | copy-start | bytes 1572868
  2.9 1.0 %copy-start.4 = (f32[2,256,256]{2,1,0:T(8,128)S(1)}, f32[2,256,256]{2,1,0:T(8,128)}, u32[]{:S(2)}) copy-start(f32[2,256,256]{2,1,0:T(8,128)} %coupling.1) | copy-start | bytes 1572868
  4.0 0.7 copy-start.5
  5.7 7.2 %collective-permute-start = (f32[2,256,256]{2,1,0:T(8,128)S(1)}, f32[2,256,256]{2,1,0:T(8,128)S(1)}, u32[]{:S(2)}, u32[]{:S(2)}) collective-permute-start(f32[2,256,256]{2,1,0:T(8,128)S(1)} %shard_map.83), channel_id=1, source_target_pairs={{0,1},{3,2},{4,5},{7,6},{8,9},{11,10},{12,13},{15,14},{16,17},{19,... | collective-permute-start | bytes 1572872 | tf_op jit(solution)/shard_map/ppermute | solution.py:451
  17.6 14.9 %copy-start = (f32[4,256,256]{2,1,0:T(8,128)S(1)}, f32[4,256,256]{2,1,0:T(8,128)}, u32[]{:S(2)}) copy-start(f32[4,256,256]{2,1,0:T(8,128)} %local_ref.1) | copy-start | bytes 3145732
  17.6 14.9 %copy-start.1 = (f32[4,256,256]{2,1,0:T(8,128)S(1)}, f32[4,256,256]{2,1,0:T(8,128)}, u32[]{:S(2)}) copy-start(f32[4,256,256]{2,1,0:T(8,128)} %side_ref.1) | copy-start | bytes 3145732
  17.6 14.9 %copy-start.6 = (s32[4]{0:T(128)S(1)}, s32[4]{0:T(128)}, u32[]{:S(2)}) copy-start(s32[4]{0:T(128)} %shift_ref.1) | copy-start | bytes 52
  17.7 18.2 %collective-permute-start.1 = (f32[8,256,256]{2,1,0:T(8,128)S(1)}, f32[8,256,256]{2,1,0:T(8,128)S(1)}, u32[]{:S(2)}, u32[]{:S(2)}) collective-permute-start(f32[8,256,256]{2,1,0:T(8,128)S(1)} %prepare.1.refs_0_.refs_1_.refs_2_.source.refs_3_), channel_id=1, source_target_pairs={{1,0},{2,3},{5,4},{6,7},{9,8},{10,11},{13,12},{14,15},{17,16},{18,... | collective-permute-start | bytes 6291464 | tf_op jit(solution)/shard_map/ppermute | solution.py:451
  19.2 11.2 %collective-permute-start.2 = (f32[2,256,256]{2,1,0:T(8,128)S(1)}, f32[2,256,256]{2,1,0:T(8,128)S(1)}, u32[]{:S(2)}, u32[]{:S(2)}) collective-permute-start(f32[2,256,256]{2,1,0:T(8,128)S(1)} %shard_map.86._), channel_id=1, source_target_pairs={{1,2},{2,1},{5,6},{6,5},{9,10},{10,9},{13,14},{14,13},{17,18},{18,... | collective-permute-start | bytes 1572872 | tf_op jit(solution)/shard_map/ppermute | solution.py:451
  31.2 4.7 %collective-permute-start.3 = (f32[2,256,256]{2,1,0:T(8,128)S(1)}, f32[2,256,256]{2,1,0:T(8,128)S(1)}, u32[]{:S(2)}, u32[]{:S(2)}) collective-permute-start(f32[2,256,256]{2,1,0:T(8,128)S(1)} %shard_map.87.refs_2_), channel_id=1, source_target_pairs={{1,0},{2,3},{5,4},{6,7},{9,8},{10,11},{13,12},{14,15},{17,16},{18,... | collective-permute-start | bytes 1572872 | tf_op jit(solution)/shard_map/ppermute | solution.py:451
  40.4 14.6 %collective-permute-start.4 = (f32[2,256,256]{2,1,0:T(8,128)S(1)}, f32[2,256,256]{2,1,0:T(8,128)S(1)}, u32[]{:S(2)}, u32[]{:S(2)}) collective-permute-start(f32[2,256,256]{2,1,0:T(8,128)S(1)} %get-tuple-element.29.real.refs_2_), channel_id=1, source_target_pairs={{0,4},{4,0},{8,12},{12,8},{16,20},{20,16},{24,28},{28,24},{1,5},{5... | collective-permute-start | bytes 1572872 | tf_op jit(solution)/shard_map/ppermute | solution.py:454
  42.5 12.5 %collective-permute-start.6 = (f32[2,256,256]{2,1,0:T(8,128)S(1)}, f32[2,256,256]{2,1,0:T(8,128)S(1)}, u32[]{:S(2)}, u32[]{:S(2)}) collective-permute-start(f32[2,256,256]{2,1,0:T(8,128)S(1)} %get-tuple-element.30.imag.refs_4_), channel_id=1, source_target_pairs={{8,16},{12,20},{16,8},{20,12},{9,17},{13,21},{17,9},{21,13},{10,18... | collective-permute-start | bytes 1572872 | tf_op jit(solution)/shard_map/ppermute | solution.py:454
  43.2 11.9 %collective-permute-start.5 = (f32[2,256,256]{2,1,0:T(8,128)S(1)}, f32[2,256,256]{2,1,0:T(8,128)S(1)}, u32[]{:S(2)}, u32[]{:S(2)}) collective-permute-start(f32[2,256,256]{2,1,0:T(8,128)S(1)} %get-tuple-element.30.imag.refs_4_), channel_id=1, source_target_pairs={{0,8},{4,12},{8,0},{12,4},{16,24},{20,28},{24,16},{28,20},{1,9},{5... | collective-permute-start | bytes 1572872 | tf_op jit(solution)/shard_map/ppermute | solution.py:454
  47.1 8.0 %collective-permute-start.7 = (f32[256,256]{1,0:T(8,128)S(1)}, f32[256,256]{1,0:T(8,128)S(1)}, u32[]{:S(2)}, u32[]{:S(2)}) collective-permute-start(f32[256,256]{1,0:T(8,128)S(1)} %get-tuple-element.27.refs_4_.refs_3_), channel_id=1, source_target_pairs={{1,2},{2,1},{5,6},{6,5},{9,10},{10,9},{13,14},{14,13},{17,18},{18,... | collective-permute-start | bytes 786440 | tf_op jit(solution)/shard_map/ppermute | solution.py:451
  55.7 18.5 %collective-permute-start.9 = (f32[4,256,256]{2,1,0:T(8,128)S(1)}, f32[4,256,256]{2,1,0:T(8,128)S(1)}, u32[]{:S(2)}, u32[]{:S(2)}) collective-permute-start(f32[4,256,256]{2,1,0:T(8,128)S(1)} %get-tuple-element.34), channel_id=1, source_target_pairs={{0,1},{3,2},{1,0},{2,3},{4,5},{7,6},{5,4},{6,7},{8,9},{11,10},{9,8... | collective-permute-start | bytes 3145736 | tf_op jit(solution)/shard_map/ppermute | solution.py:451
  60.7 13.6 %collective-permute-start.8 = (f32[3,256,256]{2,1,0:T(8,128)S(1)}, f32[3,256,256]{2,1,0:T(8,128)S(1)}, u32[]{:S(2)}, u32[]{:S(2)}) collective-permute-start(f32[3,256,256]{2,1,0:T(8,128)S(1)} %get-tuple-element.33), channel_id=1, source_target_pairs={{1,2},{2,1},{5,6},{6,5},{9,10},{10,9},{13,14},{14,13},{17,18},{18,... | collective-permute-start | bytes 2359304 | tf_op jit(solution)/shard_map/ppermute | solution.py:451
  75.3 8.3 %collective-permute-start.10 = (f32[2,256,256]{2,1,0:T(8,128)S(1)}, f32[2,256,256]{2,1,0:T(8,128)S(1)}, u32[]{:S(2)}, u32[]{:S(2)}) collective-permute-start(f32[2,256,256]{2,1,0:T(8,128)S(1)} %get-tuple-element.36), channel_id=1, source_target_pairs={{0,8},{4,12},{8,0},{12,4},{16,24},{20,28},{24,16},{28,20},{1,9},{5... | collective-permute-start | bytes 1572872 | tf_op jit(solution)/shard_map/ppermute | solution.py:454
  77.0 6.6 %collective-permute-start.11 = (f32[2,256,256]{2,1,0:T(8,128)S(1)}, f32[2,256,256]{2,1,0:T(8,128)S(1)}, u32[]{:S(2)}, u32[]{:S(2)}) collective-permute-start(f32[2,256,256]{2,1,0:T(8,128)S(1)} %get-tuple-element.37), channel_id=1, source_target_pairs={{8,16},{12,20},{16,8},{20,12},{9,17},{13,21},{17,9},{21,13},{10,18... | collective-permute-start | bytes 1572872 | tf_op jit(solution)/shard_map/ppermute | solution.py:454
  77.7 8.1 %collective-permute-start.12 = (f32[2,256,256]{2,1,0:T(8,128)S(1)}, f32[2,256,256]{2,1,0:T(8,128)S(1)}, u32[]{:S(2)}, u32[]{:S(2)}) collective-permute-start(f32[2,256,256]{2,1,0:T(8,128)S(1)} %get-tuple-element.38), channel_id=1, source_target_pairs={{0,4},{4,0},{8,12},{12,8},{16,20},{20,16},{24,28},{28,24},{1,5},{5... | collective-permute-start | bytes 1572872 | tf_op jit(solution)/shard_map/ppermute | solution.py:454

commit v2 on v1

--- a/solution.py
+++ b/solution.py
@@ -239,7 +239,7 @@
 
 
 def prepare_kernel(
-    sections, spread, broadening, onsite, hopping, coupling, born, pack, hop, cup, sig, sems
+    sections, spread, broadening, onsite, hopping, coupling, born, pack, hop, cup, sig, levels, sems
 ):
     blocks, dimension = onsite.shape
     copies = []
@@ -254,22 +254,25 @@
             copy = pltpu.make_async_copy(source, target, sems.at[3 * index + order])
             copy.start()
             copies.append(copy)
+    copies.append(pltpu.make_async_copy(onsite, levels, sems.at[3 * blocks]))
+    copies[-1].start()
     right_half = half_of(sections)
     flip = right_half.astype(jnp.int32)
     shape = (dimension, dimension)
     eye = lax.broadcasted_iota(jnp.int32, shape, 0) == lax.broadcasted_iota(jnp.int32, shape, 1)
     position = lax.axis_index("energy").astype(F32)
     energy = -2.0 + position * (4.0 / (spread - 1))
-    broad = broadening[...]
+    copies[3 * blocks].wait()
+    width = jnp.broadcast_to(broadening[...], shape)
     for index in range(blocks):
         place = jnp.where(right_half, blocks - 1 - index, index)
         copies[3 * index].wait()
         block = hop[index]
-        level = energy - onsite[pl.ds(index, 1), :]
+        level = energy - levels[pl.ds(index, 1), :]
         real = jnp.where(eye, jnp.broadcast_to(level, shape), 0.0) - 0.5 * (block + block.T)
         copies[3 * index + 1].wait()
         pack[2 * place] = real - sig[index, 0]
-        pack[2 * place + 1] = jnp.where(eye, jnp.broadcast_to(broad, shape), 0.0) - sig[index, 1]
+        pack[2 * place + 1] = jnp.where(eye, width, 0.0) - sig[index, 1]
         copies[3 * index + 2].wait()
         link = cup[index]
         if index < blocks - 1:
@@ -287,17 +290,24 @@
     return pl.pallas_call(
         functools.partial(prepare_kernel, sections, spread),
         out_shape=jax.ShapeDtypeStruct((4 * blocks, dimension, dimension), F32),
-        in_specs=[VMEM, VMEM, outside, outside, outside],
+        in_specs=[VMEM] + [outside] * 4,
         out_specs=VMEM,
         scratch_shapes=[
             pltpu.VMEM((blocks, dimension, dimension), F32),
             pltpu.VMEM((blocks, dimension, dimension), F32),
             pltpu.VMEM((blocks, 2, dimension, dimension), F32),
-            pltpu.SemaphoreType.DMA((3 * blocks,)),
+            pltpu.VMEM((blocks, dimension), F32),
+            pltpu.SemaphoreType.DMA((3 * blocks + 1,)),
         ],
         compiler_params=pltpu.CompilerParams(vmem_limit_bytes=16 << 20),
         name="prepare",
-    )(broadening.reshape(1, 1), onsite, hopping, coupling, born)
+    )(
+        broadening.reshape(1, 1),
+        *(
+            pltpu.with_memory_space_constraint(value, pltpu.HBM)
+            for value in (onsite, hopping, coupling, born)
+        )
+    )
 
 
 OWN, NEXT, OTHER, PAIR, LONE = range(5)
@@ -337,11 +347,22 @@
     )(shifts, local_weight, side_weight, after)
 
 
-def side_terms(sections, side_weight, real, partner, imag, ahead, behind, after):
+def last_blocks(*tables):
+    last = tables[0].shape[0] - 1
+
+    def body(*refs):
+        for place, ref in enumerate(refs[:-1]):
+            refs[-1][place] = ref[last]
+
+    shape = jax.ShapeDtypeStruct((len(tables),) + tables[0].shape[1:], F32)
+    return call(body, shape, list(tables), 1)
+
+
+def side_terms(sections, side_weight, real, partner, imag, ahead, behind):
     blocks, dimension = real.shape[0], real.shape[-1]
     flat = (dimension, dimension)
 
-    def body(weight, real, partner, imag, ahead, behind, _, for_partner, own, middle, shared):
+    def body(weight, real, partner, imag, ahead, behind, for_partner, own, middle, shared):
         outer = is_at(0, sections)
         chosen = first_is_far()
         for index in range(blocks):
@@ -351,9 +372,8 @@
             for_partner[index] = weight[NEXT] * value + weight[OTHER] * far
             own[index] = weight[OWN] * value + weight[LONE] * far + weight[PAIR] * near
         last = blocks - 1
-        middle[0] = partner[last]
-        middle[1] = for_partner[last]
-        middle[2] = own[last]
+        middle[0] = for_partner[last]
+        middle[1] = own[last]
         for place, table in enumerate((real, partner, for_partner, own)):
             shared[place] = jnp.where(outer, table[last], table[0])
 
@@ -362,8 +382,8 @@
 
     return call(
         body,
-        (shape(blocks), shape(blocks), shape(3), shape(4)),
-        [side_weight, real, partner, imag, ahead, behind, after],
+        (shape(blocks), shape(blocks), shape(2), shape(4)),
+        [side_weight, real, partner, imag, ahead, behind],
         1,
     )
 
@@ -390,7 +410,7 @@
                 if index < last:
                     side = side + table[index + 1]
                 else:
-                    middle = t["middle_real"][...] if place == 0 else t["middle"][place - 1]
+                    middle = t["middle_real"][place] if place < 2 else t["middle"][place - 2]
                     side = side + jnp.where(outer, t["shared"][place], middle)
                 sides.append(side)
             n_real, n_partner, n_for, n_own = sides
@@ -443,8 +463,7 @@
     assert sections % 4 == 0 and sections // 4 == 1 and blocks >= 2
     half = sections // 2
     last = blocks - 1
-    inwards = [(0, 1), (sections - 1, sections - 2)]
-    outwards = [(b, a) for a, b in inwards]
+    pairs = [(s, s ^ 1) for s in range(sections)]
     across = [(half - 1, half), (half, half - 1)]
 
     def over_section(value, route):
@@ -454,10 +473,13 @@
         return lax.ppermute(value, "energy", route)
 
     swap = [(e, e ^ 1) for e in range(spread)]
-    pairs = [(e, e ^ 2) for e in range(spread)]
-    first_swap = [(a, b) for a, b in pairs if b < spread]
-    pairs = [(e, ((e + 2) ^ 2) - 2) for e in range(spread)]
-    second_swap = [(a, b) for a, b in pairs if 0 <= b < spread]
+    first_swap = [(e, e ^ 2) for e in range(spread) if e ^ 2 < spread]
+    second_swap = [(e, ((e + 2) ^ 2) - 2) for e in range(spread)]
+    second_swap = [(a, b) for a, b in second_swap if 0 <= b < spread]
+    crossing = []
+    for a, b in swap:
+        for s, t in across + [(0, 0), (sections - 1, sections - 1)]:
+            crossing.append((a * sections + s, (b if s == t else a) * sections + t))
 
     pack = prepare(sections, spread, broadening, onsite, hopping, coupling, born_sigma)
 
@@ -481,14 +503,17 @@
             sigma = chain_step(sections, step, pack, index, given, link, leaves=leaves)
         first.append(entering)
         leaving = sigma
-        sigma = over_section(sigma, inwards if step < half - 1 else across)
+        if step < half - 1:
+            sigma = over_section(sigma, pairs)
+        else:
+            sigma = lax.ppermute(sigma, ("energy", "section"), crossing)
 
     all_weights = weights(phonon_shift, phonon_local, phonon_side, leaving)
     local_weight, side_weight = all_weights
-    pack_in = over_section(lax.optimization_barrier((pack, leaving))[0], outwards)
+    pack_in = over_section(lax.optimization_barrier((pack, leaving))[0], pairs)
     arriving = enter_step(sections, half - 1, 0, pack, sigma)
     earlier = tuple(first[step][last] for step in range(half))
-    sigma = over_section(arriving, outwards)
+    sigma = over_section(arriving, pairs)
     ready = green_step(sections, half - 1, pack, last, earlier[1:], (arriving,), after=all_weights)
     for index in range(last, -1, -1):
         link = (
@@ -515,13 +540,13 @@
     partner = over_energy(real, swap)
     ahead = over_energy(imag, first_swap)
     behind = over_energy(imag, second_swap)
-    middle_real = over_section(joined[-1][0], across)
+    middle_real = over_section(last_blocks(real, partner), across)
 
     side_partner, side_own, middle, shared = side_terms(
-        sections, side_weight, real, partner, imag, ahead, behind, middle_real
+        sections, side_weight, real, partner, imag, ahead, behind
     )
     middle = over_section(middle, across)
-    shared = over_section(shared, inwards + outwards)
+    shared = over_section(shared, pairs)
     to_first, to_second, to_partner, own = combine(
         sections,
         {

time: 87.3 us -> 81.6 us (0.935)
  local copies, waits for them, and re-layouts: 4 us -> 0.02 us
  waiting for transfers between devices: 36.6 us -> 33.9 us
  Pallas kernels: 17.1 us -> 18.2 us
    ppermute x7 -> x6, waiting for transfers between devices: 28.8 us -> 12.1 us  [over_section(): return lax.ppermute(value, 'section', route)]
    ppermute x0 -> x1, waiting for transfers between devices: none -> 7.16 us  [step(): sigma = lax.ppermute(sigma, ('energy', 'section'), crossing)]
    ppermute x6, waiting for transfers between devices: 7.81 us -> 14.7 us  [over_energy(): return lax.ppermute(value, 'energy', route)]
    unnamed x14 -> x6, local copies, waits for them, and re-layouts: 4 us -> 0.02 us
    ppermute x0 -> x1, starting transfers between devices: none -> 2.49 us  [step(): sigma = lax.ppermute(sigma, ('energy', 'section'), crossing)]
    ppermute x7 -> x6, starting transfers between devices: 18.9 us -> 16.6 us  [over_section(): return lax.ppermute(value, 'section', route)]
    pallas_call x1, Pallas kernels: 0.89 us -> 2.07 us  [prepare(): pl.pallas_call(functools.partial(prepare_kernel, sections, spread), out_s...]
    pallas_call x15 -> x16, Pallas kernels: 14.8 us -> 14.8 us  [call(): pl.pallas_call(body, out_shape=out_shape, in_specs=[VMEM] * len(operands)...]
  transfers between devices with their start and end apart: 13 -> 13, of which waited for: 6 -> 8; matrix products, arithmetic and copies ran while one was open for 0% -> 0% of each run, Pallas kernels for 5% -> 5%
where the time goes in v2:
time: 81.6 us; the launch traced here: 81.3 us
  waiting for transfers between devices  33.9 us (42%)
  starting transfers between devices  28.3 us (35%)
  Pallas kernels  18.2 us (22%)
  between operations  0.87 us (1%)
    ppermute x6, starting transfers between devices, over_section(): return lax.ppermute(value, 'section', route)  16.6 us
    pallas_call x16, Pallas kernels, call(): pl.pallas_call(body, out_shape=out_shape, in_specs=[VMEM] * len(operands)...  14.8 us
    ppermute x6, waiting for transfers between devices, over_energy(): return lax.ppermute(value, 'energy', route)  14.7 us
    ppermute x6, waiting for transfers between devices, over_section(): return lax.ppermute(value, 'section', route)  12.1 us
    ppermute x6, starting transfers between devices, over_energy(): return lax.ppermute(value, 'energy', route)  9.25 us
    ppermute x1, waiting for transfers between devices, step(): sigma = lax.ppermute(sigma, ('energy', 'section'), crossing)  7.16 us
    ppermute x1, starting transfers between devices, step(): sigma = lax.ppermute(sigma, ('energy', 'section'), crossing)  2.49 us
    pallas_call x1, Pallas kernels, prepare(): pl.pallas_call(functools.partial(prepare_kernel, sections, spread), out_s...  2.07 us
  transfers between devices with their start and end apart: 13, of which 8 were waited for; matrix products, arithmetic and copies ran while one was open for 0% of the time, Pallas kernels for 5%

profile of v2, /device:TPU:1, one launch (start us, length us, event | category | flops | bytes accessed | tf_op | source)
XLA Modules:
  0.0 81.3 jit_solution(11150478551071402618)
XLA Ops:
  0.7 2.1 %prepare.1.refs_0_.refs_1_.refs_2_.source.refs_3_ = f32[8,256,256]{2,1,0:T(8,128)S(1)} custom-call(f32[1,1]{1,0:T(1,128)} %bitcast.1.broadening, f32[2,256]{1,0:T(2,128)} %onsite.1, f32[2,256,256]{2,1,0:T(8,128)} %hopping.1, f32[2,256,256]{2,1,0:T(8,128)} %coupling.1, f32[1,2,2,256,256]{4,3,2,1,0:T(8,128)} %born.1), custom_call_target="tpu_custom_call" | custom-call | tf_op jit(solution)/shard_map/prepare/pallas_call | solution.py:290
  2.8 4.5 %collective-permute-start = (f32[2,256,256]{2,1,0:T(8,128)S(1)}, f32[2,256,256]{2,1,0:T(8,128)S(1)}, u32[]{:S(2)}, u32[]{:S(2)}) collective-permute-start(f32[2,256,256]{2,1,0:T(8,128)S(1)} %shard_map.83), channel_id=1, source_target_pairs={{0,1},{1,0},{2,3},{3,2},{4,5},{5,4},{6,7},{7,6},{8,9},{9,8},{10,11... | collective-permute-start | bytes 1572872 | tf_op jit(solution)/shard_map/ppermute | solution.py:470
  7.4 1.5 %collective-permute-done.value = f32[2,256,256]{2,1,0:T(8,128)S(1)} collective-permute-done((f32[2,256,256]{2,1,0:T(8,128)S(1)}, f32[2,256,256]{2,1,0:T(8,128)S(1)}, u32[]{:S(2)}, u32[]{:S(2)}) %collective-permute-start) | collective-permute-done | bytes 524320 | tf_op jit(solution)/shard_map/ppermute | solution.py:470
  8.9 2.2 %shard_map.85.refs_1_ = f32[2,256,256]{2,1,0:T(8,128)S(1)} custom-call(f32[8,256,256]{2,1,0:T(8,128)S(1)} %prepare.1.refs_0_.refs_1_.refs_2_.source.refs_3_, f32[2,256,256]{2,1,0:T(8,128)S(1)} %shard_map.84.refs_1_, f32[8,256,256]{2,1,0:T(8,128)S(1)} %prepare.1.refs_0_.refs_1_.refs_2_.source.refs_3_), custom_call_target="tpu_custom_call" | custom-call | flops 1610612736 | bytes 2097152 | tf_op jit(solution)/shard_map/pallas_call | solution.py:105
  11.2 2.5 %shard_map.86._ = f32[2,256,256]{2,1,0:T(8,128)S(1)} custom-call(f32[8,256,256]{2,1,0:T(8,128)S(1)} %prepare.1.refs_0_.refs_1_.refs_2_.source.refs_3_, f32[2,256,256]{2,1,0:T(8,128)S(1)} %shard_map.85.refs_1_, f32[8,256,256]{2,1,0:T(8,128)S(1)} %prepare.1.refs_0_.refs_1_.refs_2_.source.refs_3_), custom_call_target="tpu_custom_call" | custom-call | flops 1610612736 | bytes 2097152 | tf_op jit(solution)/shard_map/pallas_call | solution.py:105
  13.8 2.5 %collective-permute-start.2 = (f32[2,256,256]{2,1,0:T(8,128)S(1)}, f32[2,256,256]{2,1,0:T(8,128)S(1)}, u32[]{:S(2)}, u32[]{:S(2)}) collective-permute-start(f32[2,256,256]{2,1,0:T(8,128)S(1)} %shard_map.86._), channel_id=1, source_target_pairs={{1,2},{2,1},{0,4},{3,7},{5,6},{6,5},{4,0},{7,3},{9,10},{10,9},{8,1... | collective-permute-start | bytes 1572872 | tf_op jit(solution)/shard_map/ppermute | solution.py:509
  16.3 7.2 %collective-permute-done.2.value = f32[2,256,256]{2,1,0:T(8,128)S(1)} collective-permute-done((f32[2,256,256]{2,1,0:T(8,128)S(1)}, f32[2,256,256]{2,1,0:T(8,128)S(1)}, u32[]{:S(2)}, u32[]{:S(2)}) %collective-permute-start.2) | collective-permute-done | bytes 524320 | tf_op jit(solution)/shard_map/ppermute | solution.py:509
  23.5 0.8 %shard_map.87.refs_2_ = f32[2,256,256]{2,1,0:T(8,128)S(1)} custom-call(f32[8,256,256]{2,1,0:T(8,128)S(1)} %prepare.1.refs_0_.refs_1_.refs_2_.source.refs_3_, f32[2,256,256]{2,1,0:T(8,128)S(1)} %collective-permute-done.2.value), custom_call_target="tpu_custom_call" | custom-call | flops 402653184 | bytes 2097152 | tf_op jit(solution)/shard_map/pallas_call | solution.py:105
  24.3 0.3 collective-permute-start.3
  24.6 1.4 %weights.1 = (f32[5,256,256]{2,1,0:T(8,128)S(1)}, f32[5,256,256]{2,1,0:T(8,128)S(1)}) custom-call(s32[4]{0:T(128)S(1)} %copy-done.2, f32[4,256,256]{2,1,0:T(8,128)S(1)} %copy-done, f32[4,256,256]{2,1,0:T(8,128)S(1)} %copy-done.1, f32[2,256,256]{2,1,0:T(8,128)S(1)} %shard_map.86._), custom_call_target="tpu_custom_call" | custom-call | flops 1048576 | bytes 8388608 | tf_op jit(solution)/shard_map/weights/pallas_call | solution.py:339
  26.0 1.9 %shard_map.88 = (f32[256,256]{1,0:T(8,128)S(1)}, f32[256,256]{1,0:T(8,128)S(1)}) custom-call(f32[8,256,256]{2,1,0:T(8,128)S(1)} %prepare.1.refs_0_.refs_1_.refs_2_.source.refs_3_, f32[2,256,256]{2,1,0:T(8,128)S(1)} %shard_map.85.refs_1_, f32[2,256,256]{2,1,0:T(8,128)S(1)} %shard_map.87.refs_2_, f32[5,256,256]{2,1,0:T(8,128)S(1)} %get-tuple-element.22.refs_3_.refs_0_, ...), custom_call_target="tpu_custom_call" | custom-call | flops 1207959552 | bytes 2097152 | tf_op jit(solution)/shard_map/pallas_call | solution.py:105
  28.0 0.3 shard_map.91
  28.3 2.3 %shard_map.92.refs_2_ = f32[2,256,256]{2,1,0:T(8,128)S(1)} custom-call(f32[8,256,256]{2,1,0:T(8,128)S(1)} %prepare.1.refs_0_.refs_1_.refs_2_.source.refs_3_, f32[2,256,256]{2,1,0:T(8,128)S(1)} %shard_map.90.refs_2_.refs_1_, f32[2,256,256]{2,1,0:T(8,128)S(1)} %shard_map.87.refs_2_, f32[8,256,256]{2,1,0:T(8,128)S(1)} %prepare.1.refs_0_.refs_1_.refs_2_.source.refs_3_, ...), custom_call_target="tpu_custom_call" | custom-call | flops 1610612736 | bytes 2097152 | tf_op jit(solution)/shard_map/pallas_call | solution.py:105
  30.5 1.8 %shard_map.93 = (f32[2,256,256]{2,1,0:T(8,128)S(1)}, f32[2,256,256]{2,1,0:T(8,128)S(1)}) custom-call(f32[8,256,256]{2,1,0:T(8,128)S(1)} %prepare.1.refs_0_.refs_1_.refs_2_.source.refs_3_, f32[2,256,256]{2,1,0:T(8,128)S(1)} %shard_map.84.refs_1_, f32[2,256,256]{2,1,0:T(8,128)S(1)} %shard_map.92.refs_2_, f32[256,256]{1,0:T(8,128)S(1)} %get-tuple-element.27.refs_4_.refs_3_, ...), custom_call_target="tpu_custom_call" | custom-call | flops 1207959552 | bytes 2097152 | tf_op jit(solution)/shard_map/pallas_call | solution.py:105
  32.4 1.9 %collective-permute-start.4 = (f32[2,256,256]{2,1,0:T(8,128)S(1)}, f32[2,256,256]{2,1,0:T(8,128)S(1)}, u32[]{:S(2)}, u32[]{:S(2)}) collective-permute-start(f32[2,256,256]{2,1,0:T(8,128)S(1)} %get-tuple-element.29.real.refs_0_.refs_2_), channel_id=1, source_target_pairs={{0,4},{4,0},{8,12},{12,8},{16,20},{20,16},{24,28},{28,24},{1,5},{5... | collective-permute-start | bytes 1572872 | tf_op jit(solution)/shard_map/ppermute | solution.py:473
  34.3 0.7 collective-permute-start.6
  35.0 3.9 %collective-permute-start.5 = (f32[2,256,256]{2,1,0:T(8,128)S(1)}, f32[2,256,256]{2,1,0:T(8,128)S(1)}, u32[]{:S(2)}, u32[]{:S(2)}) collective-permute-start(f32[2,256,256]{2,1,0:T(8,128)S(1)} %get-tuple-element.30.imag.refs_4_), channel_id=1, source_target_pairs={{0,8},{4,12},{8,0},{12,4},{16,24},{20,28},{24,16},{28,20},{1,9},{5... | collective-permute-start | bytes 1572872 | tf_op jit(solution)/shard_map/ppermute | solution.py:473
  38.9 2.8 %collective-permute-done.4.partner.refs_1_.refs_3_ = f32[2,256,256]{2,1,0:T(8,128)S(1)} collective-permute-done((f32[2,256,256]{2,1,0:T(8,128)S(1)}, f32[2,256,256]{2,1,0:T(8,128)S(1)}, u32[]{:S(2)}, u32[]{:S(2)}) %collective-permute-start.4) | collective-permute-done | bytes 524320 | tf_op jit(solution)/shard_map/ppermute | solution.py:473
  41.7 4.1 %collective-permute-done.5.ahead.refs_5_ = f32[2,256,256]{2,1,0:T(8,128)S(1)} collective-permute-done((f32[2,256,256]{2,1,0:T(8,128)S(1)}, f32[2,256,256]{2,1,0:T(8,128)S(1)}, u32[]{:S(2)}, u32[]{:S(2)}) %collective-permute-start.5) | collective-permute-done | bytes 524320 | tf_op jit(solution)/shard_map/ppermute | solution.py:473
  45.7 0.6 shard_map.94
  46.4 6.2 %collective-permute-start.9 = (f32[4,256,256]{2,1,0:T(8,128)S(1)}, f32[4,256,256]{2,1,0:T(8,128)S(1)}, u32[]{:S(2)}, u32[]{:S(2)}) collective-permute-start(f32[4,256,256]{2,1,0:T(8,128)S(1)} %get-tuple-element.34), channel_id=1, source_target_pairs={{0,1},{1,0},{2,3},{3,2},{4,5},{5,4},{6,7},{7,6},{8,9},{9,8},{10,11... | collective-permute-start | bytes 3145736 | tf_op jit(solution)/shard_map/ppermute | solution.py:470
  52.5 2.3 %collective-permute-start.7 = (f32[2,256,256]{2,1,0:T(8,128)S(1)}, f32[2,256,256]{2,1,0:T(8,128)S(1)}, u32[]{:S(2)}, u32[]{:S(2)}) collective-permute-start(f32[2,256,256]{2,1,0:T(8,128)S(1)} %shard_map.95), channel_id=1, source_target_pairs={{1,2},{2,1},{5,6},{6,5},{9,10},{10,9},{13,14},{14,13},{17,18},{18,... | collective-permute-start | bytes 1572872 | tf_op jit(solution)/shard_map/ppermute | solution.py:470
  54.9 3.2 %collective-permute-start.8 = (f32[2,256,256]{2,1,0:T(8,128)S(1)}, f32[2,256,256]{2,1,0:T(8,128)S(1)}, u32[]{:S(2)}, u32[]{:S(2)}) collective-permute-start(f32[2,256,256]{2,1,0:T(8,128)S(1)} %get-tuple-element.33), channel_id=1, source_target_pairs={{1,2},{2,1},{5,6},{6,5},{9,10},{10,9},{13,14},{14,13},{17,18},{18,... | collective-permute-start | bytes 1572872 | tf_op jit(solution)/shard_map/ppermute | solution.py:470
  58.1 5.2 %collective-permute-done.7.refs_9_ = f32[2,256,256]{2,1,0:T(8,128)S(1)} collective-permute-done((f32[2,256,256]{2,1,0:T(8,128)S(1)}, f32[2,256,256]{2,1,0:T(8,128)S(1)}, u32[]{:S(2)}, u32[]{:S(2)}) %collective-permute-start.7) | collective-permute-done | bytes 524320 | tf_op jit(solution)/shard_map/ppermute | solution.py:470
  63.3 5.3 %collective-permute-done.8.refs_10_ = f32[2,256,256]{2,1,0:T(8,128)S(1)} collective-permute-done((f32[2,256,256]{2,1,0:T(8,128)S(1)}, f32[2,256,256]{2,1,0:T(8,128)S(1)}, u32[]{:S(2)}, u32[]{:S(2)}) %collective-permute-start.8) | collective-permute-done | bytes 524320 | tf_op jit(solution)/shard_map/ppermute | solution.py:470
  68.7 1.0 %shard_map.96 = (f32[2,256,256]{2,1,0:T(8,128)S(1)}, f32[2,256,256]{2,1,0:T(8,128)S(1)}, f32[2,256,256]{2,1,0:T(8,128)S(1)}, f32[4,256,256]{2,1,0:T(8,128)S(1)}) custom-call(f32[5,256,256]{2,1,0:T(8,128)S(1)} %get-tuple-element.22.refs_3_.refs_0_, f32[5,256,256]{2,1,0:T(8,128)S(1)} %get-tuple-element.23.refs_4_.weight.refs_1_, ...), custom_call_target="tpu_custom_call" | custom-call | flops 100663296 | bytes 2097152 | tf_op jit(solution)/shard_map/pallas_call | solution.py:105
  69.7 1.8 %collective-permute-start.10 = (f32[2,256,256]{2,1,0:T(8,128)S(1)}, f32[2,256,256]{2,1,0:T(8,128)S(1)}, u32[]{:S(2)}, u32[]{:S(2)}) collective-permute-start(f32[2,256,256]{2,1,0:T(8,128)S(1)} %get-tuple-element.36), channel_id=1, source_target_pairs={{0,8},{4,12},{8,0},{12,4},{16,24},{20,28},{24,16},{28,20},{1,9},{5... | collective-permute-start | bytes 1572872 | tf_op jit(solution)/shard_map/ppermute | solution.py:473
  71.5 0.7 collective-permute-start.11
  72.1 0.3 collective-permute-start.12
  72.4 5.6 %collective-permute-done.10.from_first = f32[2,256,256]{2,1,0:T(8,128)S(1)} collective-permute-done((f32[2,256,256]{2,1,0:T(8,128)S(1)}, f32[2,256,256]{2,1,0:T(8,128)S(1)}, u32[]{:S(2)}, u32[]{:S(2)}) %collective-permute-start.10) | collective-permute-done | bytes 524320 | tf_op jit(solution)/shard_map/ppermute | solution.py:473
  78.0 2.2 %collective-permute-done.12.from_partner = f32[2,256,256]{2,1,0:T(8,128)S(1)} collective-permute-done((f32[2,256,256]{2,1,0:T(8,128)S(1)}, f32[2,256,256]{2,1,0:T(8,128)S(1)}, u32[]{:S(2)}, u32[]{:S(2)}) %collective-permute-start.12) | collective-permute-done | bytes 524320 | tf_op jit(solution)/shard_map/ppermute | solution.py:473
  80.2 1.1 %shard_map.97 = f32[1,2,2,256,256]{4,3,2,1,0:T(8,128)} custom-call(f32[4,256,256]{2,1,0:T(8,128)S(1)} %get-tuple-element.35.own, f32[2,256,256]{2,1,0:T(8,128)S(1)} %collective-permute-done.10.from_first, f32[2,256,256]{2,1,0:T(8,128)S(1)} %collective-permute-done.11.from_second, f32[2,256,256]{2,1,0:T(8,128)S(1)} %collective-permute-done.12.from_partner), custom_call_target="tpu_custom_call" | custom-call | flops 100663296 | bytes 2097152 | tf_op jit(solution)/shard_map/pallas_call | solution.py:105
  (18 shorter events, 0.4 us)
Async XLA Ops:
  2.8 6.1 %collective-permute-start = (f32[2,256,256]{2,1,0:T(8,128)S(1)}, f32[2,256,256]{2,1,0:T(8,128)S(1)}, u32[]{:S(2)}, u32[]{:S(2)}) collective-permute-start(f32[2,256,256]{2,1,0:T(8,128)S(1)} %shard_map.83), channel_id=1, source_target_pairs={{0,1},{1,0},{2,3},{3,2},{4,5},{5,4},{6,7},{7,6},{8,9},{9,8},{10,11... | collective-permute-start | bytes 1572872 | tf_op jit(solution)/shard_map/ppermute | solution.py:470
  13.7 10.9 %copy-start = (f32[4,256,256]{2,1,0:T(8,128)S(1)}, f32[4,256,256]{2,1,0:T(8,128)}, u32[]{:S(2)}) copy-start(f32[4,256,256]{2,1,0:T(8,128)} %local_ref.1) | copy-start | bytes 3145732
  13.7 10.9 %copy-start.1 = (f32[4,256,256]{2,1,0:T(8,128)S(1)}, f32[4,256,256]{2,1,0:T(8,128)}, u32[]{:S(2)}) copy-start(f32[4,256,256]{2,1,0:T(8,128)} %side_ref.1) | copy-start | bytes 3145732
  13.7 10.9 %copy-start.2 = (s32[4]{0:T(128)S(1)}, s32[4]{0:T(128)}, u32[]{:S(2)}) copy-start(s32[4]{0:T(128)} %shift_ref.1) | copy-start | bytes 52
  13.7 14.1 %collective-permute-start.1 = (f32[8,256,256]{2,1,0:T(8,128)S(1)}, f32[8,256,256]{2,1,0:T(8,128)S(1)}, u32[]{:S(2)}, u32[]{:S(2)}) collective-permute-start(f32[8,256,256]{2,1,0:T(8,128)S(1)} %prepare.1.refs_0_.refs_1_.refs_2_.source.refs_3_), channel_id=1, source_target_pairs={{0,1},{1,0},{2,3},{3,2},{4,5},{5,4},{6,7},{7,6},{8,9},{9,8},{10,11... | collective-permute-start | bytes 6291464 | tf_op jit(solution)/shard_map/ppermute | solution.py:470
  13.8 9.7 %collective-permute-start.2 = (f32[2,256,256]{2,1,0:T(8,128)S(1)}, f32[2,256,256]{2,1,0:T(8,128)S(1)}, u32[]{:S(2)}, u32[]{:S(2)}) collective-permute-start(f32[2,256,256]{2,1,0:T(8,128)S(1)} %shard_map.86._), channel_id=1, source_target_pairs={{1,2},{2,1},{0,4},{3,7},{5,6},{6,5},{4,0},{7,3},{9,10},{10,9},{8,1... | collective-permute-start | bytes 1572872 | tf_op jit(solution)/shard_map/ppermute | solution.py:509
  24.3 3.6 %collective-permute-start.3 = (f32[2,256,256]{2,1,0:T(8,128)S(1)}, f32[2,256,256]{2,1,0:T(8,128)S(1)}, u32[]{:S(2)}, u32[]{:S(2)}) collective-permute-start(f32[2,256,256]{2,1,0:T(8,128)S(1)} %shard_map.87.refs_2_), channel_id=1, source_target_pairs={{0,1},{1,0},{2,3},{3,2},{4,5},{5,4},{6,7},{7,6},{8,9},{9,8},{10,11... | collective-permute-start | bytes 1572872 | tf_op jit(solution)/shard_map/ppermute | solution.py:470
  32.4 9.3 %collective-permute-start.4 = (f32[2,256,256]{2,1,0:T(8,128)S(1)}, f32[2,256,256]{2,1,0:T(8,128)S(1)}, u32[]{:S(2)}, u32[]{:S(2)}) collective-permute-start(f32[2,256,256]{2,1,0:T(8,128)S(1)} %get-tuple-element.29.real.refs_0_.refs_2_), channel_id=1, source_target_pairs={{0,4},{4,0},{8,12},{12,8},{16,20},{20,16},{24,28},{28,24},{1,5},{5... | collective-permute-start | bytes 1572872 | tf_op jit(solution)/shard_map/ppermute | solution.py:473
  34.3 7.3 %collective-permute-start.6 = (f32[2,256,256]{2,1,0:T(8,128)S(1)}, f32[2,256,256]{2,1,0:T(8,128)S(1)}, u32[]{:S(2)}, u32[]{:S(2)}) collective-permute-start(f32[2,256,256]{2,1,0:T(8,128)S(1)} %get-tuple-element.30.imag.refs_4_), channel_id=1, source_target_pairs={{8,16},{12,20},{16,8},{20,12},{9,17},{13,21},{17,9},{21,13},{10,18... | collective-permute-start | bytes 1572872 | tf_op jit(solution)/shard_map/ppermute | solution.py:473
  35.0 10.7 %collective-permute-start.5 = (f32[2,256,256]{2,1,0:T(8,128)S(1)}, f32[2,256,256]{2,1,0:T(8,128)S(1)}, u32[]{:S(2)}, u32[]{:S(2)}) collective-permute-start(f32[2,256,256]{2,1,0:T(8,128)S(1)} %get-tuple-element.30.imag.refs_4_), channel_id=1, source_target_pairs={{0,8},{4,12},{8,0},{12,4},{16,24},{20,28},{24,16},{28,20},{1,9},{5... | collective-permute-start | bytes 1572872 | tf_op jit(solution)/shard_map/ppermute | solution.py:473
  46.4 22.3 %collective-permute-start.9 = (f32[4,256,256]{2,1,0:T(8,128)S(1)}, f32[4,256,256]{2,1,0:T(8,128)S(1)}, u32[]{:S(2)}, u32[]{:S(2)}) collective-permute-start(f32[4,256,256]{2,1,0:T(8,128)S(1)} %get-tuple-element.34), channel_id=1, source_target_pairs={{0,1},{1,0},{2,3},{3,2},{4,5},{5,4},{6,7},{7,6},{8,9},{9,8},{10,11... | collective-permute-start | bytes 3145736 | tf_op jit(solution)/shard_map/ppermute | solution.py:470
  52.5 10.8 %collective-permute-start.7 = (f32[2,256,256]{2,1,0:T(8,128)S(1)}, f32[2,256,256]{2,1,0:T(8,128)S(1)}, u32[]{:S(2)}, u32[]{:S(2)}) collective-permute-start(f32[2,256,256]{2,1,0:T(8,128)S(1)} %shard_map.95), channel_id=1, source_target_pairs={{1,2},{2,1},{5,6},{6,5},{9,10},{10,9},{13,14},{14,13},{17,18},{18,... | collective-permute-start | bytes 1572872 | tf_op jit(solution)/shard_map/ppermute | solution.py:470
  54.9 13.8 %collective-permute-start.8 = (f32[2,256,256]{2,1,0:T(8,128)S(1)}, f32[2,256,256]{2,1,0:T(8,128)S(1)}, u32[]{:S(2)}, u32[]{:S(2)}) collective-permute-start(f32[2,256,256]{2,1,0:T(8,128)S(1)} %get-tuple-element.33), channel_id=1, source_target_pairs={{1,2},{2,1},{5,6},{6,5},{9,10},{10,9},{13,14},{14,13},{17,18},{18,... | collective-permute-start | bytes 1572872 | tf_op jit(solution)/shard_map/ppermute | solution.py:470
  69.7 8.4 %collective-permute-start.10 = (f32[2,256,256]{2,1,0:T(8,128)S(1)}, f32[2,256,256]{2,1,0:T(8,128)S(1)}, u32[]{:S(2)}, u32[]{:S(2)}) collective-permute-start(f32[2,256,256]{2,1,0:T(8,128)S(1)} %get-tuple-element.36), channel_id=1, source_target_pairs={{0,8},{4,12},{8,0},{12,4},{16,24},{20,28},{24,16},{28,20},{1,9},{5... | collective-permute-start | bytes 1572872 | tf_op jit(solution)/shard_map/ppermute | solution.py:473
  71.5 6.6 %collective-permute-start.11 = (f32[2,256,256]{2,1,0:T(8,128)S(1)}, f32[2,256,256]{2,1,0:T(8,128)S(1)}, u32[]{:S(2)}, u32[]{:S(2)}) collective-permute-start(f32[2,256,256]{2,1,0:T(8,128)S(1)} %get-tuple-element.37), channel_id=1, source_target_pairs={{8,16},{12,20},{16,8},{20,12},{9,17},{13,21},{17,9},{21,13},{10,18... | collective-permute-start | bytes 1572872 | tf_op jit(solution)/shard_map/ppermute | solution.py:473
  72.1 8.1 %collective-permute-start.12 = (f32[2,256,256]{2,1,0:T(8,128)S(1)}, f32[2,256,256]{2,1,0:T(8,128)S(1)}, u32[]{:S(2)}, u32[]{:S(2)}) collective-permute-start(f32[2,256,256]{2,1,0:T(8,128)S(1)} %get-tuple-element.38), channel_id=1, source_target_pairs={{0,4},{4,0},{8,12},{12,8},{16,20},{20,16},{24,28},{28,24},{1,5},{5... | collective-permute-start | bytes 1572872 | tf_op jit(solution)/shard_map/ppermute | solution.py:473

commit v3 on v2

--- a/solution.py
+++ b/solution.py
@@ -388,31 +388,24 @@
     )
 
 
-def combine(sections, tables):
+def combine(sections, tables, early):
     names = list(tables)
     blocks, dimension = tables["real"].shape[0], tables["real"].shape[-1]
+    last = blocks - 1
+    count = 1 if early else last
 
     def body(*refs):
         t = dict(zip(names, refs))
         to_first, to_second, to_partner, own = refs[len(names) :]
         a, b = t["local_weight"], t["side_weight"]
-        outer = is_at(0, sections)
         chosen = first_is_far()
-        last = blocks - 1
-        for index in range(blocks):
+
+        def emit(place, index, ends):
             sides = []
-            for place, name in enumerate(("real", "partner", "side_partner", "side_own")):
-                table = t[name]
-                if index == 0:
-                    side = jnp.where(outer, 0.0, t["shared"][place])
-                else:
-                    side = table[index - 1]
-                if index < last:
-                    side = side + table[index + 1]
-                else:
-                    middle = t["middle_real"][place] if place < 2 else t["middle"][place - 2]
-                    side = side + jnp.where(outer, t["shared"][place], middle)
-                sides.append(side)
+            for number, name in enumerate(("real", "partner", "side_partner", "side_own")):
+                terms = [t[name][i] for i in (index - 1, index + 1) if 0 <= i <= last]
+                terms += [end(number) for end in ends]
+                sides.append(functools.reduce(jnp.add, terms))
             n_real, n_partner, n_for, n_own = sides
             real, partner, imag = t["real"][index], t["partner"][index], t["imag"][index]
             ahead, behind = t["ahead"][index], t["behind"][index]
@@ -420,37 +413,64 @@
             near = jnp.where(chosen, behind, ahead)
             pair = a[PAIR] * real + a[NEXT] * partner + b[PAIR] * n_real + b[NEXT] * n_partner
             lone = a[LONE] * real + b[LONE] * n_real
-            to_first[index] = jnp.where(chosen, pair, lone)
-            to_second[index] = jnp.where(chosen, lone, pair)
-            to_partner[index] = a[NEXT] * imag + a[OTHER] * far + n_for
-            own[2 * index] = (
+            to_first[place] = jnp.where(chosen, pair, lone)
+            to_second[place] = jnp.where(chosen, lone, pair)
+            to_partner[place] = a[NEXT] * imag + a[OTHER] * far + n_for
+            own[2 * place] = (
                 a[OWN] * real + a[OTHER] * partner + b[OWN] * n_real + b[OTHER] * n_partner
             )
-            own[2 * index + 1] = a[OWN] * imag + a[LONE] * far + a[PAIR] * near + n_own
+            own[2 * place + 1] = a[OWN] * imag + a[LONE] * far + a[PAIR] * near + n_own
+
+        def middle(number):
+            return t["middle_real"][number] if number < 2 else t["middle"][number - 2]
+
+        def shared(number):
+            return t["shared"][number]
+
+        outer = is_at(0, sections)
+
+        @pl.when(outer)
+        def _():
+            for place in range(count):
+                index = 0 if early else place + 1
+                emit(place, index, [shared] if not early and index == last else [])
+
+        @pl.when(jnp.logical_not(outer))
+        def _():
+            for place in range(count):
+                index = last if early else place
+                emit(place, index, [middle] if early else [shared] if index == 0 else [])
 
     def shape(count):
         return jax.ShapeDtypeStruct((count, dimension, dimension), F32)
 
     return call(
         body,
-        (shape(blocks), shape(blocks), shape(blocks), shape(2 * blocks)),
+        (shape(count), shape(count), shape(count), shape(2 * count)),
         [tables[name] for name in names],
         1,
     )
 
 
-def finish(sections, own, from_first, from_second, from_partner):
-    blocks, dimension = from_first.shape[0], from_first.shape[-1]
-
-    def body(own, from_first, from_second, from_partner, out):
+def finish(sections, early, late):
+    blocks, dimension = 1 + late[1].shape[0], late[1].shape[-1]
+    last = blocks - 1
+
+    def body(*refs):
+        out = refs[-1]
         right_half = half_of(sections)
-        for index in range(blocks):
-            place = jnp.where(right_half, blocks - 1 - index, index)
-            out[0, place, 0] = own[2 * index] + (from_first[index] + from_second[index])
-            out[0, place, 1] = own[2 * index + 1] + from_partner[index]
+        outer = is_at(0, sections)
+        for number, group in enumerate((refs[:4], refs[4:8])):
+            own, from_first, from_second, from_partner = group
+            for k in range(1 if number == 0 else last):
+                low, high = (0, last) if number == 0 else (k + 1, k)
+                index = jnp.where(outer, low, high)
+                place = jnp.where(right_half, last - index, index)
+                out[0, place, 0] = own[2 * k] + (from_first[k] + from_second[k])
+                out[0, place, 1] = own[2 * k + 1] + from_partner[k]
 
     shape = jax.ShapeDtypeStruct((1, blocks, 2, dimension, dimension), F32)
-    return call(body, shape, [own, from_first, from_second, from_partner], 1)
+    return call(body, shape, list(early) + list(late), 1)
 
 
 def step(
@@ -510,7 +530,7 @@
 
     all_weights = weights(phonon_shift, phonon_local, phonon_side, leaving)
     local_weight, side_weight = all_weights
-    pack_in = over_section(lax.optimization_barrier((pack, leaving))[0], pairs)
+    pack_in = over_section(pack, pairs)
     arriving = enter_step(sections, half - 1, 0, pack, sigma)
     earlier = tuple(first[step][last] for step in range(half))
     sigma = over_section(arriving, pairs)
@@ -547,30 +567,30 @@
     )
     middle = over_section(middle, across)
     shared = over_section(shared, pairs)
-    to_first, to_second, to_partner, own = combine(
-        sections,
-        {
-            "local_weight": local_weight,
-            "side_weight": side_weight,
-            "real": real,
-            "partner": partner,
-            "imag": imag,
-            "ahead": ahead,
-            "behind": behind,
-            "side_partner": side_partner,
-            "side_own": side_own,
-            "middle_real": middle_real,
-            "middle": middle,
-            "shared": shared,
-        },
-    )
-    return finish(
-        sections,
-        own,
-        over_energy(to_first, first_swap),
-        over_energy(to_second, second_swap),
-        over_energy(to_partner, swap),
-    )
+    tables = {
+        "local_weight": local_weight,
+        "side_weight": side_weight,
+        "real": real,
+        "partner": partner,
+        "imag": imag,
+        "ahead": ahead,
+        "behind": behind,
+        "side_partner": side_partner,
+        "side_own": side_own,
+    }
+
+    def exchange(to_first, to_second, to_partner, own):
+        from_first = over_energy(to_first, first_swap)
+        from_second = over_energy(to_second, second_swap)
+        from_partner = over_energy(to_partner, swap)
+        return own, from_first, from_second, from_partner
+
+    ends = {"middle_real": middle_real, "middle": middle}
+    early = combine(sections, tables | ends, True)
+    early = exchange(*early)
+    late = combine(sections, tables | {"shared": shared}, False)
+    late = exchange(*late)
+    return finish(sections, early, late)
 
 
 def solution(mesh):

time: 81.6 us -> 82.9 us (1.016)
  the two profiles are of different devices: /device:TPU:1 before, /device:TPU:10 now
where the time goes in v3:
time: 82.9 us; the launch traced here: 82.6 us
  waiting for transfers between devices  36.7 us (44%)
  starting transfers between devices  27.1 us (33%)
  Pallas kernels  17.8 us (21%)
  between operations  0.93 us (1%)
    ppermute x9, waiting for transfers between devices, over_energy(): return lax.ppermute(value, 'energy', route)  16.2 us
    pallas_call x17, Pallas kernels, call(): pl.pallas_call(body, out_shape=out_shape, in_specs=[VMEM] * len(operands)...  14.4 us
    ppermute x6, starting transfers between devices, over_section(): return lax.ppermute(value, 'section', route)  13.6 us
    ppermute x9, starting transfers between devices, over_energy(): return lax.ppermute(value, 'energy', route)  13.3 us
    ppermute x6, waiting for transfers between devices, over_section(): return lax.ppermute(value, 'section', route)  12.1 us
    ppermute x1, waiting for transfers between devices, step(): sigma = lax.ppermute(sigma, ('energy', 'section'), crossing)  8.45 us
    pallas_call x1, Pallas kernels, prepare(): pl.pallas_call(functools.partial(prepare_kernel, sections, spread), out_s...  2.07 us
  transfers between devices with their start and end apart: 16, of which 11 were waited for; matrix products, arithmetic and copies ran while one was open for 0% of the time, Pallas kernels for 12%

profile of v3, /device:TPU:10, one launch (start us, length us, event | category | flops | bytes accessed | tf_op | source)
XLA Modules:
  0.0 82.6 jit_solution(2152596554036556359)
XLA Ops:
  0.7 2.1 %prepare.1.refs_0_.refs_1_.refs_2_.source.refs_3_ = f32[8,256,256]{2,1,0:T(8,128)S(1)} custom-call(f32[1,1]{1,0:T(1,128)} %bitcast.1.broadening, f32[2,256]{1,0:T(2,128)} %onsite.1, f32[2,256,256]{2,1,0:T(8,128)} %hopping.1, f32[2,256,256]{2,1,0:T(8,128)} %coupling.1, f32[1,2,2,256,256]{4,3,2,1,0:T(8,128)} %born.1), custom_call_target="tpu_custom_call" | custom-call | tf_op jit(solution)/shard_map/prepare/pallas_call | solution.py:290
  2.9 4.6 %collective-permute-start = (f32[2,256,256]{2,1,0:T(8,128)S(1)}, f32[2,256,256]{2,1,0:T(8,128)S(1)}, u32[]{:S(2)}, u32[]{:S(2)}) collective-permute-start(f32[2,256,256]{2,1,0:T(8,128)S(1)} %shard_map.83), channel_id=1, source_target_pairs={{0,1},{1,0},{2,3},{3,2},{4,5},{5,4},{6,7},{7,6},{8,9},{9,8},{10,11... | collective-permute-start | bytes 1572872 | tf_op jit(solution)/shard_map/ppermute | solution.py:490
  7.5 1.5 %collective-permute-done.value = f32[2,256,256]{2,1,0:T(8,128)S(1)} collective-permute-done((f32[2,256,256]{2,1,0:T(8,128)S(1)}, f32[2,256,256]{2,1,0:T(8,128)S(1)}, u32[]{:S(2)}, u32[]{:S(2)}) %collective-permute-start) | collective-permute-done | bytes 524320 | tf_op jit(solution)/shard_map/ppermute | solution.py:490
  9.1 0.8 shard_map.84.refs_1_
  9.9 2.3 %shard_map.85.refs_1_ = f32[2,256,256]{2,1,0:T(8,128)S(1)} custom-call(f32[8,256,256]{2,1,0:T(8,128)S(1)} %prepare.1.refs_0_.refs_1_.refs_2_.source.refs_3_, f32[2,256,256]{2,1,0:T(8,128)S(1)} %shard_map.84.refs_1_, f32[8,256,256]{2,1,0:T(8,128)S(1)} %prepare.1.refs_0_.refs_1_.refs_2_.source.refs_3_), custom_call_target="tpu_custom_call" | custom-call | flops 1610612736 | bytes 2097152 | tf_op jit(solution)/shard_map/pallas_call | solution.py:105
  12.2 2.1 %shard_map.86._ = f32[2,256,256]{2,1,0:T(8,128)S(1)} custom-call(f32[8,256,256]{2,1,0:T(8,128)S(1)} %prepare.1.refs_0_.refs_1_.refs_2_.source.refs_3_, f32[2,256,256]{2,1,0:T(8,128)S(1)} %shard_map.85.refs_1_, f32[8,256,256]{2,1,0:T(8,128)S(1)} %prepare.1.refs_0_.refs_1_.refs_2_.source.refs_3_), custom_call_target="tpu_custom_call" | custom-call | flops 1610612736 | bytes 2097152 | tf_op jit(solution)/shard_map/pallas_call | solution.py:105
  14.5 8.5 %collective-permute-done.2.value = f32[2,256,256]{2,1,0:T(8,128)S(1)} collective-permute-done((f32[2,256,256]{2,1,0:T(8,128)S(1)}, f32[2,256,256]{2,1,0:T(8,128)S(1)}, u32[]{:S(2)}, u32[]{:S(2)}) %collective-permute-start.2) | collective-permute-done | bytes 524320 | tf_op jit(solution)/shard_map/ppermute | solution.py:529
  23.1 1.4 %weights.1 = (f32[5,256,256]{2,1,0:T(8,128)S(1)}, f32[5,256,256]{2,1,0:T(8,128)S(1)}) custom-call(s32[4]{0:T(128)S(1)} %copy-done.2, f32[4,256,256]{2,1,0:T(8,128)S(1)} %copy-done, f32[4,256,256]{2,1,0:T(8,128)S(1)} %copy-done.1, f32[2,256,256]{2,1,0:T(8,128)S(1)} %shard_map.86._), custom_call_target="tpu_custom_call" | custom-call | flops 1048576 | bytes 8388608 | tf_op jit(solution)/shard_map/weights/pallas_call | solution.py:339
  24.5 1.9 %shard_map.88 = (f32[256,256]{1,0:T(8,128)S(1)}, f32[256,256]{1,0:T(8,128)S(1)}) custom-call(f32[8,256,256]{2,1,0:T(8,128)S(1)} %prepare.1.refs_0_.refs_1_.refs_2_.source.refs_3_, f32[2,256,256]{2,1,0:T(8,128)S(1)} %shard_map.85.refs_1_, f32[2,256,256]{2,1,0:T(8,128)S(1)} %shard_map.87.refs_2_, f32[5,256,256]{2,1,0:T(8,128)S(1)} %get-tuple-element.25.refs_3_.refs_0_, ...), custom_call_target="tpu_custom_call" | custom-call | flops 1207959552 | bytes 2097152 | tf_op jit(solution)/shard_map/pallas_call | solution.py:105
  26.8 2.3 %shard_map.92.refs_2_ = f32[2,256,256]{2,1,0:T(8,128)S(1)} custom-call(f32[8,256,256]{2,1,0:T(8,128)S(1)} %prepare.1.refs_0_.refs_1_.refs_2_.source.refs_3_, f32[2,256,256]{2,1,0:T(8,128)S(1)} %shard_map.90.refs_2_.refs_1_, f32[2,256,256]{2,1,0:T(8,128)S(1)} %shard_map.87.refs_2_, f32[8,256,256]{2,1,0:T(8,128)S(1)} %prepare.1.refs_0_.refs_1_.refs_2_.source.refs_3_, ...), custom_call_target="tpu_custom_call" | custom-call | flops 1610612736 | bytes 2097152 | tf_op jit(solution)/shard_map/pallas_call | solution.py:105
  29.1 1.8 %shard_map.93 = (f32[2,256,256]{2,1,0:T(8,128)S(1)}, f32[2,256,256]{2,1,0:T(8,128)S(1)}) custom-call(f32[8,256,256]{2,1,0:T(8,128)S(1)} %prepare.1.refs_0_.refs_1_.refs_2_.source.refs_3_, f32[2,256,256]{2,1,0:T(8,128)S(1)} %shard_map.84.refs_1_, f32[2,256,256]{2,1,0:T(8,128)S(1)} %shard_map.92.refs_2_, f32[256,256]{1,0:T(8,128)S(1)} %get-tuple-element.29.refs_4_.refs_3_, ...), custom_call_target="tpu_custom_call" | custom-call | flops 1207959552 | bytes 2097152 | tf_op jit(solution)/shard_map/pallas_call | solution.py:105
  30.9 1.6 %collective-permute-start.4 = (f32[2,256,256]{2,1,0:T(8,128)S(1)}, f32[2,256,256]{2,1,0:T(8,128)S(1)}, u32[]{:S(2)}, u32[]{:S(2)}) collective-permute-start(f32[2,256,256]{2,1,0:T(8,128)S(1)} %get-tuple-element.31.real.refs_0_.refs_2_), channel_id=1, source_target_pairs={{0,4},{4,0},{8,12},{12,8},{16,20},{20,16},{24,28},{28,24},{1,5},{5... | collective-permute-start | bytes 1572872 | tf_op jit(solution)/shard_map/ppermute | solution.py:493
  32.5 3.5 %collective-permute-start.6 = (f32[2,256,256]{2,1,0:T(8,128)S(1)}, f32[2,256,256]{2,1,0:T(8,128)S(1)}, u32[]{:S(2)}, u32[]{:S(2)}) collective-permute-start(f32[2,256,256]{2,1,0:T(8,128)S(1)} %get-tuple-element.32.imag.refs_4_), channel_id=1, source_target_pairs={{8,16},{12,20},{16,8},{20,12},{9,17},{13,21},{17,9},{21,13},{10,18... | collective-permute-start | bytes 1572872 | tf_op jit(solution)/shard_map/ppermute | solution.py:493
  36.1 5.7 %collective-permute-done.4.partner.refs_1_.refs_3_ = f32[2,256,256]{2,1,0:T(8,128)S(1)} collective-permute-done((f32[2,256,256]{2,1,0:T(8,128)S(1)}, f32[2,256,256]{2,1,0:T(8,128)S(1)}, u32[]{:S(2)}, u32[]{:S(2)}) %collective-permute-start.4) | collective-permute-done | bytes 524320 | tf_op jit(solution)/shard_map/ppermute | solution.py:493
  41.8 3.7 %collective-permute-done.6.behind.refs_6_ = f32[2,256,256]{2,1,0:T(8,128)S(1)} collective-permute-done((f32[2,256,256]{2,1,0:T(8,128)S(1)}, f32[2,256,256]{2,1,0:T(8,128)S(1)}, u32[]{:S(2)}, u32[]{:S(2)}) %collective-permute-start.6) | collective-permute-done | bytes 524320 | tf_op jit(solution)/shard_map/ppermute | solution.py:493
  45.5 1.9 %collective-permute-done.5.ahead.refs_5_ = f32[2,256,256]{2,1,0:T(8,128)S(1)} collective-permute-done((f32[2,256,256]{2,1,0:T(8,128)S(1)}, f32[2,256,256]{2,1,0:T(8,128)S(1)}, u32[]{:S(2)}, u32[]{:S(2)}) %collective-permute-start.5) | collective-permute-done | bytes 524320 | tf_op jit(solution)/shard_map/ppermute | solution.py:493
  47.4 0.6 shard_map.94
  48.0 3.3 %collective-permute-start.12 = (f32[4,256,256]{2,1,0:T(8,128)S(1)}, f32[4,256,256]{2,1,0:T(8,128)S(1)}, u32[]{:S(2)}, u32[]{:S(2)}) collective-permute-start(f32[4,256,256]{2,1,0:T(8,128)S(1)} %get-tuple-element.40), channel_id=1, source_target_pairs={{0,1},{1,0},{2,3},{3,2},{4,5},{5,4},{6,7},{7,6},{8,9},{9,8},{10,11... | collective-permute-start | bytes 3145736 | tf_op jit(solution)/shard_map/ppermute | solution.py:490
  51.4 2.4 %collective-permute-start.7 = (f32[2,256,256]{2,1,0:T(8,128)S(1)}, f32[2,256,256]{2,1,0:T(8,128)S(1)}, u32[]{:S(2)}, u32[]{:S(2)}) collective-permute-start(f32[2,256,256]{2,1,0:T(8,128)S(1)} %shard_map.95), channel_id=1, source_target_pairs={{1,2},{2,1},{5,6},{6,5},{9,10},{10,9},{13,14},{14,13},{17,18},{18,... | collective-permute-start | bytes 1572872 | tf_op jit(solution)/shard_map/ppermute | solution.py:490
  53.8 3.2 %collective-permute-start.8 = (f32[2,256,256]{2,1,0:T(8,128)S(1)}, f32[2,256,256]{2,1,0:T(8,128)S(1)}, u32[]{:S(2)}, u32[]{:S(2)}) collective-permute-start(f32[2,256,256]{2,1,0:T(8,128)S(1)} %get-tuple-element.35), channel_id=1, source_target_pairs={{1,2},{2,1},{5,6},{6,5},{9,10},{10,9},{13,14},{14,13},{17,18},{18,... | collective-permute-start | bytes 1572872 | tf_op jit(solution)/shard_map/ppermute | solution.py:490
  57.0 4.9 %collective-permute-done.7.refs_9_ = f32[2,256,256]{2,1,0:T(8,128)S(1)} collective-permute-done((f32[2,256,256]{2,1,0:T(8,128)S(1)}, f32[2,256,256]{2,1,0:T(8,128)S(1)}, u32[]{:S(2)}, u32[]{:S(2)}) %collective-permute-start.7) | collective-permute-done | bytes 524320 | tf_op jit(solution)/shard_map/ppermute | solution.py:490
  61.9 5.6 %collective-permute-done.8.refs_10_ = f32[2,256,256]{2,1,0:T(8,128)S(1)} collective-permute-done((f32[2,256,256]{2,1,0:T(8,128)S(1)}, f32[2,256,256]{2,1,0:T(8,128)S(1)}, u32[]{:S(2)}, u32[]{:S(2)}) %collective-permute-start.8) | collective-permute-done | bytes 524320 | tf_op jit(solution)/shard_map/ppermute | solution.py:490
  67.5 0.5 shard_map.96
  68.1 2.4 %collective-permute-start.10 = (f32[1,256,256]{2,1,0:T(8,128)S(1)}, f32[1,256,256]{2,1,0:T(8,128)S(1)}, u32[]{:S(2)}, u32[]{:S(2)}) collective-permute-start(f32[1,256,256]{2,1,0:T(8,128)S(1)} %get-tuple-element.38), channel_id=1, source_target_pairs={{8,16},{12,20},{16,8},{20,12},{9,17},{13,21},{17,9},{21,13},{10,18... | collective-permute-start | bytes 786440 | tf_op jit(solution)/shard_map/ppermute | solution.py:493
  70.4 0.6 collective-permute-start.11
  71.0 0.5 shard_map.97
  71.9 3.2 %collective-permute-start.14 = (f32[1,256,256]{2,1,0:T(8,128)S(1)}, f32[1,256,256]{2,1,0:T(8,128)S(1)}, u32[]{:S(2)}, u32[]{:S(2)}) collective-permute-start(f32[1,256,256]{2,1,0:T(8,128)S(1)} %get-tuple-element.43), channel_id=1, source_target_pairs={{8,16},{12,20},{16,8},{20,12},{9,17},{13,21},{17,9},{21,13},{10,18... | collective-permute-start | bytes 786440 | tf_op jit(solution)/shard_map/ppermute | solution.py:493
  75.1 1.6 %collective-permute-start.15 = (f32[1,256,256]{2,1,0:T(8,128)S(1)}, f32[1,256,256]{2,1,0:T(8,128)S(1)}, u32[]{:S(2)}, u32[]{:S(2)}) collective-permute-start(f32[1,256,256]{2,1,0:T(8,128)S(1)} %get-tuple-element.44), channel_id=1, source_target_pairs={{0,4},{4,0},{8,12},{12,8},{16,20},{20,16},{24,28},{28,24},{1,5},{5... | collective-permute-start | bytes 786440 | tf_op jit(solution)/shard_map/ppermute | solution.py:493
  76.9 1.1 %collective-permute-done.13.refs_5_ = f32[1,256,256]{2,1,0:T(8,128)S(1)} collective-permute-done((f32[1,256,256]{2,1,0:T(8,128)S(1)}, f32[1,256,256]{2,1,0:T(8,128)S(1)}, u32[]{:S(2)}, u32[]{:S(2)}) %collective-permute-start.13) | collective-permute-done | bytes 262176 | tf_op jit(solution)/shard_map/ppermute | solution.py:493
  78.0 2.2 %collective-permute-done.14.refs_6_ = f32[1,256,256]{2,1,0:T(8,128)S(1)} collective-permute-done((f32[1,256,256]{2,1,0:T(8,128)S(1)}, f32[1,256,256]{2,1,0:T(8,128)S(1)}, u32[]{:S(2)}, u32[]{:S(2)}) %collective-permute-start.14) | collective-permute-done | bytes 262176 | tf_op jit(solution)/shard_map/ppermute | solution.py:493
  80.2 1.4 %collective-permute-done.15.refs_7_ = f32[1,256,256]{2,1,0:T(8,128)S(1)} collective-permute-done((f32[1,256,256]{2,1,0:T(8,128)S(1)}, f32[1,256,256]{2,1,0:T(8,128)S(1)}, u32[]{:S(2)}, u32[]{:S(2)}) %collective-permute-start.15) | collective-permute-done | bytes 262176 | tf_op jit(solution)/shard_map/ppermute | solution.py:493
  81.5 1.1 %shard_map.98 = f32[1,2,2,256,256]{4,3,2,1,0:T(8,128)} custom-call(f32[2,256,256]{2,1,0:T(8,128)S(1)} %get-tuple-element.36.refs_0_, f32[1,256,256]{2,1,0:T(8,128)S(1)} %collective-permute-done.9.refs_1_, f32[1,256,256]{2,1,0:T(8,128)S(1)} %collective-permute-done.10.refs_2_, f32[1,256,256]{2,1,0:T(8,128)S(1)} %collective-permute-done.11.refs_3_, ...), custom_call_target="tpu_custom_call" | custom-call | flops 100663296 | bytes 2097152 | tf_op jit(solution)/shard_map/pallas_call | solution.py:105
  (25 shorter events, 1.7 us)
Async XLA Ops:
  2.7 23.7 %collective-permute-start.1 = (f32[8,256,256]{2,1,0:T(8,128)S(1)}, f32[8,256,256]{2,1,0:T(8,128)S(1)}, u32[]{:S(2)}, u32[]{:S(2)}) collective-permute-start(f32[8,256,256]{2,1,0:T(8,128)S(1)} %prepare.1.refs_0_.refs_1_.refs_2_.source.refs_3_), channel_id=1, source_target_pairs={{0,1},{1,0},{2,3},{3,2},{4,5},{5,4},{6,7},{7,6},{8,9},{9,8},{10,11... | collective-permute-start | bytes 6291464 | tf_op jit(solution)/shard_map/ppermute | solution.py:490
  2.9 6.1 %collective-permute-start = (f32[2,256,256]{2,1,0:T(8,128)S(1)}, f32[2,256,256]{2,1,0:T(8,128)S(1)}, u32[]{:S(2)}, u32[]{:S(2)}) collective-permute-start(f32[2,256,256]{2,1,0:T(8,128)S(1)} %shard_map.83), channel_id=1, source_target_pairs={{0,1},{1,0},{2,3},{3,2},{4,5},{5,4},{6,7},{7,6},{8,9},{9,8},{10,11... | collective-permute-start | bytes 1572872 | tf_op jit(solution)/shard_map/ppermute | solution.py:490
  14.3 8.8 %copy-start = (f32[4,256,256]{2,1,0:T(8,128)S(1)}, f32[4,256,256]{2,1,0:T(8,128)}, u32[]{:S(2)}) copy-start(f32[4,256,256]{2,1,0:T(8,128)} %local_ref.1) | copy-start | bytes 3145732
  14.3 8.8 %copy-start.1 = (f32[4,256,256]{2,1,0:T(8,128)S(1)}, f32[4,256,256]{2,1,0:T(8,128)}, u32[]{:S(2)}) copy-start(f32[4,256,256]{2,1,0:T(8,128)} %side_ref.1) | copy-start | bytes 3145732
  14.3 8.8 %copy-start.2 = (s32[4]{0:T(128)S(1)}, s32[4]{0:T(128)}, u32[]{:S(2)}) copy-start(s32[4]{0:T(128)} %shift_ref.1) | copy-start | bytes 52
  14.3 8.7 %collective-permute-start.2 = (f32[2,256,256]{2,1,0:T(8,128)S(1)}, f32[2,256,256]{2,1,0:T(8,128)S(1)}, u32[]{:S(2)}, u32[]{:S(2)}) collective-permute-start(f32[2,256,256]{2,1,0:T(8,128)S(1)} %shard_map.86._), channel_id=1, source_target_pairs={{1,2},{2,1},{0,4},{3,7},{5,6},{6,5},{4,0},{7,3},{9,10},{10,9},{8,1... | collective-permute-start | bytes 1572872 | tf_op jit(solution)/shard_map/ppermute | solution.py:529
  23.0 3.4 %collective-permute-start.3 = (f32[2,256,256]{2,1,0:T(8,128)S(1)}, f32[2,256,256]{2,1,0:T(8,128)S(1)}, u32[]{:S(2)}, u32[]{:S(2)}) collective-permute-start(f32[2,256,256]{2,1,0:T(8,128)S(1)} %shard_map.87.refs_2_), channel_id=1, source_target_pairs={{0,1},{1,0},{2,3},{3,2},{4,5},{5,4},{6,7},{7,6},{8,9},{9,8},{10,11... | collective-permute-start | bytes 1572872 | tf_op jit(solution)/shard_map/ppermute | solution.py:490
  30.9 10.9 %collective-permute-start.4 = (f32[2,256,256]{2,1,0:T(8,128)S(1)}, f32[2,256,256]{2,1,0:T(8,128)S(1)}, u32[]{:S(2)}, u32[]{:S(2)}) collective-permute-start(f32[2,256,256]{2,1,0:T(8,128)S(1)} %get-tuple-element.31.real.refs_0_.refs_2_), channel_id=1, source_target_pairs={{0,4},{4,0},{8,12},{12,8},{16,20},{20,16},{24,28},{28,24},{1,5},{5... | collective-permute-start | bytes 1572872 | tf_op jit(solution)/shard_map/ppermute | solution.py:493
  32.5 13.0 %collective-permute-start.6 = (f32[2,256,256]{2,1,0:T(8,128)S(1)}, f32[2,256,256]{2,1,0:T(8,128)S(1)}, u32[]{:S(2)}, u32[]{:S(2)}) collective-permute-start(f32[2,256,256]{2,1,0:T(8,128)S(1)} %get-tuple-element.32.imag.refs_4_), channel_id=1, source_target_pairs={{8,16},{12,20},{16,8},{20,12},{9,17},{13,21},{17,9},{21,13},{10,18... | collective-permute-start | bytes 1572872 | tf_op jit(solution)/shard_map/ppermute | solution.py:493
  36.0 11.4 %collective-permute-start.5 = (f32[2,256,256]{2,1,0:T(8,128)S(1)}, f32[2,256,256]{2,1,0:T(8,128)S(1)}, u32[]{:S(2)}, u32[]{:S(2)}) collective-permute-start(f32[2,256,256]{2,1,0:T(8,128)S(1)} %get-tuple-element.32.imag.refs_4_), channel_id=1, source_target_pairs={{0,8},{4,12},{8,0},{12,4},{16,24},{20,28},{24,16},{28,20},{1,9},{5... | collective-permute-start | bytes 1572872 | tf_op jit(solution)/shard_map/ppermute | solution.py:493
  48.0 23.0 %collective-permute-start.12 = (f32[4,256,256]{2,1,0:T(8,128)S(1)}, f32[4,256,256]{2,1,0:T(8,128)S(1)}, u32[]{:S(2)}, u32[]{:S(2)}) collective-permute-start(f32[4,256,256]{2,1,0:T(8,128)S(1)} %get-tuple-element.40), channel_id=1, source_target_pairs={{0,1},{1,0},{2,3},{3,2},{4,5},{5,4},{6,7},{7,6},{8,9},{9,8},{10,11... | collective-permute-start | bytes 3145736 | tf_op jit(solution)/shard_map/ppermute | solution.py:490
  51.4 10.5 %collective-permute-start.7 = (f32[2,256,256]{2,1,0:T(8,128)S(1)}, f32[2,256,256]{2,1,0:T(8,128)S(1)}, u32[]{:S(2)}, u32[]{:S(2)}) collective-permute-start(f32[2,256,256]{2,1,0:T(8,128)S(1)} %shard_map.95), channel_id=1, source_target_pairs={{1,2},{2,1},{5,6},{6,5},{9,10},{10,9},{13,14},{14,13},{17,18},{18,... | collective-permute-start | bytes 1572872 | tf_op jit(solution)/shard_map/ppermute | solution.py:490
  53.8 13.7 %collective-permute-start.8 = (f32[2,256,256]{2,1,0:T(8,128)S(1)}, f32[2,256,256]{2,1,0:T(8,128)S(1)}, u32[]{:S(2)}, u32[]{:S(2)}) collective-permute-start(f32[2,256,256]{2,1,0:T(8,128)S(1)} %get-tuple-element.35), channel_id=1, source_target_pairs={{1,2},{2,1},{5,6},{6,5},{9,10},{10,9},{13,14},{14,13},{17,18},{18,... | collective-permute-start | bytes 1572872 | tf_op jit(solution)/shard_map/ppermute | solution.py:490
  68.0 7.1 %collective-permute-start.9 = (f32[1,256,256]{2,1,0:T(8,128)S(1)}, f32[1,256,256]{2,1,0:T(8,128)S(1)}, u32[]{:S(2)}, u32[]{:S(2)}) collective-permute-start(f32[1,256,256]{2,1,0:T(8,128)S(1)} %get-tuple-element.37), channel_id=1, source_target_pairs={{0,8},{4,12},{8,0},{12,4},{16,24},{20,28},{24,16},{28,20},{1,9},{5... | collective-permute-start | bytes 786440 | tf_op jit(solution)/shard_map/ppermute | solution.py:493
  68.1 8.6 %collective-permute-start.10 = (f32[1,256,256]{2,1,0:T(8,128)S(1)}, f32[1,256,256]{2,1,0:T(8,128)S(1)}, u32[]{:S(2)}, u32[]{:S(2)}) collective-permute-start(f32[1,256,256]{2,1,0:T(8,128)S(1)} %get-tuple-element.38), channel_id=1, source_target_pairs={{8,16},{12,20},{16,8},{20,12},{9,17},{13,21},{17,9},{21,13},{10,18... | collective-permute-start | bytes 786440 | tf_op jit(solution)/shard_map/ppermute | solution.py:493
  70.4 6.4 %collective-permute-start.11 = (f32[1,256,256]{2,1,0:T(8,128)S(1)}, f32[1,256,256]{2,1,0:T(8,128)S(1)}, u32[]{:S(2)}, u32[]{:S(2)}) collective-permute-start(f32[1,256,256]{2,1,0:T(8,128)S(1)} %get-tuple-element.39), channel_id=1, source_target_pairs={{0,4},{4,0},{8,12},{12,8},{16,20},{20,16},{24,28},{28,24},{1,5},{5... | collective-permute-start | bytes 786440 | tf_op jit(solution)/shard_map/ppermute | solution.py:493
  71.5 6.4 %collective-permute-start.13 = (f32[1,256,256]{2,1,0:T(8,128)S(1)}, f32[1,256,256]{2,1,0:T(8,128)S(1)}, u32[]{:S(2)}, u32[]{:S(2)}) collective-permute-start(f32[1,256,256]{2,1,0:T(8,128)S(1)} %get-tuple-element.42), channel_id=1, source_target_pairs={{0,8},{4,12},{8,0},{12,4},{16,24},{20,28},{24,16},{28,20},{1,9},{5... | collective-permute-start | bytes 786440 | tf_op jit(solution)/shard_map/ppermute | solution.py:493
  71.9 8.3 %collective-permute-start.14 = (f32[1,256,256]{2,1,0:T(8,128)S(1)}, f32[1,256,256]{2,1,0:T(8,128)S(1)}, u32[]{:S(2)}, u32[]{:S(2)}) collective-permute-start(f32[1,256,256]{2,1,0:T(8,128)S(1)} %get-tuple-element.43), channel_id=1, source_target_pairs={{8,16},{12,20},{16,8},{20,12},{9,17},{13,21},{17,9},{21,13},{10,18... | collective-permute-start | bytes 786440 | tf_op jit(solution)/shard_map/ppermute | solution.py:493
  75.1 6.4 %collective-permute-start.15 = (f32[1,256,256]{2,1,0:T(8,128)S(1)}, f32[1,256,256]{2,1,0:T(8,128)S(1)}, u32[]{:S(2)}, u32[]{:S(2)}) collective-permute-start(f32[1,256,256]{2,1,0:T(8,128)S(1)} %get-tuple-element.44), channel_id=1, source_target_pairs={{0,4},{4,0},{8,12},{12,8},{16,20},{20,16},{24,28},{28,24},{1,5},{5... | collective-permute-start | bytes 786440 | tf_op jit(solution)/shard_map/ppermute | solution.py:493

commit v4 on v3

--- a/solution.py
+++ b/solution.py
@@ -452,25 +452,47 @@
     )
 
 
-def finish(sections, early, late):
-    blocks, dimension = 1 + late[1].shape[0], late[1].shape[-1]
+def finish(sections, blocks, group, early, written):
+    own, dimension = group[0], group[0].shape[-1]
     last = blocks - 1
-
-    def body(*refs):
-        out = refs[-1]
+    count = own.shape[0] // 2
+
+    def body(own, from_first, from_second, from_partner, *rest):
+        out, total, sems = rest[-3:]
         right_half = half_of(sections)
         outer = is_at(0, sections)
-        for number, group in enumerate((refs[:4], refs[4:8])):
-            own, from_first, from_second, from_partner = group
-            for k in range(1 if number == 0 else last):
-                low, high = (0, last) if number == 0 else (k + 1, k)
-                index = jnp.where(outer, low, high)
-                place = jnp.where(right_half, last - index, index)
-                out[0, place, 0] = own[2 * k] + (from_first[k] + from_second[k])
-                out[0, place, 1] = own[2 * k + 1] + from_partner[k]
-
-    shape = jax.ShapeDtypeStruct((1, blocks, 2, dimension, dimension), F32)
-    return call(body, shape, list(early) + list(late), 1)
+        copies = []
+        for k in range(count):
+            low, high = (0, last) if early else (k + 1, k)
+            index = jnp.where(outer, low, high)
+            place = jnp.where(right_half, last - index, index)
+            for part in (1, 0):
+                slot = 2 * k + part
+                if part:
+                    total[slot] = own[slot] + from_partner[k]
+                else:
+                    total[slot] = own[slot] + (from_first[k] + from_second[k])
+                copies.append(
+                    pltpu.make_async_copy(total.at[slot], out.at[0, place, part], sems.at[slot])
+                )
+                copies[-1].start()
+        for copy in copies:
+            copy.wait()
+
+    outside = pl.BlockSpec(memory_space=pltpu.HBM)
+    before = [] if written is None else [written]
+    return pl.pallas_call(
+        body,
+        out_shape=jax.ShapeDtypeStruct((1, blocks, 2, dimension, dimension), F32),
+        in_specs=[VMEM] * 4 + [outside] * len(before),
+        out_specs=outside,
+        scratch_shapes=[
+            pltpu.VMEM((2 * count, dimension, dimension), F32),
+            pltpu.SemaphoreType.DMA((2 * count,)),
+        ],
+        input_output_aliases={4: 0} if before else {},
+        compiler_params=pltpu.CompilerParams(vmem_limit_bytes=12 << 20),
+    )(*group, *before)
 
 
 def step(
@@ -560,7 +582,7 @@
     partner = over_energy(real, swap)
     ahead = over_energy(imag, first_swap)
     behind = over_energy(imag, second_swap)
-    middle_real = over_section(last_blocks(real, partner), across)
+    middle_real = lax.ppermute(last_blocks(real, partner), ("energy", "section"), crossing)
 
     side_partner, side_own, middle, shared = side_terms(
         sections, side_weight, real, partner, imag, ahead, behind
@@ -590,7 +612,8 @@
     early = exchange(*early)
     late = combine(sections, tables | {"shared": shared}, False)
     late = exchange(*late)
-    return finish(sections, early, late)
+    result = finish(sections, blocks, early, True, None)
+    return finish(sections, blocks, late, False, result)
 
 
 def solution(mesh):

time: 82.9 us -> 83.2 us (level)
  the two profiles are of different devices: /device:TPU:10 before, /device:TPU:17 now
where the time goes in v4:
time: 83.2 us; the launch traced here: 83 us
  waiting for transfers between devices  35.8 us (43%)
  starting transfers between devices  27.4 us (33%)
  Pallas kernels  18.8 us (23%)
  between operations  1.11 us (1%)
    ppermute x9, waiting for transfers between devices, over_energy(): return lax.ppermute(value, 'energy', route)  16.3 us
    ppermute x5, starting transfers between devices, over_section(): return lax.ppermute(value, 'section', route)  14.2 us
    pallas_call x16, Pallas kernels, call(): pl.pallas_call(body, out_shape=out_shape, in_specs=[VMEM] * len(operands)...  13.7 us
    ppermute x9, starting transfers between devices, over_energy(): return lax.ppermute(value, 'energy', route)  10.2 us
    ppermute x5, waiting for transfers between devices, over_section(): return lax.ppermute(value, 'section', route)  7.26 us
    ppermute x1, waiting for transfers between devices, step(): sigma = lax.ppermute(sigma, ('energy', 'section'), crossing)  7.01 us
    ppermute x1, waiting for transfers between devices, step(): lax.ppermute(last_blocks(real, partner), ('energy', 'section'), crossing)  5.16 us
    pallas_call x1, Pallas kernels, prepare(): pl.pallas_call(functools.partial(prepare_kernel, sections, spread), out_s...  2.07 us
  transfers between devices with their start and end apart: 16, of which 9 were waited for; matrix products, arithmetic and copies ran while one was open for 0% of the time, Pallas kernels for 13%

profile of v4, /device:TPU:17, one launch (start us, length us, event | category | flops | bytes accessed | tf_op | source)
XLA Modules:
  0.0 83.0 jit_solution(6172635288753572855)
XLA Ops:
  0.7 2.1 %prepare.1.refs_0_.refs_1_.refs_2_.source.refs_3_ = f32[8,256,256]{2,1,0:T(8,128)S(1)} custom-call(f32[1,1]{1,0:T(1,128)} %bitcast.1.broadening, f32[2,256]{1,0:T(2,128)} %onsite.1, f32[2,256,256]{2,1,0:T(8,128)} %hopping.1, f32[2,256,256]{2,1,0:T(8,128)} %coupling.1, f32[1,2,2,256,256]{4,3,2,1,0:T(8,128)} %born.1), custom_call_target="tpu_custom_call" | custom-call | tf_op jit(solution)/shard_map/prepare/pallas_call | solution.py:290
  2.7 0.7 collective-permute-start.1
  3.6 4.5 %collective-permute-start = (f32[2,256,256]{2,1,0:T(8,128)S(1)}, f32[2,256,256]{2,1,0:T(8,128)S(1)}, u32[]{:S(2)}, u32[]{:S(2)}) collective-permute-start(f32[2,256,256]{2,1,0:T(8,128)S(1)} %shard_map.83), channel_id=1, source_target_pairs={{0,1},{1,0},{2,3},{3,2},{4,5},{5,4},{6,7},{7,6},{8,9},{9,8},{10,11... | collective-permute-start | bytes 1572872 | tf_op jit(solution)/shard_map/ppermute | solution.py:512
  8.1 1.5 %collective-permute-done.value = f32[2,256,256]{2,1,0:T(8,128)S(1)} collective-permute-done((f32[2,256,256]{2,1,0:T(8,128)S(1)}, f32[2,256,256]{2,1,0:T(8,128)S(1)}, u32[]{:S(2)}, u32[]{:S(2)}) %collective-permute-start) | collective-permute-done | bytes 524320 | tf_op jit(solution)/shard_map/ppermute | solution.py:512
  9.7 2.2 %shard_map.85.refs_1_ = f32[2,256,256]{2,1,0:T(8,128)S(1)} custom-call(f32[8,256,256]{2,1,0:T(8,128)S(1)} %prepare.1.refs_0_.refs_1_.refs_2_.source.refs_3_, f32[2,256,256]{2,1,0:T(8,128)S(1)} %shard_map.84.refs_1_, f32[8,256,256]{2,1,0:T(8,128)S(1)} %prepare.1.refs_0_.refs_1_.refs_2_.source.refs_3_), custom_call_target="tpu_custom_call" | custom-call | flops 1610612736 | bytes 2097152 | tf_op jit(solution)/shard_map/pallas_call | solution.py:105
  11.9 2.5 %shard_map.86._ = f32[2,256,256]{2,1,0:T(8,128)S(1)} custom-call(f32[8,256,256]{2,1,0:T(8,128)S(1)} %prepare.1.refs_0_.refs_1_.refs_2_.source.refs_3_, f32[2,256,256]{2,1,0:T(8,128)S(1)} %shard_map.85.refs_1_, f32[8,256,256]{2,1,0:T(8,128)S(1)} %prepare.1.refs_0_.refs_1_.refs_2_.source.refs_3_), custom_call_target="tpu_custom_call" | custom-call | flops 1610612736 | bytes 2097152 | tf_op jit(solution)/shard_map/pallas_call | solution.py:105
  14.5 1.7 %collective-permute-start.2 = (f32[2,256,256]{2,1,0:T(8,128)S(1)}, f32[2,256,256]{2,1,0:T(8,128)S(1)}, u32[]{:S(2)}, u32[]{:S(2)}) collective-permute-start(f32[2,256,256]{2,1,0:T(8,128)S(1)} %shard_map.86._), channel_id=1, source_target_pairs={{1,2},{2,1},{0,4},{3,7},{5,6},{6,5},{4,0},{7,3},{9,10},{10,9},{8,1... | collective-permute-start | bytes 1572872 | tf_op jit(solution)/shard_map/ppermute | solution.py:551
  16.1 7.0 %collective-permute-done.2.value = f32[2,256,256]{2,1,0:T(8,128)S(1)} collective-permute-done((f32[2,256,256]{2,1,0:T(8,128)S(1)}, f32[2,256,256]{2,1,0:T(8,128)S(1)}, u32[]{:S(2)}, u32[]{:S(2)}) %collective-permute-start.2) | collective-permute-done | bytes 524320 | tf_op jit(solution)/shard_map/ppermute | solution.py:551
  23.1 0.8 shard_map.87.refs_2_
  24.1 1.4 %weights.1 = (f32[5,256,256]{2,1,0:T(8,128)S(1)}, f32[5,256,256]{2,1,0:T(8,128)S(1)}) custom-call(s32[4]{0:T(128)S(1)} %copy-done.2, f32[4,256,256]{2,1,0:T(8,128)S(1)} %copy-done, f32[4,256,256]{2,1,0:T(8,128)S(1)} %copy-done.1, f32[2,256,256]{2,1,0:T(8,128)S(1)} %shard_map.86._), custom_call_target="tpu_custom_call" | custom-call | flops 1048576 | bytes 8388608 | tf_op jit(solution)/shard_map/weights/pallas_call | solution.py:339
  25.5 1.9 %shard_map.88 = (f32[256,256]{1,0:T(8,128)S(1)}, f32[256,256]{1,0:T(8,128)S(1)}) custom-call(f32[8,256,256]{2,1,0:T(8,128)S(1)} %prepare.1.refs_0_.refs_1_.refs_2_.source.refs_3_, f32[2,256,256]{2,1,0:T(8,128)S(1)} %shard_map.85.refs_1_, f32[2,256,256]{2,1,0:T(8,128)S(1)} %shard_map.87.refs_2_, f32[5,256,256]{2,1,0:T(8,128)S(1)} %get-tuple-element.25.refs_3_.refs_0_, ...), custom_call_target="tpu_custom_call" | custom-call | flops 1207959552 | bytes 2097152 | tf_op jit(solution)/shard_map/pallas_call | solution.py:105
  27.8 2.3 %shard_map.92.refs_2_ = f32[2,256,256]{2,1,0:T(8,128)S(1)} custom-call(f32[8,256,256]{2,1,0:T(8,128)S(1)} %prepare.1.refs_0_.refs_1_.refs_2_.source.refs_3_, f32[2,256,256]{2,1,0:T(8,128)S(1)} %shard_map.90.refs_2_.refs_1_, f32[2,256,256]{2,1,0:T(8,128)S(1)} %shard_map.87.refs_2_, f32[8,256,256]{2,1,0:T(8,128)S(1)} %prepare.1.refs_0_.refs_1_.refs_2_.source.refs_3_, ...), custom_call_target="tpu_custom_call" | custom-call | flops 1610612736 | bytes 2097152 | tf_op jit(solution)/shard_map/pallas_call | solution.py:105
  30.1 1.8 %shard_map.93 = (f32[2,256,256]{2,1,0:T(8,128)S(1)}, f32[2,256,256]{2,1,0:T(8,128)S(1)}) custom-call(f32[8,256,256]{2,1,0:T(8,128)S(1)} %prepare.1.refs_0_.refs_1_.refs_2_.source.refs_3_, f32[2,256,256]{2,1,0:T(8,128)S(1)} %shard_map.84.refs_1_, f32[2,256,256]{2,1,0:T(8,128)S(1)} %shard_map.92.refs_2_, f32[256,256]{1,0:T(8,128)S(1)} %get-tuple-element.29.refs_4_.refs_3_, ...), custom_call_target="tpu_custom_call" | custom-call | flops 1207959552 | bytes 2097152 | tf_op jit(solution)/shard_map/pallas_call | solution.py:105
  31.9 1.3 %collective-permute-start.4 = (f32[2,256,256]{2,1,0:T(8,128)S(1)}, f32[2,256,256]{2,1,0:T(8,128)S(1)}, u32[]{:S(2)}, u32[]{:S(2)}) collective-permute-start(f32[2,256,256]{2,1,0:T(8,128)S(1)} %get-tuple-element.31.real.refs_2_.refs_0_), channel_id=1, source_target_pairs={{0,4},{4,0},{8,12},{12,8},{16,20},{20,16},{24,28},{28,24},{1,5},{5... | collective-permute-start | bytes 1572872 | tf_op jit(solution)/shard_map/ppermute | solution.py:515
  33.2 1.3 %collective-permute-start.5 = (f32[2,256,256]{2,1,0:T(8,128)S(1)}, f32[2,256,256]{2,1,0:T(8,128)S(1)}, u32[]{:S(2)}, u32[]{:S(2)}) collective-permute-start(f32[2,256,256]{2,1,0:T(8,128)S(1)} %get-tuple-element.32.imag.refs_4_), channel_id=1, source_target_pairs={{0,8},{4,12},{8,0},{12,4},{16,24},{20,28},{24,16},{28,20},{1,9},{5... | collective-permute-start | bytes 1572872 | tf_op jit(solution)/shard_map/ppermute | solution.py:515
  34.5 1.9 %collective-permute-start.6 = (f32[2,256,256]{2,1,0:T(8,128)S(1)}, f32[2,256,256]{2,1,0:T(8,128)S(1)}, u32[]{:S(2)}, u32[]{:S(2)}) collective-permute-start(f32[2,256,256]{2,1,0:T(8,128)S(1)} %get-tuple-element.32.imag.refs_4_), channel_id=1, source_target_pairs={{8,16},{12,20},{16,8},{20,12},{9,17},{13,21},{17,9},{21,13},{10,18... | collective-permute-start | bytes 1572872 | tf_op jit(solution)/shard_map/ppermute | solution.py:515
  36.4 4.1 %collective-permute-done.4.partner.refs_3_.refs_1_ = f32[2,256,256]{2,1,0:T(8,128)S(1)} collective-permute-done((f32[2,256,256]{2,1,0:T(8,128)S(1)}, f32[2,256,256]{2,1,0:T(8,128)S(1)}, u32[]{:S(2)}, u32[]{:S(2)}) %collective-permute-start.4) | collective-permute-done | bytes 524320 | tf_op jit(solution)/shard_map/ppermute | solution.py:515
  40.5 1.0 %collective-permute-done.5.ahead.refs_5_ = f32[2,256,256]{2,1,0:T(8,128)S(1)} collective-permute-done((f32[2,256,256]{2,1,0:T(8,128)S(1)}, f32[2,256,256]{2,1,0:T(8,128)S(1)}, u32[]{:S(2)}, u32[]{:S(2)}) %collective-permute-start.5) | collective-permute-done | bytes 524320 | tf_op jit(solution)/shard_map/ppermute | solution.py:515
  41.5 3.2 %collective-permute-done.6.behind.refs_6_ = f32[2,256,256]{2,1,0:T(8,128)S(1)} collective-permute-done((f32[2,256,256]{2,1,0:T(8,128)S(1)}, f32[2,256,256]{2,1,0:T(8,128)S(1)}, u32[]{:S(2)}, u32[]{:S(2)}) %collective-permute-start.6) | collective-permute-done | bytes 524320 | tf_op jit(solution)/shard_map/ppermute | solution.py:515
  44.7 0.6 shard_map.94
  45.3 6.4 %collective-permute-start.7 = (f32[4,256,256]{2,1,0:T(8,128)S(1)}, f32[4,256,256]{2,1,0:T(8,128)S(1)}, u32[]{:S(2)}, u32[]{:S(2)}) collective-permute-start(f32[4,256,256]{2,1,0:T(8,128)S(1)} %get-tuple-element.35), channel_id=1, source_target_pairs={{0,1},{1,0},{2,3},{3,2},{4,5},{5,4},{6,7},{7,6},{8,9},{9,8},{10,11... | collective-permute-start | bytes 3145736 | tf_op jit(solution)/shard_map/ppermute | solution.py:512
  51.8 1.3 %collective-permute-start.11 = (f32[2,256,256]{2,1,0:T(8,128)S(1)}, f32[2,256,256]{2,1,0:T(8,128)S(1)}, u32[]{:S(2)}, u32[]{:S(2)}) collective-permute-start(f32[2,256,256]{2,1,0:T(8,128)S(1)} %shard_map.96), channel_id=1, source_target_pairs={{1,2},{2,1},{0,4},{3,7},{5,6},{6,5},{4,0},{7,3},{9,10},{10,9},{8,1... | collective-permute-start | bytes 1572872 | tf_op jit(solution)/shard_map/ppermute | solution.py:585
  53.1 2.4 %collective-permute-start.12 = (f32[2,256,256]{2,1,0:T(8,128)S(1)}, f32[2,256,256]{2,1,0:T(8,128)S(1)}, u32[]{:S(2)}, u32[]{:S(2)}) collective-permute-start(f32[2,256,256]{2,1,0:T(8,128)S(1)} %get-tuple-element.40), channel_id=1, source_target_pairs={{1,2},{2,1},{5,6},{6,5},{9,10},{10,9},{13,14},{14,13},{17,18},{18,... | collective-permute-start | bytes 1572872 | tf_op jit(solution)/shard_map/ppermute | solution.py:512
  55.5 5.2 %collective-permute-done.11.refs_9_ = f32[2,256,256]{2,1,0:T(8,128)S(1)} collective-permute-done((f32[2,256,256]{2,1,0:T(8,128)S(1)}, f32[2,256,256]{2,1,0:T(8,128)S(1)}, u32[]{:S(2)}, u32[]{:S(2)}) %collective-permute-start.11) | collective-permute-done | bytes 524320 | tf_op jit(solution)/shard_map/ppermute | solution.py:585
  60.7 5.7 %collective-permute-done.12.refs_10_ = f32[2,256,256]{2,1,0:T(8,128)S(1)} collective-permute-done((f32[2,256,256]{2,1,0:T(8,128)S(1)}, f32[2,256,256]{2,1,0:T(8,128)S(1)}, u32[]{:S(2)}, u32[]{:S(2)}) %collective-permute-start.12) | collective-permute-done | bytes 524320 | tf_op jit(solution)/shard_map/ppermute | solution.py:512
  67.0 1.9 %collective-permute-start.14 = (f32[1,256,256]{2,1,0:T(8,128)S(1)}, f32[1,256,256]{2,1,0:T(8,128)S(1)}, u32[]{:S(2)}, u32[]{:S(2)}) collective-permute-start(f32[1,256,256]{2,1,0:T(8,128)S(1)} %get-tuple-element.43), channel_id=1, source_target_pairs={{8,16},{12,20},{16,8},{20,12},{9,17},{13,21},{17,9},{21,13},{10,18... | collective-permute-start | bytes 786440 | tf_op jit(solution)/shard_map/ppermute | solution.py:515
  69.7 1.3 %collective-permute-start.10 = (f32[1,256,256]{2,1,0:T(8,128)S(1)}, f32[1,256,256]{2,1,0:T(8,128)S(1)}, u32[]{:S(2)}, u32[]{:S(2)}) collective-permute-start(f32[1,256,256]{2,1,0:T(8,128)S(1)} %get-tuple-element.39), channel_id=1, source_target_pairs={{0,4},{4,0},{8,12},{12,8},{16,20},{20,16},{24,28},{28,24},{1,5},{5... | collective-permute-start | bytes 786440 | tf_op jit(solution)/shard_map/ppermute | solution.py:515
  71.2 3.7 %collective-permute-done.13.from_first = f32[1,256,256]{2,1,0:T(8,128)S(1)} collective-permute-done((f32[1,256,256]{2,1,0:T(8,128)S(1)}, f32[1,256,256]{2,1,0:T(8,128)S(1)}, u32[]{:S(2)}, u32[]{:S(2)}) %collective-permute-start.13) | collective-permute-done | bytes 262176 | tf_op jit(solution)/shard_map/ppermute | solution.py:515
  74.9 1.9 %collective-permute-start.9 = (f32[1,256,256]{2,1,0:T(8,128)S(1)}, f32[1,256,256]{2,1,0:T(8,128)S(1)}, u32[]{:S(2)}, u32[]{:S(2)}) collective-permute-start(f32[1,256,256]{2,1,0:T(8,128)S(1)} %get-tuple-element.38), channel_id=1, source_target_pairs={{8,16},{12,20},{16,8},{20,12},{9,17},{13,21},{17,9},{21,13},{10,18... | collective-permute-start | bytes 786440 | tf_op jit(solution)/shard_map/ppermute | solution.py:515
  76.8 0.8 %shard_map.98.rest_0_ = f32[1,2,2,256,256]{4,3,2,1,0:T(8,128)} custom-call(f32[2,256,256]{2,1,0:T(8,128)S(1)} %get-tuple-element.41.own, f32[1,256,256]{2,1,0:T(8,128)S(1)} %collective-permute-done.13.from_first, f32[1,256,256]{2,1,0:T(8,128)S(1)} %collective-permute-done.14.from_second, f32[1,256,256]{2,1,0:T(8,128)S(1)} %collective-permute-done.15.from_partner), custom_call_target="tpu_custom_call" | custom-call | tf_op jit(solution)/shard_map/pallas_call | solution.py:484
  77.7 4.3 %collective-permute-done.9.from_second = f32[1,256,256]{2,1,0:T(8,128)S(1)} collective-permute-done((f32[1,256,256]{2,1,0:T(8,128)S(1)}, f32[1,256,256]{2,1,0:T(8,128)S(1)}, u32[]{:S(2)}, u32[]{:S(2)}) %collective-permute-start.9) | collective-permute-done | bytes 262176 | tf_op jit(solution)/shard_map/ppermute | solution.py:515
  82.0 0.8 %shard_map.99 = f32[1,2,2,256,256]{4,3,2,1,0:T(8,128)} custom-call(f32[2,256,256]{2,1,0:T(8,128)S(1)} %get-tuple-element.36.own, f32[1,256,256]{2,1,0:T(8,128)S(1)} %collective-permute-done.8.from_first, f32[1,256,256]{2,1,0:T(8,128)S(1)} %collective-permute-done.9.from_second, ...), custom_call_target="tpu_custom_call", output_to_operand_aliasing={{}: (4, {})} | custom-call | tf_op jit(solution)/shard_map/pallas_call | solution.py:484
  (26 shorter events, 2.2 us)
Async XLA Ops:
  2.7 24.6 %collective-permute-start.1 = (f32[8,256,256]{2,1,0:T(8,128)S(1)}, f32[8,256,256]{2,1,0:T(8,128)S(1)}, u32[]{:S(2)}, u32[]{:S(2)}) collective-permute-start(f32[8,256,256]{2,1,0:T(8,128)S(1)} %prepare.1.refs_0_.refs_1_.refs_2_.source.refs_3_), channel_id=1, source_target_pairs={{0,1},{1,0},{2,3},{3,2},{4,5},{5,4},{6,7},{7,6},{8,9},{9,8},{10,11... | collective-permute-start | bytes 6291464 | tf_op jit(solution)/shard_map/ppermute | solution.py:512
  3.6 6.1 %collective-permute-start = (f32[2,256,256]{2,1,0:T(8,128)S(1)}, f32[2,256,256]{2,1,0:T(8,128)S(1)}, u32[]{:S(2)}, u32[]{:S(2)}) collective-permute-start(f32[2,256,256]{2,1,0:T(8,128)S(1)} %shard_map.83), channel_id=1, source_target_pairs={{0,1},{1,0},{2,3},{3,2},{4,5},{5,4},{6,7},{7,6},{8,9},{9,8},{10,11... | collective-permute-start | bytes 1572872 | tf_op jit(solution)/shard_map/ppermute | solution.py:512
  14.4 9.6 %copy-start = (f32[4,256,256]{2,1,0:T(8,128)S(1)}, f32[4,256,256]{2,1,0:T(8,128)}, u32[]{:S(2)}) copy-start(f32[4,256,256]{2,1,0:T(8,128)} %local_ref.1) | copy-start | bytes 3145732
  14.5 9.6 %copy-start.1 = (f32[4,256,256]{2,1,0:T(8,128)S(1)}, f32[4,256,256]{2,1,0:T(8,128)}, u32[]{:S(2)}) copy-start(f32[4,256,256]{2,1,0:T(8,128)} %side_ref.1) | copy-start | bytes 3145732
  14.5 9.6 %copy-start.2 = (s32[4]{0:T(128)S(1)}, s32[4]{0:T(128)}, u32[]{:S(2)}) copy-start(s32[4]{0:T(128)} %shift_ref.1) | copy-start | bytes 52
  14.5 8.7 %collective-permute-start.2 = (f32[2,256,256]{2,1,0:T(8,128)S(1)}, f32[2,256,256]{2,1,0:T(8,128)S(1)}, u32[]{:S(2)}, u32[]{:S(2)}) collective-permute-start(f32[2,256,256]{2,1,0:T(8,128)S(1)} %shard_map.86._), channel_id=1, source_target_pairs={{1,2},{2,1},{0,4},{3,7},{5,6},{6,5},{4,0},{7,3},{9,10},{10,9},{8,1... | collective-permute-start | bytes 1572872 | tf_op jit(solution)/shard_map/ppermute | solution.py:551
  24.0 3.4 %collective-permute-start.3 = (f32[2,256,256]{2,1,0:T(8,128)S(1)}, f32[2,256,256]{2,1,0:T(8,128)S(1)}, u32[]{:S(2)}, u32[]{:S(2)}) collective-permute-start(f32[2,256,256]{2,1,0:T(8,128)S(1)} %shard_map.87.refs_2_), channel_id=1, source_target_pairs={{0,1},{1,0},{2,3},{3,2},{4,5},{5,4},{6,7},{7,6},{8,9},{9,8},{10,11... | collective-permute-start | bytes 1572872 | tf_op jit(solution)/shard_map/ppermute | solution.py:512
  31.9 8.6 %collective-permute-start.4 = (f32[2,256,256]{2,1,0:T(8,128)S(1)}, f32[2,256,256]{2,1,0:T(8,128)S(1)}, u32[]{:S(2)}, u32[]{:S(2)}) collective-permute-start(f32[2,256,256]{2,1,0:T(8,128)S(1)} %get-tuple-element.31.real.refs_2_.refs_0_), channel_id=1, source_target_pairs={{0,4},{4,0},{8,12},{12,8},{16,20},{20,16},{24,28},{28,24},{1,5},{5... | collective-permute-start | bytes 1572872 | tf_op jit(solution)/shard_map/ppermute | solution.py:515
  33.2 8.3 %collective-permute-start.5 = (f32[2,256,256]{2,1,0:T(8,128)S(1)}, f32[2,256,256]{2,1,0:T(8,128)S(1)}, u32[]{:S(2)}, u32[]{:S(2)}) collective-permute-start(f32[2,256,256]{2,1,0:T(8,128)S(1)} %get-tuple-element.32.imag.refs_4_), channel_id=1, source_target_pairs={{0,8},{4,12},{8,0},{12,4},{16,24},{20,28},{24,16},{28,20},{1,9},{5... | collective-permute-start | bytes 1572872 | tf_op jit(solution)/shard_map/ppermute | solution.py:515
  34.5 10.2 %collective-permute-start.6 = (f32[2,256,256]{2,1,0:T(8,128)S(1)}, f32[2,256,256]{2,1,0:T(8,128)S(1)}, u32[]{:S(2)}, u32[]{:S(2)}) collective-permute-start(f32[2,256,256]{2,1,0:T(8,128)S(1)} %get-tuple-element.32.imag.refs_4_), channel_id=1, source_target_pairs={{8,16},{12,20},{16,8},{20,12},{9,17},{13,21},{17,9},{21,13},{10,18... | collective-permute-start | bytes 1572872 | tf_op jit(solution)/shard_map/ppermute | solution.py:515
  45.3 23.9 %collective-permute-start.7 = (f32[4,256,256]{2,1,0:T(8,128)S(1)}, f32[4,256,256]{2,1,0:T(8,128)S(1)}, u32[]{:S(2)}, u32[]{:S(2)}) collective-permute-start(f32[4,256,256]{2,1,0:T(8,128)S(1)} %get-tuple-element.35), channel_id=1, source_target_pairs={{0,1},{1,0},{2,3},{3,2},{4,5},{5,4},{6,7},{7,6},{8,9},{9,8},{10,11... | collective-permute-start | bytes 3145736 | tf_op jit(solution)/shard_map/ppermute | solution.py:512
  51.8 8.9 %collective-permute-start.11 = (f32[2,256,256]{2,1,0:T(8,128)S(1)}, f32[2,256,256]{2,1,0:T(8,128)S(1)}, u32[]{:S(2)}, u32[]{:S(2)}) collective-permute-start(f32[2,256,256]{2,1,0:T(8,128)S(1)} %shard_map.96), channel_id=1, source_target_pairs={{1,2},{2,1},{0,4},{3,7},{5,6},{6,5},{4,0},{7,3},{9,10},{10,9},{8,1... | collective-permute-start | bytes 1572872 | tf_op jit(solution)/shard_map/ppermute | solution.py:585
  53.1 13.2 %collective-permute-start.12 = (f32[2,256,256]{2,1,0:T(8,128)S(1)}, f32[2,256,256]{2,1,0:T(8,128)S(1)}, u32[]{:S(2)}, u32[]{:S(2)}) collective-permute-start(f32[2,256,256]{2,1,0:T(8,128)S(1)} %get-tuple-element.40), channel_id=1, source_target_pairs={{1,2},{2,1},{5,6},{6,5},{9,10},{10,9},{13,14},{14,13},{17,18},{18,... | collective-permute-start | bytes 1572872 | tf_op jit(solution)/shard_map/ppermute | solution.py:512
  66.9 8.0 %collective-permute-start.13 = (f32[1,256,256]{2,1,0:T(8,128)S(1)}, f32[1,256,256]{2,1,0:T(8,128)S(1)}, u32[]{:S(2)}, u32[]{:S(2)}) collective-permute-start(f32[1,256,256]{2,1,0:T(8,128)S(1)} %get-tuple-element.42), channel_id=1, source_target_pairs={{0,8},{4,12},{8,0},{12,4},{16,24},{20,28},{24,16},{28,20},{1,9},{5... | collective-permute-start | bytes 786440 | tf_op jit(solution)/shard_map/ppermute | solution.py:515
  67.0 9.9 %collective-permute-start.14 = (f32[1,256,256]{2,1,0:T(8,128)S(1)}, f32[1,256,256]{2,1,0:T(8,128)S(1)}, u32[]{:S(2)}, u32[]{:S(2)}) collective-permute-start(f32[1,256,256]{2,1,0:T(8,128)S(1)} %get-tuple-element.43), channel_id=1, source_target_pairs={{8,16},{12,20},{16,8},{20,12},{9,17},{13,21},{17,9},{21,13},{10,18... | collective-permute-start | bytes 786440 | tf_op jit(solution)/shard_map/ppermute | solution.py:515
  68.9 8.0 %collective-permute-start.15 = (f32[1,256,256]{2,1,0:T(8,128)S(1)}, f32[1,256,256]{2,1,0:T(8,128)S(1)}, u32[]{:S(2)}, u32[]{:S(2)}) collective-permute-start(f32[1,256,256]{2,1,0:T(8,128)S(1)} %get-tuple-element.44), channel_id=1, source_target_pairs={{0,4},{4,0},{8,12},{12,8},{16,20},{20,16},{24,28},{28,24},{1,5},{5... | collective-permute-start | bytes 786440 | tf_op jit(solution)/shard_map/ppermute | solution.py:515
  69.7 8.0 %collective-permute-start.10 = (f32[1,256,256]{2,1,0:T(8,128)S(1)}, f32[1,256,256]{2,1,0:T(8,128)S(1)}, u32[]{:S(2)}, u32[]{:S(2)}) collective-permute-start(f32[1,256,256]{2,1,0:T(8,128)S(1)} %get-tuple-element.39), channel_id=1, source_target_pairs={{0,4},{4,0},{8,12},{12,8},{16,20},{20,16},{24,28},{28,24},{1,5},{5... | collective-permute-start | bytes 786440 | tf_op jit(solution)/shard_map/ppermute | solution.py:515
  71.0 6.7 %collective-permute-start.8 = (f32[1,256,256]{2,1,0:T(8,128)S(1)}, f32[1,256,256]{2,1,0:T(8,128)S(1)}, u32[]{:S(2)}, u32[]{:S(2)}) collective-permute-start(f32[1,256,256]{2,1,0:T(8,128)S(1)} %get-tuple-element.37), channel_id=1, source_target_pairs={{0,8},{4,12},{8,0},{12,4},{16,24},{20,28},{24,16},{28,20},{1,9},{5... | collective-permute-start | bytes 786440 | tf_op jit(solution)/shard_map/ppermute | solution.py:515
  74.9 7.1 %collective-permute-start.9 = (f32[1,256,256]{2,1,0:T(8,128)S(1)}, f32[1,256,256]{2,1,0:T(8,128)S(1)}, u32[]{:S(2)}, u32[]{:S(2)}) collective-permute-start(f32[1,256,256]{2,1,0:T(8,128)S(1)} %get-tuple-element.38), channel_id=1, source_target_pairs={{8,16},{12,20},{16,8},{20,12},{9,17},{13,21},{17,9},{21,13},{10,18... | collective-permute-start | bytes 786440 | tf_op jit(solution)/shard_map/ppermute | solution.py:515

commit v5 on v4

--- a/solution.py
+++ b/solution.py
@@ -39,17 +39,11 @@
 def start_series(real, imag):
     shape = real.shape
     eye = lax.broadcasted_iota(jnp.int32, shape, 0) == lax.broadcasted_iota(jnp.int32, shape, 1)
-    diag_real = jnp.where(eye, real, 0.0)
-    diag_imag = jnp.where(eye, imag, 0.0)
-
-    def inverse(axis):
-        a = jnp.sum(diag_real, axis, keepdims=True)
-        b = jnp.sum(diag_imag, axis, keepdims=True)
-        modulus = a * a + b * b
-        return a / modulus, -b / modulus
-
-    col_real, col_imag = inverse(0)
-    row_real, row_imag = inverse(1)
+    a = jnp.sum(jnp.where(eye, real, 0.0), 0, keepdims=True)
+    b = jnp.sum(jnp.where(eye, imag, 0.0), 0, keepdims=True)
+    modulus = a * a + b * b
+    col_real, col_imag = a / modulus, -b / modulus
+    row_real, row_imag = col_real.reshape(-1, 1), col_imag.reshape(-1, 1)
     e_real = jnp.where(eye, 0.0, imag * col_imag - real * col_real)
     e_imag = jnp.where(eye, 0.0, -(real * col_imag + imag * col_real))
     t_real = e_real + jnp.where(eye, 1.0, 0.0)
@@ -187,55 +181,83 @@
     return call(body, shape, arrays + list(after), 16)
 
 
-def green_step(sections, active, pack, block, first, second, passed=(), joined=(), after=()):
-    arrays = [pack] + [a for a in first + second if a is not None]
-    count = len(arrays)
-    arrays = arrays + list(passed) + [a for pair in joined for a in pair] + list(after)
-    size = 1 + len(joined)
+def green_value(source, block, terms):
+    value = [source[2 * block], source[2 * block + 1]]
+    for place in (0, 1):
+        for term in terms:
+            value[place] = value[place] - term(place)
+    return value
+
+
+def green_step(sections, active, pack, block, sigmas, after=()):
+    arrays = [pack] + list(sigmas)
 
     def body(*refs):
         outs = refs[-2:]
 
         def put(place, value):
-            if joined:
-                outs[place][0] = value
-            else:
-                outs[place][...] = value
+            outs[place][...] = value
 
         def work():
-            rest = list(refs[1:count])
-            value = [refs[0][2 * block], refs[0][2 * block + 1]]
-            outer = is_at(0, sections)
-            for pair in (first, second):
-                taken = [None if a is None else rest.pop(0) for a in pair]
-                for place in (0, 1):
-                    terms = [
-                        jnp.zeros_like(value[0]) if t is None else t[place] for t in taken
-                    ]
-                    term = terms[0] if len(terms) == 1 else jnp.where(outer, *terms)
-                    value[place] = value[place] - term
-            inverse_core(*value, put)
+            terms = [lambda place, ref=ref: ref[place] for ref in refs[1 : len(arrays)]]
+            inverse_core(*green_value(refs[0], block, terms), put)
 
         if active is None:
             work()
-        else:
-            mine = is_at(active, sections)
-            pl.when(mine)(work)
-
-            @pl.when(jnp.logical_not(mine))
-            def _():
-                for place in (0, 1):
-                    if passed:
-                        put(place, refs[count + place][...])
-                    else:
-                        put(place, jnp.zeros(refs[0].shape[1:], F32))
-
-        for number in range(len(joined)):
+            return
+        mine = is_at(active, sections)
+        pl.when(mine)(work)
+
+        @pl.when(jnp.logical_not(mine))
+        def _():
             for place in (0, 1):
-                outs[place][1 + number] = refs[count + len(passed) + 2 * number + place][...]
-
-    flat = jax.ShapeDtypeStruct(((size,) if joined else ()) + pack.shape[1:], F32)
-    return call(body, (flat, flat), arrays, 12)
+                put(place, jnp.zeros(refs[0].shape[1:], F32))
+
+    flat = jax.ShapeDtypeStruct(pack.shape[1:], F32)
+    return call(body, (flat, flat), arrays + list(after), 12)
+
+
+def greens_at_ends(sections, pack, outer_terms, ready, inner_first, second, between):
+    last = len(between) + 1
+    flat_between = [a for pair in between for a in pair]
+    arrays = [pack, *outer_terms, *ready, inner_first, second, *flat_between]
+    count = len(outer_terms)
+
+    def body(*refs):
+        outs = refs[-2:]
+        source = refs[0]
+        extra = refs[1 : 1 + count]
+        done = refs[1 + count : 3 + count]
+        inner_sigma, sigma = refs[3 + count : 5 + count]
+        rest = refs[5 + count : -2]
+        outer = is_at(0, sections)
+
+        def at(ref):
+            return lambda place: ref[place]
+
+        def put_at(index):
+            def put(place, value):
+                outs[place][index] = value
+
+            return put
+
+        @pl.when(outer)
+        def _():
+            inverse_core(*green_value(source, last, [at(ref) for ref in extra]), put_at(last))
+            inverse_core(*green_value(source, 0, [at(sigma)]), put_at(0))
+
+        @pl.when(jnp.logical_not(outer))
+        def _():
+            inverse_core(*green_value(source, 0, [at(inner_sigma), at(sigma)]), put_at(0))
+            for place in (0, 1):
+                outs[place][last] = done[place][...]
+
+        for number in range(last - 1):
+            for place in (0, 1):
+                outs[place][1 + number] = rest[2 * number + place][...]
+
+    stack = jax.ShapeDtypeStruct((last + 1,) + pack.shape[1:], F32)
+    return call(body, (stack, stack), arrays, 24)
 
 
 def prepare_kernel(
@@ -495,6 +517,10 @@
     )(*group, *before)
 
 
+def chosen_first(sections, outer_value, inner_value):
+    return jnp.where(is_at(0, sections), outer_value, inner_value)
+
+
 def step(
     onsite, hopping, coupling, broadening, born_sigma, phonon_shift, phonon_local, phonon_side
 ):
@@ -556,7 +582,9 @@
     arriving = enter_step(sections, half - 1, 0, pack, sigma)
     earlier = tuple(first[step][last] for step in range(half))
     sigma = over_section(arriving, pairs)
-    ready = green_step(sections, half - 1, pack, last, earlier[1:], (arriving,), after=all_weights)
+    ready = green_step(
+        sections, half - 1, pack, last, (first[half - 1][last], arriving), after=all_weights
+    )
     for index in range(last, -1, -1):
         link = (
             inner_link(pack_in, index - 1, True)
@@ -565,24 +593,22 @@
         )
         after = ready if index == last else ()
         sigma = chain_step(sections, 0, pack_in, index, [sigma], link, after=after)
-    green = green_step(sections, 0, pack, last, earlier[:1], (sigma,), passed=ready)
-    second = (sigma, arriving)
-    joined = []
+    entered = (sigma, arriving)
+    between = []
     for index in range(last, 0, -1):
-        joined.insert(0, green)
         link = inner_link(pack, index - 1, True)
-        second = (
-            chain_step(sections, None, pack, index, second, link, after=green),
-        )
-        earlier = tuple(first[step][index - 1] for step in range(half))
-        green = green_step(
-            sections, None, pack, index - 1, earlier, second, joined=joined if index == 1 else ()
-        )
-    real, imag = green
+        sent = chain_step(sections, None, pack, index, entered, link, after=ready)
+        entered = (sent,)
+        if index > 1:
+            kept = chosen_first(sections, *(first[step][index - 1] for step in range(half)))
+            between.insert(0, green_step(sections, None, pack, index - 1, (kept, sent)))
+    real, imag = greens_at_ends(
+        sections, pack, (first[0][last], sigma), ready, first[half - 1][0], entered[0], between
+    )
     partner = over_energy(real, swap)
     ahead = over_energy(imag, first_swap)
     behind = over_energy(imag, second_swap)
-    middle_real = lax.ppermute(last_blocks(real, partner), ("energy", "section"), crossing)
+    middle_real = over_section(last_blocks(real, partner), across)
 
     side_partner, side_own, middle, shared = side_terms(
         sections, side_weight, real, partner, imag, ahead, behind

time: 83.2 us -> 83.7 us (level)
  the two profiles are of different devices: /device:TPU:17 before, /device:TPU:18 now
where the time goes in v5:
time: 83.7 us; the launch traced here: 83.5 us
  waiting for transfers between devices  38.4 us (46%)
  starting transfers between devices  25.7 us (31%)
  Pallas kernels  18.3 us (22%)
  between operations  1.11 us (1%)
    ppermute x9, waiting for transfers between devices, over_energy(): return lax.ppermute(value, 'energy', route)  17.9 us
    ppermute x6, starting transfers between devices, over_section(): return lax.ppermute(value, 'section', route)  13.3 us
    pallas_call x15, Pallas kernels, call(): pl.pallas_call(body, out_shape=out_shape, in_specs=[VMEM] * len(operands)...  13.2 us
    ppermute x9, starting transfers between devices, over_energy(): return lax.ppermute(value, 'energy', route)  12.1 us
    ppermute x6, waiting for transfers between devices, over_section(): return lax.ppermute(value, 'section', route)  12.1 us
    ppermute x1, waiting for transfers between devices, step(): sigma = lax.ppermute(sigma, ('energy', 'section'), crossing)  8.45 us
    pallas_call x1, Pallas kernels, prepare(): pl.pallas_call(functools.partial(prepare_kernel, sections, spread), out_s...  2.07 us
  transfers between devices with their start and end apart: 16, of which 10 were waited for; matrix products, arithmetic and copies ran while one was open for 0% of the time, Pallas kernels for 12%

profile of v5, /device:TPU:18, one launch (start us, length us, event | category | flops | bytes accessed | tf_op | source)
XLA Modules:
  0.0 83.5 jit_solution(371821809478029394)
XLA Ops:
  0.7 2.1 %prepare.1.refs_0_.refs_1_.refs_2_.source.refs_3_ = f32[8,256,256]{2,1,0:T(8,128)S(1)} custom-call(f32[1,1]{1,0:T(1,128)} %bitcast.1.broadening, f32[2,256]{1,0:T(2,128)} %onsite.1, f32[2,256,256]{2,1,0:T(8,128)} %hopping.1, f32[2,256,256]{2,1,0:T(8,128)} %coupling.1, f32[1,2,2,256,256]{4,3,2,1,0:T(8,128)} %born.1), custom_call_target="tpu_custom_call" | custom-call | tf_op jit(solution)/shard_map/prepare/pallas_call | solution.py:312
  2.9 4.6 %collective-permute-start = (f32[2,256,256]{2,1,0:T(8,128)S(1)}, f32[2,256,256]{2,1,0:T(8,128)S(1)}, u32[]{:S(2)}, u32[]{:S(2)}) collective-permute-start(f32[2,256,256]{2,1,0:T(8,128)S(1)} %shard_map.83), channel_id=1, source_target_pairs={{0,1},{1,0},{2,3},{3,2},{4,5},{5,4},{6,7},{7,6},{8,9},{9,8},{10,11... | collective-permute-start | bytes 1572872 | tf_op jit(solution)/shard_map/ppermute | solution.py:538
  7.5 1.5 %collective-permute-done.value = f32[2,256,256]{2,1,0:T(8,128)S(1)} collective-permute-done((f32[2,256,256]{2,1,0:T(8,128)S(1)}, f32[2,256,256]{2,1,0:T(8,128)S(1)}, u32[]{:S(2)}, u32[]{:S(2)}) %collective-permute-start) | collective-permute-done | bytes 524320 | tf_op jit(solution)/shard_map/ppermute | solution.py:538
  9.0 0.8 shard_map.84.refs_1_.refs_5_
  9.9 2.2 %shard_map.85.refs_1_ = f32[2,256,256]{2,1,0:T(8,128)S(1)} custom-call(f32[8,256,256]{2,1,0:T(8,128)S(1)} %prepare.1.refs_0_.refs_1_.refs_2_.source.refs_3_, f32[2,256,256]{2,1,0:T(8,128)S(1)} %shard_map.84.refs_1_.refs_5_, f32[8,256,256]{2,1,0:T(8,128)S(1)} %prepare.1.refs_0_.refs_1_.refs_2_.source.refs_3_), custom_call_target="tpu_custom_call" | custom-call | flops 1610612736 | bytes 2097152 | tf_op jit(solution)/shard_map/pallas_call | solution.py:99
  12.1 2.1 %shard_map.86._ = f32[2,256,256]{2,1,0:T(8,128)S(1)} custom-call(f32[8,256,256]{2,1,0:T(8,128)S(1)} %prepare.1.refs_0_.refs_1_.refs_2_.source.refs_3_, f32[2,256,256]{2,1,0:T(8,128)S(1)} %shard_map.85.refs_1_, f32[8,256,256]{2,1,0:T(8,128)S(1)} %prepare.1.refs_0_.refs_1_.refs_2_.source.refs_3_), custom_call_target="tpu_custom_call" | custom-call | flops 1610612736 | bytes 2097152 | tf_op jit(solution)/shard_map/pallas_call | solution.py:99
  14.5 8.4 %collective-permute-done.2.value = f32[2,256,256]{2,1,0:T(8,128)S(1)} collective-permute-done((f32[2,256,256]{2,1,0:T(8,128)S(1)}, f32[2,256,256]{2,1,0:T(8,128)S(1)}, u32[]{:S(2)}, u32[]{:S(2)}) %collective-permute-start.2) | collective-permute-done | bytes 524320 | tf_op jit(solution)/shard_map/ppermute | solution.py:577
  23.1 1.4 %weights.1 = (f32[5,256,256]{2,1,0:T(8,128)S(1)}, f32[5,256,256]{2,1,0:T(8,128)S(1)}) custom-call(s32[4]{0:T(128)S(1)} %copy-done.2, f32[4,256,256]{2,1,0:T(8,128)S(1)} %copy-done, f32[4,256,256]{2,1,0:T(8,128)S(1)} %copy-done.1, f32[2,256,256]{2,1,0:T(8,128)S(1)} %shard_map.86._), custom_call_target="tpu_custom_call" | custom-call | flops 1048576 | bytes 8388608 | tf_op jit(solution)/shard_map/weights/pallas_call | solution.py:361
  24.4 1.9 %shard_map.88 = (f32[256,256]{1,0:T(8,128)S(1)}, f32[256,256]{1,0:T(8,128)S(1)}) custom-call(f32[8,256,256]{2,1,0:T(8,128)S(1)} %prepare.1.refs_0_.refs_1_.refs_2_.source.refs_3_, f32[2,256,256]{2,1,0:T(8,128)S(1)} %shard_map.85.refs_1_, f32[2,256,256]{2,1,0:T(8,128)S(1)} %shard_map.87.refs_2_, f32[5,256,256]{2,1,0:T(8,128)S(1)} %get-tuple-element.23.refs_3_.refs_0_, ...), custom_call_target="tpu_custom_call" | custom-call | flops 1207959552 | bytes 2097152 | tf_op jit(solution)/shard_map/pallas_call | solution.py:99
  26.5 2.2 %shard_map.91.refs_6_ = f32[2,256,256]{2,1,0:T(8,128)S(1)} custom-call(f32[8,256,256]{2,1,0:T(8,128)S(1)} %prepare.1.refs_0_.refs_1_.refs_2_.source.refs_3_, f32[2,256,256]{2,1,0:T(8,128)S(1)} %shard_map.90.refs_1_.refs_2_, f32[2,256,256]{2,1,0:T(8,128)S(1)} %shard_map.87.refs_2_, f32[8,256,256]{2,1,0:T(8,128)S(1)} %prepare.1.refs_0_.refs_1_.refs_2_.source.refs_3_, ...), custom_call_target="tpu_custom_call" | custom-call | flops 1610612736 | bytes 2097152 | tf_op jit(solution)/shard_map/pallas_call | solution.py:99
  28.7 2.1 %shard_map.92 = (f32[2,256,256]{2,1,0:T(8,128)S(1)}, f32[2,256,256]{2,1,0:T(8,128)S(1)}) custom-call(f32[8,256,256]{2,1,0:T(8,128)S(1)} %prepare.1.refs_0_.refs_1_.refs_2_.source.refs_3_, f32[2,256,256]{2,1,0:T(8,128)S(1)} %shard_map.82.refs_1_, f32[2,256,256]{2,1,0:T(8,128)S(1)} %shard_map.90.refs_1_.refs_2_, ...), custom_call_target="tpu_custom_call" | custom-call | flops 2415919104 | bytes 2097152 | tf_op jit(solution)/shard_map/pallas_call | solution.py:99
  30.8 1.6 %collective-permute-start.4 = (f32[2,256,256]{2,1,0:T(8,128)S(1)}, f32[2,256,256]{2,1,0:T(8,128)S(1)}, u32[]{:S(2)}, u32[]{:S(2)}) collective-permute-start(f32[2,256,256]{2,1,0:T(8,128)S(1)} %get-tuple-element.27.real.refs_2_.refs_0_), channel_id=1, source_target_pairs={{0,4},{4,0},{8,12},{12,8},{16,20},{20,16},{24,28},{28,24},{1,5},{5... | collective-permute-start | bytes 1572872 | tf_op jit(solution)/shard_map/ppermute | solution.py:541
  32.4 1.6 %collective-permute-start.5 = (f32[2,256,256]{2,1,0:T(8,128)S(1)}, f32[2,256,256]{2,1,0:T(8,128)S(1)}, u32[]{:S(2)}, u32[]{:S(2)}) collective-permute-start(f32[2,256,256]{2,1,0:T(8,128)S(1)} %get-tuple-element.28.imag.refs_4_), channel_id=1, source_target_pairs={{0,8},{4,12},{8,0},{12,4},{16,24},{20,28},{24,16},{28,20},{1,9},{5... | collective-permute-start | bytes 1572872 | tf_op jit(solution)/shard_map/ppermute | solution.py:541
  34.0 1.9 %collective-permute-start.6 = (f32[2,256,256]{2,1,0:T(8,128)S(1)}, f32[2,256,256]{2,1,0:T(8,128)S(1)}, u32[]{:S(2)}, u32[]{:S(2)}) collective-permute-start(f32[2,256,256]{2,1,0:T(8,128)S(1)} %get-tuple-element.28.imag.refs_4_), channel_id=1, source_target_pairs={{8,16},{12,20},{16,8},{20,12},{9,17},{13,21},{17,9},{21,13},{10,18... | collective-permute-start | bytes 1572872 | tf_op jit(solution)/shard_map/ppermute | solution.py:541
  35.9 6.1 %collective-permute-done.4.partner.refs_3_.refs_1_ = f32[2,256,256]{2,1,0:T(8,128)S(1)} collective-permute-done((f32[2,256,256]{2,1,0:T(8,128)S(1)}, f32[2,256,256]{2,1,0:T(8,128)S(1)}, u32[]{:S(2)}, u32[]{:S(2)}) %collective-permute-start.4) | collective-permute-done | bytes 524320 | tf_op jit(solution)/shard_map/ppermute | solution.py:541
  42.0 1.8 %collective-permute-done.5.ahead.refs_5_ = f32[2,256,256]{2,1,0:T(8,128)S(1)} collective-permute-done((f32[2,256,256]{2,1,0:T(8,128)S(1)}, f32[2,256,256]{2,1,0:T(8,128)S(1)}, u32[]{:S(2)}, u32[]{:S(2)}) %collective-permute-start.5) | collective-permute-done | bytes 524320 | tf_op jit(solution)/shard_map/ppermute | solution.py:541
  43.8 3.7 %collective-permute-done.6.behind.refs_6_ = f32[2,256,256]{2,1,0:T(8,128)S(1)} collective-permute-done((f32[2,256,256]{2,1,0:T(8,128)S(1)}, f32[2,256,256]{2,1,0:T(8,128)S(1)}, u32[]{:S(2)}, u32[]{:S(2)}) %collective-permute-start.6) | collective-permute-done | bytes 524320 | tf_op jit(solution)/shard_map/ppermute | solution.py:541
  47.5 0.6 shard_map.93
  48.1 3.0 %collective-permute-start.7 = (f32[4,256,256]{2,1,0:T(8,128)S(1)}, f32[4,256,256]{2,1,0:T(8,128)S(1)}, u32[]{:S(2)}, u32[]{:S(2)}) collective-permute-start(f32[4,256,256]{2,1,0:T(8,128)S(1)} %get-tuple-element.31), channel_id=1, source_target_pairs={{0,1},{1,0},{2,3},{3,2},{4,5},{5,4},{6,7},{7,6},{8,9},{9,8},{10,11... | collective-permute-start | bytes 3145736 | tf_op jit(solution)/shard_map/ppermute | solution.py:538
  51.2 2.1 %collective-permute-start.11 = (f32[2,256,256]{2,1,0:T(8,128)S(1)}, f32[2,256,256]{2,1,0:T(8,128)S(1)}, u32[]{:S(2)}, u32[]{:S(2)}) collective-permute-start(f32[2,256,256]{2,1,0:T(8,128)S(1)} %shard_map.95), channel_id=1, source_target_pairs={{1,2},{2,1},{5,6},{6,5},{9,10},{10,9},{13,14},{14,13},{17,18},{18,... | collective-permute-start | bytes 1572872 | tf_op jit(solution)/shard_map/ppermute | solution.py:538
  53.3 3.5 %collective-permute-start.12 = (f32[2,256,256]{2,1,0:T(8,128)S(1)}, f32[2,256,256]{2,1,0:T(8,128)S(1)}, u32[]{:S(2)}, u32[]{:S(2)}) collective-permute-start(f32[2,256,256]{2,1,0:T(8,128)S(1)} %get-tuple-element.36), channel_id=1, source_target_pairs={{1,2},{2,1},{5,6},{6,5},{9,10},{10,9},{13,14},{14,13},{17,18},{18,... | collective-permute-start | bytes 1572872 | tf_op jit(solution)/shard_map/ppermute | solution.py:538
  56.8 4.9 %collective-permute-done.11.refs_9_ = f32[2,256,256]{2,1,0:T(8,128)S(1)} collective-permute-done((f32[2,256,256]{2,1,0:T(8,128)S(1)}, f32[2,256,256]{2,1,0:T(8,128)S(1)}, u32[]{:S(2)}, u32[]{:S(2)}) %collective-permute-start.11) | collective-permute-done | bytes 524320 | tf_op jit(solution)/shard_map/ppermute | solution.py:538
  61.7 5.6 %collective-permute-done.12.refs_10_ = f32[2,256,256]{2,1,0:T(8,128)S(1)} collective-permute-done((f32[2,256,256]{2,1,0:T(8,128)S(1)}, f32[2,256,256]{2,1,0:T(8,128)S(1)}, u32[]{:S(2)}, u32[]{:S(2)}) %collective-permute-start.12) | collective-permute-done | bytes 524320 | tf_op jit(solution)/shard_map/ppermute | solution.py:538
  67.9 1.9 %collective-permute-start.14 = (f32[1,256,256]{2,1,0:T(8,128)S(1)}, f32[1,256,256]{2,1,0:T(8,128)S(1)}, u32[]{:S(2)}, u32[]{:S(2)}) collective-permute-start(f32[1,256,256]{2,1,0:T(8,128)S(1)} %get-tuple-element.39), channel_id=1, source_target_pairs={{8,16},{12,20},{16,8},{20,12},{9,17},{13,21},{17,9},{21,13},{10,18... | collective-permute-start | bytes 786440 | tf_op jit(solution)/shard_map/ppermute | solution.py:541
  70.9 1.6 %collective-permute-start.10 = (f32[1,256,256]{2,1,0:T(8,128)S(1)}, f32[1,256,256]{2,1,0:T(8,128)S(1)}, u32[]{:S(2)}, u32[]{:S(2)}) collective-permute-start(f32[1,256,256]{2,1,0:T(8,128)S(1)} %get-tuple-element.35), channel_id=1, source_target_pairs={{0,4},{4,0},{8,12},{12,8},{16,20},{20,16},{24,28},{28,24},{1,5},{5... | collective-permute-start | bytes 786440 | tf_op jit(solution)/shard_map/ppermute | solution.py:541
  72.5 0.8 collective-permute-start.8
  73.2 1.0 %collective-permute-done.13.from_first = f32[1,256,256]{2,1,0:T(8,128)S(1)} collective-permute-done((f32[1,256,256]{2,1,0:T(8,128)S(1)}, f32[1,256,256]{2,1,0:T(8,128)S(1)}, u32[]{:S(2)}, u32[]{:S(2)}) %collective-permute-start.13) | collective-permute-done | bytes 262176 | tf_op jit(solution)/shard_map/ppermute | solution.py:541
  74.2 2.1 %collective-permute-start.9 = (f32[1,256,256]{2,1,0:T(8,128)S(1)}, f32[1,256,256]{2,1,0:T(8,128)S(1)}, u32[]{:S(2)}, u32[]{:S(2)}) collective-permute-start(f32[1,256,256]{2,1,0:T(8,128)S(1)} %get-tuple-element.34), channel_id=1, source_target_pairs={{8,16},{12,20},{16,8},{20,12},{9,17},{13,21},{17,9},{21,13},{10,18... | collective-permute-start | bytes 786440 | tf_op jit(solution)/shard_map/ppermute | solution.py:541
  76.4 0.8 shard_map.97.rest_0_
  77.2 1.8 %collective-permute-done.10.from_partner = f32[1,256,256]{2,1,0:T(8,128)S(1)} collective-permute-done((f32[1,256,256]{2,1,0:T(8,128)S(1)}, f32[1,256,256]{2,1,0:T(8,128)S(1)}, u32[]{:S(2)}, u32[]{:S(2)}) %collective-permute-start.10) | collective-permute-done | bytes 262176 | tf_op jit(solution)/shard_map/ppermute | solution.py:541
  79.1 3.4 %collective-permute-done.9.from_second = f32[1,256,256]{2,1,0:T(8,128)S(1)} collective-permute-done((f32[1,256,256]{2,1,0:T(8,128)S(1)}, f32[1,256,256]{2,1,0:T(8,128)S(1)}, u32[]{:S(2)}, u32[]{:S(2)}) %collective-permute-start.9) | collective-permute-done | bytes 262176 | tf_op jit(solution)/shard_map/ppermute | solution.py:541
  82.5 0.8 shard_map.98
  (25 shorter events, 2.3 us)
Async XLA Ops:
  2.7 23.6 %collective-permute-start.1 = (f32[8,256,256]{2,1,0:T(8,128)S(1)}, f32[8,256,256]{2,1,0:T(8,128)S(1)}, u32[]{:S(2)}, u32[]{:S(2)}) collective-permute-start(f32[8,256,256]{2,1,0:T(8,128)S(1)} %prepare.1.refs_0_.refs_1_.refs_2_.source.refs_3_), channel_id=1, source_target_pairs={{0,1},{1,0},{2,3},{3,2},{4,5},{5,4},{6,7},{7,6},{8,9},{9,8},{10,11... | collective-permute-start | bytes 6291464 | tf_op jit(solution)/shard_map/ppermute | solution.py:538
  2.9 6.1 %collective-permute-start = (f32[2,256,256]{2,1,0:T(8,128)S(1)}, f32[2,256,256]{2,1,0:T(8,128)S(1)}, u32[]{:S(2)}, u32[]{:S(2)}) collective-permute-start(f32[2,256,256]{2,1,0:T(8,128)S(1)} %shard_map.83), channel_id=1, source_target_pairs={{0,1},{1,0},{2,3},{3,2},{4,5},{5,4},{6,7},{7,6},{8,9},{9,8},{10,11... | collective-permute-start | bytes 1572872 | tf_op jit(solution)/shard_map/ppermute | solution.py:538
  14.2 8.8 %copy-start = (f32[4,256,256]{2,1,0:T(8,128)S(1)}, f32[4,256,256]{2,1,0:T(8,128)}, u32[]{:S(2)}) copy-start(f32[4,256,256]{2,1,0:T(8,128)} %local_ref.1) | copy-start | bytes 3145732
  14.2 8.8 %copy-start.1 = (f32[4,256,256]{2,1,0:T(8,128)S(1)}, f32[4,256,256]{2,1,0:T(8,128)}, u32[]{:S(2)}) copy-start(f32[4,256,256]{2,1,0:T(8,128)} %side_ref.1) | copy-start | bytes 3145732
  14.2 8.8 %copy-start.2 = (s32[4]{0:T(128)S(1)}, s32[4]{0:T(128)}, u32[]{:S(2)}) copy-start(s32[4]{0:T(128)} %shift_ref.1) | copy-start | bytes 52
  14.2 8.7 %collective-permute-start.2 = (f32[2,256,256]{2,1,0:T(8,128)S(1)}, f32[2,256,256]{2,1,0:T(8,128)S(1)}, u32[]{:S(2)}, u32[]{:S(2)}) collective-permute-start(f32[2,256,256]{2,1,0:T(8,128)S(1)} %shard_map.86._), channel_id=1, source_target_pairs={{1,2},{2,1},{0,4},{3,7},{5,6},{6,5},{4,0},{7,3},{9,10},{10,9},{8,1... | collective-permute-start | bytes 1572872 | tf_op jit(solution)/shard_map/ppermute | solution.py:577
  22.9 3.4 %collective-permute-start.3 = (f32[2,256,256]{2,1,0:T(8,128)S(1)}, f32[2,256,256]{2,1,0:T(8,128)S(1)}, u32[]{:S(2)}, u32[]{:S(2)}) collective-permute-start(f32[2,256,256]{2,1,0:T(8,128)S(1)} %shard_map.87.refs_2_), channel_id=1, source_target_pairs={{0,1},{1,0},{2,3},{3,2},{4,5},{5,4},{6,7},{7,6},{8,9},{9,8},{10,11... | collective-permute-start | bytes 1572872 | tf_op jit(solution)/shard_map/ppermute | solution.py:538
  30.8 11.2 %collective-permute-start.4 = (f32[2,256,256]{2,1,0:T(8,128)S(1)}, f32[2,256,256]{2,1,0:T(8,128)S(1)}, u32[]{:S(2)}, u32[]{:S(2)}) collective-permute-start(f32[2,256,256]{2,1,0:T(8,128)S(1)} %get-tuple-element.27.real.refs_2_.refs_0_), channel_id=1, source_target_pairs={{0,4},{4,0},{8,12},{12,8},{16,20},{20,16},{24,28},{28,24},{1,5},{5... | collective-permute-start | bytes 1572872 | tf_op jit(solution)/shard_map/ppermute | solution.py:541
  32.4 11.4 %collective-permute-start.5 = (f32[2,256,256]{2,1,0:T(8,128)S(1)}, f32[2,256,256]{2,1,0:T(8,128)S(1)}, u32[]{:S(2)}, u32[]{:S(2)}) collective-permute-start(f32[2,256,256]{2,1,0:T(8,128)S(1)} %get-tuple-element.28.imag.refs_4_), channel_id=1, source_target_pairs={{0,8},{4,12},{8,0},{12,4},{16,24},{20,28},{24,16},{28,20},{1,9},{5... | collective-permute-start | bytes 1572872 | tf_op jit(solution)/shard_map/ppermute | solution.py:541
  34.0 13.5 %collective-permute-start.6 = (f32[2,256,256]{2,1,0:T(8,128)S(1)}, f32[2,256,256]{2,1,0:T(8,128)S(1)}, u32[]{:S(2)}, u32[]{:S(2)}) collective-permute-start(f32[2,256,256]{2,1,0:T(8,128)S(1)} %get-tuple-element.28.imag.refs_4_), channel_id=1, source_target_pairs={{8,16},{12,20},{16,8},{20,12},{9,17},{13,21},{17,9},{21,13},{10,18... | collective-permute-start | bytes 1572872 | tf_op jit(solution)/shard_map/ppermute | solution.py:541
  48.1 22.3 %collective-permute-start.7 = (f32[4,256,256]{2,1,0:T(8,128)S(1)}, f32[4,256,256]{2,1,0:T(8,128)S(1)}, u32[]{:S(2)}, u32[]{:S(2)}) collective-permute-start(f32[4,256,256]{2,1,0:T(8,128)S(1)} %get-tuple-element.31), channel_id=1, source_target_pairs={{0,1},{1,0},{2,3},{3,2},{4,5},{5,4},{6,7},{7,6},{8,9},{9,8},{10,11... | collective-permute-start | bytes 3145736 | tf_op jit(solution)/shard_map/ppermute | solution.py:538
  51.2 10.5 %collective-permute-start.11 = (f32[2,256,256]{2,1,0:T(8,128)S(1)}, f32[2,256,256]{2,1,0:T(8,128)S(1)}, u32[]{:S(2)}, u32[]{:S(2)}) collective-permute-start(f32[2,256,256]{2,1,0:T(8,128)S(1)} %shard_map.95), channel_id=1, source_target_pairs={{1,2},{2,1},{5,6},{6,5},{9,10},{10,9},{13,14},{14,13},{17,18},{18,... | collective-permute-start | bytes 1572872 | tf_op jit(solution)/shard_map/ppermute | solution.py:538
  53.3 14.0 %collective-permute-start.12 = (f32[2,256,256]{2,1,0:T(8,128)S(1)}, f32[2,256,256]{2,1,0:T(8,128)S(1)}, u32[]{:S(2)}, u32[]{:S(2)}) collective-permute-start(f32[2,256,256]{2,1,0:T(8,128)S(1)} %get-tuple-element.36), channel_id=1, source_target_pairs={{1,2},{2,1},{5,6},{6,5},{9,10},{10,9},{13,14},{14,13},{17,18},{18,... | collective-permute-start | bytes 1572872 | tf_op jit(solution)/shard_map/ppermute | solution.py:538
  67.8 6.4 %collective-permute-start.13 = (f32[1,256,256]{2,1,0:T(8,128)S(1)}, f32[1,256,256]{2,1,0:T(8,128)S(1)}, u32[]{:S(2)}, u32[]{:S(2)}) collective-permute-start(f32[1,256,256]{2,1,0:T(8,128)S(1)} %get-tuple-element.38), channel_id=1, source_target_pairs={{0,8},{4,12},{8,0},{12,4},{16,24},{20,28},{24,16},{28,20},{1,9},{5... | collective-permute-start | bytes 786440 | tf_op jit(solution)/shard_map/ppermute | solution.py:541
  67.9 8.5 %collective-permute-start.14 = (f32[1,256,256]{2,1,0:T(8,128)S(1)}, f32[1,256,256]{2,1,0:T(8,128)S(1)}, u32[]{:S(2)}, u32[]{:S(2)}) collective-permute-start(f32[1,256,256]{2,1,0:T(8,128)S(1)} %get-tuple-element.39), channel_id=1, source_target_pairs={{8,16},{12,20},{16,8},{20,12},{9,17},{13,21},{17,9},{21,13},{10,18... | collective-permute-start | bytes 786440 | tf_op jit(solution)/shard_map/ppermute | solution.py:541
  69.8 6.6 %collective-permute-start.15 = (f32[1,256,256]{2,1,0:T(8,128)S(1)}, f32[1,256,256]{2,1,0:T(8,128)S(1)}, u32[]{:S(2)}, u32[]{:S(2)}) collective-permute-start(f32[1,256,256]{2,1,0:T(8,128)S(1)} %get-tuple-element.40), channel_id=1, source_target_pairs={{0,4},{4,0},{8,12},{12,8},{16,20},{20,16},{24,28},{28,24},{1,5},{5... | collective-permute-start | bytes 786440 | tf_op jit(solution)/shard_map/ppermute | solution.py:541
  70.9 8.2 %collective-permute-start.10 = (f32[1,256,256]{2,1,0:T(8,128)S(1)}, f32[1,256,256]{2,1,0:T(8,128)S(1)}, u32[]{:S(2)}, u32[]{:S(2)}) collective-permute-start(f32[1,256,256]{2,1,0:T(8,128)S(1)} %get-tuple-element.35), channel_id=1, source_target_pairs={{0,4},{4,0},{8,12},{12,8},{16,20},{20,16},{24,28},{28,24},{1,5},{5... | collective-permute-start | bytes 786440 | tf_op jit(solution)/shard_map/ppermute | solution.py:541
  72.5 6.6 %collective-permute-start.8 = (f32[1,256,256]{2,1,0:T(8,128)S(1)}, f32[1,256,256]{2,1,0:T(8,128)S(1)}, u32[]{:S(2)}, u32[]{:S(2)}) collective-permute-start(f32[1,256,256]{2,1,0:T(8,128)S(1)} %get-tuple-element.33), channel_id=1, source_target_pairs={{0,8},{4,12},{8,0},{12,4},{16,24},{20,28},{24,16},{28,20},{1,9},{5... | collective-permute-start | bytes 786440 | tf_op jit(solution)/shard_map/ppermute | solution.py:541
  74.2 8.3 %collective-permute-start.9 = (f32[1,256,256]{2,1,0:T(8,128)S(1)}, f32[1,256,256]{2,1,0:T(8,128)S(1)}, u32[]{:S(2)}, u32[]{:S(2)}) collective-permute-start(f32[1,256,256]{2,1,0:T(8,128)S(1)} %get-tuple-element.34), channel_id=1, source_target_pairs={{8,16},{12,20},{16,8},{20,12},{9,17},{13,21},{17,9},{21,13},{10,18... | collective-permute-start | bytes 786440 | tf_op jit(solution)/shard_map/ppermute | solution.py:541

commit v6 on v5

--- a/solution.py
+++ b/solution.py
@@ -261,49 +261,60 @@
 
 
 def prepare_kernel(
-    sections, spread, broadening, onsite, hopping, coupling, born, pack, hop, cup, sig, levels, sems
+    sections, spread, broadening, onsite, hopping, coupling, born, pack, first, hop, cup, sig, levels, sems
 ):
     blocks, dimension = onsite.shape
+    right_half = half_of(sections)
+    local_of = [jnp.where(right_half, blocks - 1 - k, k) for k in range(blocks)]
+    link_of = [jnp.where(right_half, blocks - 2 - k, k) for k in range(blocks - 1)] + [blocks - 1]
+    levels_copy = pltpu.make_async_copy(onsite, levels, sems.at[3 * blocks])
+    levels_copy.start()
     copies = []
     for index in range(blocks):
         for order, (source, target) in enumerate(
             (
-                (hopping.at[index], hop.at[index]),
-                (born.at[0, index], sig.at[index]),
-                (coupling.at[index], cup.at[index]),
+                (hopping.at[local_of[index]], hop.at[index]),
+                (born.at[0, local_of[index]], sig.at[index]),
+                (coupling.at[link_of[index]], cup.at[index]),
             )
         ):
             copy = pltpu.make_async_copy(source, target, sems.at[3 * index + order])
             copy.start()
             copies.append(copy)
-    copies.append(pltpu.make_async_copy(onsite, levels, sems.at[3 * blocks]))
-    copies[-1].start()
-    right_half = half_of(sections)
     flip = right_half.astype(jnp.int32)
     shape = (dimension, dimension)
     eye = lax.broadcasted_iota(jnp.int32, shape, 0) == lax.broadcasted_iota(jnp.int32, shape, 1)
     position = lax.axis_index("energy").astype(F32)
     energy = -2.0 + position * (4.0 / (spread - 1))
-    copies[3 * blocks].wait()
+    levels_copy.wait()
     width = jnp.broadcast_to(broadening[...], shape)
     for index in range(blocks):
-        place = jnp.where(right_half, blocks - 1 - index, index)
         copies[3 * index].wait()
         block = hop[index]
-        level = energy - levels[pl.ds(index, 1), :]
+        level = energy - levels[pl.ds(local_of[index], 1), :]
         real = jnp.where(eye, jnp.broadcast_to(level, shape), 0.0) - 0.5 * (block + block.T)
         copies[3 * index + 1].wait()
-        pack[2 * place] = real - sig[index, 0]
-        pack[2 * place + 1] = jnp.where(eye, width, 0.0) - sig[index, 1]
+        pack[2 * index] = real - sig[index, 0]
+        pack[2 * index + 1] = jnp.where(eye, width, 0.0) - sig[index, 1]
         copies[3 * index + 2].wait()
         link = cup[index]
-        if index < blocks - 1:
-            place = 2 * blocks + 2 * jnp.where(right_half, blocks - 2 - index, index)
+        place = 2 * blocks + 2 * index
+        if index == blocks - 1:
+            pack[place] = link
+            pack[place + 1] = link.T
+        else:
             pack[place + flip] = link
             pack[place + 1 - flip] = link.T
-        else:
-            pack[4 * blocks - 2] = link
-            pack[4 * blocks - 1] = link.T
+        if index == 0:
+            active = is_at(0, sections)
+
+            @pl.when(active)
+            def _():
+                chain_core(pack[0], pack[1], pack[2 * blocks], pack[2 * blocks + 1], first)
+
+            @pl.when(jnp.logical_not(active))
+            def _():
+                first[...] = jnp.zeros_like(first)
 
 
 def prepare(sections, spread, broadening, onsite, hopping, coupling, born):
@@ -311,9 +322,12 @@
     outside = pl.BlockSpec(memory_space=pltpu.HBM)
     return pl.pallas_call(
         functools.partial(prepare_kernel, sections, spread),
-        out_shape=jax.ShapeDtypeStruct((4 * blocks, dimension, dimension), F32),
+        out_shape=(
+            jax.ShapeDtypeStruct((4 * blocks, dimension, dimension), F32),
+            jax.ShapeDtypeStruct((2, dimension, dimension), F32),
+        ),
         in_specs=[VMEM] + [outside] * 4,
-        out_specs=VMEM,
+        out_specs=(VMEM, VMEM),
         scratch_shapes=[
             pltpu.VMEM((blocks, dimension, dimension), F32),
             pltpu.VMEM((blocks, dimension, dimension), F32),
@@ -549,7 +563,7 @@
         for s, t in across + [(0, 0), (sections - 1, sections - 1)]:
             crossing.append((a * sections + s, (b if s == t else a) * sections + t))
 
-    pack = prepare(sections, spread, broadening, onsite, hopping, coupling, born_sigma)
+    pack, begun = prepare(sections, spread, broadening, onsite, hopping, coupling, born_sigma)
 
     def inner_link(table, index, reverse=False):
         place = 2 * blocks + 2 * index
@@ -566,6 +580,9 @@
         for index in range(blocks):
             entering.append(sigma)
             given = [] if sigma is None else [sigma]
+            if step == 0 and index == 0:
+                sigma = begun
+                continue
             leaves = index == last
             link = [(pack, end, end + 1)] if leaves else inner_link(pack, index)
             sigma = chain_step(sections, step, pack, index, given, link, leaves=leaves)

time: 83.7 us -> 83.7 us (level)
    ppermute x6, waiting for transfers between devices: 12.1 us -> 13.1 us  [over_section(): return lax.ppermute(value, 'section', route)]
    pallas_call x15 -> x14, Pallas kernels: 13.2 us -> 13.1 us  [call(): pl.pallas_call(body, out_shape=out_shape, in_specs=[VMEM] * len(operands)...]
where the time goes in v6:
time: 83.7 us; the launch traced here: 83.5 us
  waiting for transfers between devices  39.2 us (47%)
  starting transfers between devices  25.3 us (30%)
  Pallas kernels  17.9 us (21%)
  between operations  1.09 us (1%)
    ppermute x9, waiting for transfers between devices, over_energy(): return lax.ppermute(value, 'energy', route)  17.9 us
    pallas_call x14, Pallas kernels, call(): pl.pallas_call(body, out_shape=out_shape, in_specs=[VMEM] * len(operands)...  13.1 us
    ppermute x6, waiting for transfers between devices, over_section(): return lax.ppermute(value, 'section', route)  13.1 us
    ppermute x6, starting transfers between devices, over_section(): return lax.ppermute(value, 'section', route)  12.7 us
    ppermute x9, starting transfers between devices, over_energy(): return lax.ppermute(value, 'energy', route)  12.1 us
    ppermute x1, waiting for transfers between devices, step(): sigma = lax.ppermute(sigma, ('energy', 'section'), crossing)  8.19 us
    pallas_call x1, Pallas kernels, prepare(): pl.pallas_call(functools.partial(prepare_kernel, sections, spread), out_s...  1.75 us
  transfers between devices with their start and end apart: 16, of which 10 were waited for; matrix products, arithmetic and copies ran while one was open for 0% of the time, Pallas kernels for 12%

profile of v6, /device:TPU:18, one launch (start us, length us, event | category | flops | bytes accessed | tf_op | source)
XLA Modules:
  0.0 83.5 jit_solution(13328384011598134652)
XLA Ops:
  0.7 1.7 %prepare.1 = (f32[8,256,256]{2,1,0:T(8,128)S(1)}, f32[2,256,256]{2,1,0:T(8,128)S(1)}) custom-call(f32[1,1]{1,0:T(1,128)} %bitcast.1.broadening, f32[2,256]{1,0:T(2,128)} %onsite.1, f32[2,256,256]{2,1,0:T(8,128)} %hopping.1, f32[2,256,256]{2,1,0:T(8,128)} %coupling.1, f32[1,2,2,256,256]{4,3,2,1,0:T(8,128)} %born.1), custom_call_target="tpu_custom_call" | custom-call | tf_op jit(solution)/shard_map/prepare/pallas_call | solution.py:323
  2.4 2.1 %collective-permute-start.1 = (f32[8,256,256]{2,1,0:T(8,128)S(1)}, f32[8,256,256]{2,1,0:T(8,128)S(1)}, u32[]{:S(2)}, u32[]{:S(2)}) collective-permute-start(f32[8,256,256]{2,1,0:T(8,128)S(1)} %get-tuple-element.25.refs_0_.refs_2_.source.refs_3_), channel_id=1, source_target_pairs={{0,1},{1,0},{2,3},{3,2},{4,5},{5,4},{6,7},{7,6},{8,9},{9,8},{10,11... | collective-permute-start | bytes 6291464 | tf_op jit(solution)/shard_map/ppermute | solution.py:552
  4.5 2.0 %collective-permute-start = (f32[2,256,256]{2,1,0:T(8,128)S(1)}, f32[2,256,256]{2,1,0:T(8,128)S(1)}, u32[]{:S(2)}, u32[]{:S(2)}) collective-permute-start(f32[2,256,256]{2,1,0:T(8,128)S(1)} %shard_map.82), channel_id=1, source_target_pairs={{0,1},{1,0},{2,3},{3,2},{4,5},{5,4},{6,7},{7,6},{8,9},{9,8},{10,11... | collective-permute-start | bytes 1572872 | tf_op jit(solution)/shard_map/ppermute | solution.py:552
  6.5 2.5 %collective-permute-done.value = f32[2,256,256]{2,1,0:T(8,128)S(1)} collective-permute-done((f32[2,256,256]{2,1,0:T(8,128)S(1)}, f32[2,256,256]{2,1,0:T(8,128)S(1)}, u32[]{:S(2)}, u32[]{:S(2)}) %collective-permute-start) | collective-permute-done | bytes 524320 | tf_op jit(solution)/shard_map/ppermute | solution.py:552
  9.0 0.8 shard_map.83.refs_1_.refs_5_
  9.8 2.2 %shard_map.84.refs_1_ = f32[2,256,256]{2,1,0:T(8,128)S(1)} custom-call(f32[8,256,256]{2,1,0:T(8,128)S(1)} %get-tuple-element.25.refs_0_.refs_2_.source.refs_3_, f32[2,256,256]{2,1,0:T(8,128)S(1)} %shard_map.83.refs_1_.refs_5_, f32[8,256,256]{2,1,0:T(8,128)S(1)} %get-tuple-element.25.refs_0_.refs_2_.source.refs_3_), custom_call_target="tpu_custom_call" | custom-call | flops 1610612736 | bytes 2097152 | tf_op jit(solution)/shard_map/pallas_call | solution.py:99
  12.1 2.1 %shard_map.85._ = f32[2,256,256]{2,1,0:T(8,128)S(1)} custom-call(f32[8,256,256]{2,1,0:T(8,128)S(1)} %get-tuple-element.25.refs_0_.refs_2_.source.refs_3_, f32[2,256,256]{2,1,0:T(8,128)S(1)} %shard_map.84.refs_1_, f32[8,256,256]{2,1,0:T(8,128)S(1)} %get-tuple-element.25.refs_0_.refs_2_.source.refs_3_), custom_call_target="tpu_custom_call" | custom-call | flops 1610612736 | bytes 2097152 | tf_op jit(solution)/shard_map/pallas_call | solution.py:99
  14.7 8.2 %collective-permute-done.2.value = f32[2,256,256]{2,1,0:T(8,128)S(1)} collective-permute-done((f32[2,256,256]{2,1,0:T(8,128)S(1)}, f32[2,256,256]{2,1,0:T(8,128)S(1)}, u32[]{:S(2)}, u32[]{:S(2)}) %collective-permute-start.2) | collective-permute-done | bytes 524320 | tf_op jit(solution)/shard_map/ppermute | solution.py:594
  23.0 1.4 %weights.1 = (f32[5,256,256]{2,1,0:T(8,128)S(1)}, f32[5,256,256]{2,1,0:T(8,128)S(1)}) custom-call(s32[4]{0:T(128)S(1)} %copy-done.2, f32[4,256,256]{2,1,0:T(8,128)S(1)} %copy-done, f32[4,256,256]{2,1,0:T(8,128)S(1)} %copy-done.1, f32[2,256,256]{2,1,0:T(8,128)S(1)} %shard_map.85._), custom_call_target="tpu_custom_call" | custom-call | flops 1048576 | bytes 8388608 | tf_op jit(solution)/shard_map/weights/pallas_call | solution.py:375
  24.4 1.9 %shard_map.87 = (f32[256,256]{1,0:T(8,128)S(1)}, f32[256,256]{1,0:T(8,128)S(1)}) custom-call(f32[8,256,256]{2,1,0:T(8,128)S(1)} %get-tuple-element.25.refs_0_.refs_2_.source.refs_3_, f32[2,256,256]{2,1,0:T(8,128)S(1)} %shard_map.84.refs_1_, f32[2,256,256]{2,1,0:T(8,128)S(1)} %shard_map.86.refs_2_, f32[5,256,256]{2,1,0:T(8,128)S(1)} %get-tuple-element.27.refs_3_.refs_0_, ...), custom_call_target="tpu_custom_call" | custom-call | flops 1207959552 | bytes 2097152 | tf_op jit(solution)/shard_map/pallas_call | solution.py:99
  26.4 2.2 %shard_map.90.refs_6_ = f32[2,256,256]{2,1,0:T(8,128)S(1)} custom-call(f32[8,256,256]{2,1,0:T(8,128)S(1)} %get-tuple-element.25.refs_0_.refs_2_.source.refs_3_, f32[2,256,256]{2,1,0:T(8,128)S(1)} %shard_map.89.refs_1_.refs_2_, f32[2,256,256]{2,1,0:T(8,128)S(1)} %shard_map.86.refs_2_, f32[8,256,256]{2,1,0:T(8,128)S(1)} %get-tuple-element.25.refs_0_.refs_2_.source.refs_3_, ...), custom_call_target="tpu_custom_call" | custom-call | flops 1610612736 | bytes 2097152 | tf_op jit(solution)/shard_map/pallas_call | solution.py:99
  28.7 2.1 %shard_map.91 = (f32[2,256,256]{2,1,0:T(8,128)S(1)}, f32[2,256,256]{2,1,0:T(8,128)S(1)}) custom-call(f32[8,256,256]{2,1,0:T(8,128)S(1)} %get-tuple-element.25.refs_0_.refs_2_.source.refs_3_, f32[2,256,256]{2,1,0:T(8,128)S(1)} %get-tuple-element.26.refs_1_, f32[2,256,256]{2,1,0:T(8,128)S(1)} %shard_map.89.refs_1_.refs_2_, ...), custom_call_target="tpu_custom_call" | custom-call | flops 2415919104 | bytes 2097152 | tf_op jit(solution)/shard_map/pallas_call | solution.py:99
  30.8 1.6 %collective-permute-start.4 = (f32[2,256,256]{2,1,0:T(8,128)S(1)}, f32[2,256,256]{2,1,0:T(8,128)S(1)}, u32[]{:S(2)}, u32[]{:S(2)}) collective-permute-start(f32[2,256,256]{2,1,0:T(8,128)S(1)} %get-tuple-element.31.real.refs_2_.refs_0_), channel_id=1, source_target_pairs={{0,4},{4,0},{8,12},{12,8},{16,20},{20,16},{24,28},{28,24},{1,5},{5... | collective-permute-start | bytes 1572872 | tf_op jit(solution)/shard_map/ppermute | solution.py:555
  32.4 1.6 %collective-permute-start.5 = (f32[2,256,256]{2,1,0:T(8,128)S(1)}, f32[2,256,256]{2,1,0:T(8,128)S(1)}, u32[]{:S(2)}, u32[]{:S(2)}) collective-permute-start(f32[2,256,256]{2,1,0:T(8,128)S(1)} %get-tuple-element.32.imag.refs_4_), channel_id=1, source_target_pairs={{0,8},{4,12},{8,0},{12,4},{16,24},{20,28},{24,16},{28,20},{1,9},{5... | collective-permute-start | bytes 1572872 | tf_op jit(solution)/shard_map/ppermute | solution.py:555
  33.9 1.9 %collective-permute-start.6 = (f32[2,256,256]{2,1,0:T(8,128)S(1)}, f32[2,256,256]{2,1,0:T(8,128)S(1)}, u32[]{:S(2)}, u32[]{:S(2)}) collective-permute-start(f32[2,256,256]{2,1,0:T(8,128)S(1)} %get-tuple-element.32.imag.refs_4_), channel_id=1, source_target_pairs={{8,16},{12,20},{16,8},{20,12},{9,17},{13,21},{17,9},{21,13},{10,18... | collective-permute-start | bytes 1572872 | tf_op jit(solution)/shard_map/ppermute | solution.py:555
  35.9 6.1 %collective-permute-done.4.partner.refs_3_.refs_1_ = f32[2,256,256]{2,1,0:T(8,128)S(1)} collective-permute-done((f32[2,256,256]{2,1,0:T(8,128)S(1)}, f32[2,256,256]{2,1,0:T(8,128)S(1)}, u32[]{:S(2)}, u32[]{:S(2)}) %collective-permute-start.4) | collective-permute-done | bytes 524320 | tf_op jit(solution)/shard_map/ppermute | solution.py:555
  41.9 1.8 %collective-permute-done.5.ahead.refs_5_ = f32[2,256,256]{2,1,0:T(8,128)S(1)} collective-permute-done((f32[2,256,256]{2,1,0:T(8,128)S(1)}, f32[2,256,256]{2,1,0:T(8,128)S(1)}, u32[]{:S(2)}, u32[]{:S(2)}) %collective-permute-start.5) | collective-permute-done | bytes 524320 | tf_op jit(solution)/shard_map/ppermute | solution.py:555
  43.7 3.7 %collective-permute-done.6.behind.refs_6_ = f32[2,256,256]{2,1,0:T(8,128)S(1)} collective-permute-done((f32[2,256,256]{2,1,0:T(8,128)S(1)}, f32[2,256,256]{2,1,0:T(8,128)S(1)}, u32[]{:S(2)}, u32[]{:S(2)}) %collective-permute-start.6) | collective-permute-done | bytes 524320 | tf_op jit(solution)/shard_map/ppermute | solution.py:555
  48.1 3.0 %collective-permute-start.7 = (f32[4,256,256]{2,1,0:T(8,128)S(1)}, f32[4,256,256]{2,1,0:T(8,128)S(1)}, u32[]{:S(2)}, u32[]{:S(2)}) collective-permute-start(f32[4,256,256]{2,1,0:T(8,128)S(1)} %get-tuple-element.35), channel_id=1, source_target_pairs={{0,1},{1,0},{2,3},{3,2},{4,5},{5,4},{6,7},{7,6},{8,9},{9,8},{10,11... | collective-permute-start | bytes 3145736 | tf_op jit(solution)/shard_map/ppermute | solution.py:552
  51.2 2.4 %collective-permute-start.11 = (f32[2,256,256]{2,1,0:T(8,128)S(1)}, f32[2,256,256]{2,1,0:T(8,128)S(1)}, u32[]{:S(2)}, u32[]{:S(2)}) collective-permute-start(f32[2,256,256]{2,1,0:T(8,128)S(1)} %shard_map.94), channel_id=1, source_target_pairs={{1,2},{2,1},{5,6},{6,5},{9,10},{10,9},{13,14},{14,13},{17,18},{18,... | collective-permute-start | bytes 1572872 | tf_op jit(solution)/shard_map/ppermute | solution.py:552
  53.5 3.2 %collective-permute-start.12 = (f32[2,256,256]{2,1,0:T(8,128)S(1)}, f32[2,256,256]{2,1,0:T(8,128)S(1)}, u32[]{:S(2)}, u32[]{:S(2)}) collective-permute-start(f32[2,256,256]{2,1,0:T(8,128)S(1)} %get-tuple-element.40), channel_id=1, source_target_pairs={{1,2},{2,1},{5,6},{6,5},{9,10},{10,9},{13,14},{14,13},{17,18},{18,... | collective-permute-start | bytes 1572872 | tf_op jit(solution)/shard_map/ppermute | solution.py:552
  56.7 4.9 %collective-permute-done.11.refs_9_ = f32[2,256,256]{2,1,0:T(8,128)S(1)} collective-permute-done((f32[2,256,256]{2,1,0:T(8,128)S(1)}, f32[2,256,256]{2,1,0:T(8,128)S(1)}, u32[]{:S(2)}, u32[]{:S(2)}) %collective-permute-start.11) | collective-permute-done | bytes 524320 | tf_op jit(solution)/shard_map/ppermute | solution.py:552
  61.7 5.6 %collective-permute-done.12.refs_10_ = f32[2,256,256]{2,1,0:T(8,128)S(1)} collective-permute-done((f32[2,256,256]{2,1,0:T(8,128)S(1)}, f32[2,256,256]{2,1,0:T(8,128)S(1)}, u32[]{:S(2)}, u32[]{:S(2)}) %collective-permute-start.12) | collective-permute-done | bytes 524320 | tf_op jit(solution)/shard_map/ppermute | solution.py:552
  67.8 1.9 %collective-permute-start.14 = (f32[1,256,256]{2,1,0:T(8,128)S(1)}, f32[1,256,256]{2,1,0:T(8,128)S(1)}, u32[]{:S(2)}, u32[]{:S(2)}) collective-permute-start(f32[1,256,256]{2,1,0:T(8,128)S(1)} %get-tuple-element.43), channel_id=1, source_target_pairs={{8,16},{12,20},{16,8},{20,12},{9,17},{13,21},{17,9},{21,13},{10,18... | collective-permute-start | bytes 786440 | tf_op jit(solution)/shard_map/ppermute | solution.py:555
  70.8 1.6 %collective-permute-start.10 = (f32[1,256,256]{2,1,0:T(8,128)S(1)}, f32[1,256,256]{2,1,0:T(8,128)S(1)}, u32[]{:S(2)}, u32[]{:S(2)}) collective-permute-start(f32[1,256,256]{2,1,0:T(8,128)S(1)} %get-tuple-element.39), channel_id=1, source_target_pairs={{0,4},{4,0},{8,12},{12,8},{16,20},{20,16},{24,28},{28,24},{1,5},{5... | collective-permute-start | bytes 786440 | tf_op jit(solution)/shard_map/ppermute | solution.py:555
  72.4 0.8 collective-permute-start.8
  73.2 1.0 %collective-permute-done.13.from_first = f32[1,256,256]{2,1,0:T(8,128)S(1)} collective-permute-done((f32[1,256,256]{2,1,0:T(8,128)S(1)}, f32[1,256,256]{2,1,0:T(8,128)S(1)}, u32[]{:S(2)}, u32[]{:S(2)}) %collective-permute-start.13) | collective-permute-done | bytes 262176 | tf_op jit(solution)/shard_map/ppermute | solution.py:555
  74.2 2.1 %collective-permute-start.9 = (f32[1,256,256]{2,1,0:T(8,128)S(1)}, f32[1,256,256]{2,1,0:T(8,128)S(1)}, u32[]{:S(2)}, u32[]{:S(2)}) collective-permute-start(f32[1,256,256]{2,1,0:T(8,128)S(1)} %get-tuple-element.38), channel_id=1, source_target_pairs={{8,16},{12,20},{16,8},{20,12},{9,17},{13,21},{17,9},{21,13},{10,18... | collective-permute-start | bytes 786440 | tf_op jit(solution)/shard_map/ppermute | solution.py:555
  76.4 0.8 %shard_map.96.rest_0_ = f32[1,2,2,256,256]{4,3,2,1,0:T(8,128)} custom-call(f32[2,256,256]{2,1,0:T(8,128)S(1)} %get-tuple-element.41.own, f32[1,256,256]{2,1,0:T(8,128)S(1)} %collective-permute-done.13.from_first, f32[1,256,256]{2,1,0:T(8,128)S(1)} %collective-permute-done.14.from_second, f32[1,256,256]{2,1,0:T(8,128)S(1)} %collective-permute-done.15.from_partner), custom_call_target="tpu_custom_call" | custom-call | tf_op jit(solution)/shard_map/pallas_call | solution.py:520
  77.2 1.8 %collective-permute-done.10.from_partner = f32[1,256,256]{2,1,0:T(8,128)S(1)} collective-permute-done((f32[1,256,256]{2,1,0:T(8,128)S(1)}, f32[1,256,256]{2,1,0:T(8,128)S(1)}, u32[]{:S(2)}, u32[]{:S(2)}) %collective-permute-start.10) | collective-permute-done | bytes 262176 | tf_op jit(solution)/shard_map/ppermute | solution.py:555
  79.0 3.4 %collective-permute-done.9.from_second = f32[1,256,256]{2,1,0:T(8,128)S(1)} collective-permute-done((f32[1,256,256]{2,1,0:T(8,128)S(1)}, f32[1,256,256]{2,1,0:T(8,128)S(1)}, u32[]{:S(2)}, u32[]{:S(2)}) %collective-permute-start.9) | collective-permute-done | bytes 262176 | tf_op jit(solution)/shard_map/ppermute | solution.py:555
  82.5 0.8 shard_map.97
  (24 shorter events, 3.0 us)
Async XLA Ops:
  2.4 23.9 %collective-permute-start.1 = (f32[8,256,256]{2,1,0:T(8,128)S(1)}, f32[8,256,256]{2,1,0:T(8,128)S(1)}, u32[]{:S(2)}, u32[]{:S(2)}) collective-permute-start(f32[8,256,256]{2,1,0:T(8,128)S(1)} %get-tuple-element.25.refs_0_.refs_2_.source.refs_3_), channel_id=1, source_target_pairs={{0,1},{1,0},{2,3},{3,2},{4,5},{5,4},{6,7},{7,6},{8,9},{9,8},{10,11... | collective-permute-start | bytes 6291464 | tf_op jit(solution)/shard_map/ppermute | solution.py:552
  4.5 4.5 %collective-permute-start = (f32[2,256,256]{2,1,0:T(8,128)S(1)}, f32[2,256,256]{2,1,0:T(8,128)S(1)}, u32[]{:S(2)}, u32[]{:S(2)}) collective-permute-start(f32[2,256,256]{2,1,0:T(8,128)S(1)} %shard_map.82), channel_id=1, source_target_pairs={{0,1},{1,0},{2,3},{3,2},{4,5},{5,4},{6,7},{7,6},{8,9},{9,8},{10,11... | collective-permute-start | bytes 1572872 | tf_op jit(solution)/shard_map/ppermute | solution.py:552
  14.2 8.8 %copy-start = (f32[4,256,256]{2,1,0:T(8,128)S(1)}, f32[4,256,256]{2,1,0:T(8,128)}, u32[]{:S(2)}) copy-start(f32[4,256,256]{2,1,0:T(8,128)} %local_ref.1) | copy-start | bytes 3145732
  14.2 8.8 %copy-start.1 = (f32[4,256,256]{2,1,0:T(8,128)S(1)}, f32[4,256,256]{2,1,0:T(8,128)}, u32[]{:S(2)}) copy-start(f32[4,256,256]{2,1,0:T(8,128)} %side_ref.1) | copy-start | bytes 3145732
  14.2 8.8 %copy-start.2 = (s32[4]{0:T(128)S(1)}, s32[4]{0:T(128)}, u32[]{:S(2)}) copy-start(s32[4]{0:T(128)} %shift_ref.1) | copy-start | bytes 52
  14.2 8.7 %collective-permute-start.2 = (f32[2,256,256]{2,1,0:T(8,128)S(1)}, f32[2,256,256]{2,1,0:T(8,128)S(1)}, u32[]{:S(2)}, u32[]{:S(2)}) collective-permute-start(f32[2,256,256]{2,1,0:T(8,128)S(1)} %shard_map.85._), channel_id=1, source_target_pairs={{1,2},{2,1},{0,4},{3,7},{5,6},{6,5},{4,0},{7,3},{9,10},{10,9},{8,1... | collective-permute-start | bytes 1572872 | tf_op jit(solution)/shard_map/ppermute | solution.py:594
  22.9 3.4 %collective-permute-start.3 = (f32[2,256,256]{2,1,0:T(8,128)S(1)}, f32[2,256,256]{2,1,0:T(8,128)S(1)}, u32[]{:S(2)}, u32[]{:S(2)}) collective-permute-start(f32[2,256,256]{2,1,0:T(8,128)S(1)} %shard_map.86.refs_2_), channel_id=1, source_target_pairs={{0,1},{1,0},{2,3},{3,2},{4,5},{5,4},{6,7},{7,6},{8,9},{9,8},{10,11... | collective-permute-start | bytes 1572872 | tf_op jit(solution)/shard_map/ppermute | solution.py:552
  30.8 11.2 %collective-permute-start.4 = (f32[2,256,256]{2,1,0:T(8,128)S(1)}, f32[2,256,256]{2,1,0:T(8,128)S(1)}, u32[]{:S(2)}, u32[]{:S(2)}) collective-permute-start(f32[2,256,256]{2,1,0:T(8,128)S(1)} %get-tuple-element.31.real.refs_2_.refs_0_), channel_id=1, source_target_pairs={{0,4},{4,0},{8,12},{12,8},{16,20},{20,16},{24,28},{28,24},{1,5},{5... | collective-permute-start | bytes 1572872 | tf_op jit(solution)/shard_map/ppermute | solution.py:555
  32.4 11.4 %collective-permute-start.5 = (f32[2,256,256]{2,1,0:T(8,128)S(1)}, f32[2,256,256]{2,1,0:T(8,128)S(1)}, u32[]{:S(2)}, u32[]{:S(2)}) collective-permute-start(f32[2,256,256]{2,1,0:T(8,128)S(1)} %get-tuple-element.32.imag.refs_4_), channel_id=1, source_target_pairs={{0,8},{4,12},{8,0},{12,4},{16,24},{20,28},{24,16},{28,20},{1,9},{5... | collective-permute-start | bytes 1572872 | tf_op jit(solution)/shard_map/ppermute | solution.py:555
  33.9 13.5 %collective-permute-start.6 = (f32[2,256,256]{2,1,0:T(8,128)S(1)}, f32[2,256,256]{2,1,0:T(8,128)S(1)}, u32[]{:S(2)}, u32[]{:S(2)}) collective-permute-start(f32[2,256,256]{2,1,0:T(8,128)S(1)} %get-tuple-element.32.imag.refs_4_), channel_id=1, source_target_pairs={{8,16},{12,20},{16,8},{20,12},{9,17},{13,21},{17,9},{21,13},{10,18... | collective-permute-start | bytes 1572872 | tf_op jit(solution)/shard_map/ppermute | solution.py:555
  48.1 22.3 %collective-permute-start.7 = (f32[4,256,256]{2,1,0:T(8,128)S(1)}, f32[4,256,256]{2,1,0:T(8,128)S(1)}, u32[]{:S(2)}, u32[]{:S(2)}) collective-permute-start(f32[4,256,256]{2,1,0:T(8,128)S(1)} %get-tuple-element.35), channel_id=1, source_target_pairs={{0,1},{1,0},{2,3},{3,2},{4,5},{5,4},{6,7},{7,6},{8,9},{9,8},{10,11... | collective-permute-start | bytes 3145736 | tf_op jit(solution)/shard_map/ppermute | solution.py:552
  51.2 10.5 %collective-permute-start.11 = (f32[2,256,256]{2,1,0:T(8,128)S(1)}, f32[2,256,256]{2,1,0:T(8,128)S(1)}, u32[]{:S(2)}, u32[]{:S(2)}) collective-permute-start(f32[2,256,256]{2,1,0:T(8,128)S(1)} %shard_map.94), channel_id=1, source_target_pairs={{1,2},{2,1},{5,6},{6,5},{9,10},{10,9},{13,14},{14,13},{17,18},{18,... | collective-permute-start | bytes 1572872 | tf_op jit(solution)/shard_map/ppermute | solution.py:552
  53.5 13.8 %collective-permute-start.12 = (f32[2,256,256]{2,1,0:T(8,128)S(1)}, f32[2,256,256]{2,1,0:T(8,128)S(1)}, u32[]{:S(2)}, u32[]{:S(2)}) collective-permute-start(f32[2,256,256]{2,1,0:T(8,128)S(1)} %get-tuple-element.40), channel_id=1, source_target_pairs={{1,2},{2,1},{5,6},{6,5},{9,10},{10,9},{13,14},{14,13},{17,18},{18,... | collective-permute-start | bytes 1572872 | tf_op jit(solution)/shard_map/ppermute | solution.py:552
  67.8 6.4 %collective-permute-start.13 = (f32[1,256,256]{2,1,0:T(8,128)S(1)}, f32[1,256,256]{2,1,0:T(8,128)S(1)}, u32[]{:S(2)}, u32[]{:S(2)}) collective-permute-start(f32[1,256,256]{2,1,0:T(8,128)S(1)} %get-tuple-element.42), channel_id=1, source_target_pairs={{0,8},{4,12},{8,0},{12,4},{16,24},{20,28},{24,16},{28,20},{1,9},{5... | collective-permute-start | bytes 786440 | tf_op jit(solution)/shard_map/ppermute | solution.py:555
  67.8 8.5 %collective-permute-start.14 = (f32[1,256,256]{2,1,0:T(8,128)S(1)}, f32[1,256,256]{2,1,0:T(8,128)S(1)}, u32[]{:S(2)}, u32[]{:S(2)}) collective-permute-start(f32[1,256,256]{2,1,0:T(8,128)S(1)} %get-tuple-element.43), channel_id=1, source_target_pairs={{8,16},{12,20},{16,8},{20,12},{9,17},{13,21},{17,9},{21,13},{10,18... | collective-permute-start | bytes 786440 | tf_op jit(solution)/shard_map/ppermute | solution.py:555
  69.8 6.6 %collective-permute-start.15 = (f32[1,256,256]{2,1,0:T(8,128)S(1)}, f32[1,256,256]{2,1,0:T(8,128)S(1)}, u32[]{:S(2)}, u32[]{:S(2)}) collective-permute-start(f32[1,256,256]{2,1,0:T(8,128)S(1)} %get-tuple-element.44), channel_id=1, source_target_pairs={{0,4},{4,0},{8,12},{12,8},{16,20},{20,16},{24,28},{28,24},{1,5},{5... | collective-permute-start | bytes 786440 | tf_op jit(solution)/shard_map/ppermute | solution.py:555
  70.8 8.2 %collective-permute-start.10 = (f32[1,256,256]{2,1,0:T(8,128)S(1)}, f32[1,256,256]{2,1,0:T(8,128)S(1)}, u32[]{:S(2)}, u32[]{:S(2)}) collective-permute-start(f32[1,256,256]{2,1,0:T(8,128)S(1)} %get-tuple-element.39), channel_id=1, source_target_pairs={{0,4},{4,0},{8,12},{12,8},{16,20},{20,16},{24,28},{28,24},{1,5},{5... | collective-permute-start | bytes 786440 | tf_op jit(solution)/shard_map/ppermute | solution.py:555
  72.4 6.6 %collective-permute-start.8 = (f32[1,256,256]{2,1,0:T(8,128)S(1)}, f32[1,256,256]{2,1,0:T(8,128)S(1)}, u32[]{:S(2)}, u32[]{:S(2)}) collective-permute-start(f32[1,256,256]{2,1,0:T(8,128)S(1)} %get-tuple-element.37), channel_id=1, source_target_pairs={{0,8},{4,12},{8,0},{12,4},{16,24},{20,28},{24,16},{28,20},{1,9},{5... | collective-permute-start | bytes 786440 | tf_op jit(solution)/shard_map/ppermute | solution.py:555
  74.2 8.3 %collective-permute-start.9 = (f32[1,256,256]{2,1,0:T(8,128)S(1)}, f32[1,256,256]{2,1,0:T(8,128)S(1)}, u32[]{:S(2)}, u32[]{:S(2)}) collective-permute-start(f32[1,256,256]{2,1,0:T(8,128)S(1)} %get-tuple-element.38), channel_id=1, source_target_pairs={{8,16},{12,20},{16,8},{20,12},{9,17},{13,21},{17,9},{21,13},{10,18... | collective-permute-start | bytes 786440 | tf_op jit(solution)/shard_map/ppermute | solution.py:555
